TPU v7x, 32 devices: a whole 2x2x4 slice. The times are simulated.
32 devices in a mesh: dp: 8 (over y, x, core), head: 4 (over z).
Axes of the slice: x: 2, y: 2, z: 4, core: 2. Of those that a mesh axis runs over, the one named last changes fastest.
Arguments:
- latents: bfloat16 [12288, 1024], P('dp'), may hold values from -6 to 6
- media_tokens: bfloat16 [49152, 1024], P('dp'), may hold values from -6 to 6
- image_counts: int32 [64], replicated, may hold values from 1 to 5, 192 in all
- time_table: bfloat16 [5, 1024], replicated, may hold values from -3 to 3
- media_gain: float32 [1024], replicated, may hold values from 0.5 to 1.5
- media_bias: float32 [1024], replicated, may hold values from -1 to 1
- latent_gain: float32 [1024], replicated, may hold values from 0.5 to 1.5
- latent_bias: float32 [1024], replicated, may hold values from -1 to 1
- feed_gain: float32 [1024], replicated, may hold values from 0.5 to 1.5
- feed_bias: float32 [1024], replicated, may hold values from -1 to 1
- query_weight: bfloat16 [1024, 512], P('dp', 'head'), may hold values from -0.1875 to 0.1875
- key_weight: bfloat16 [1024, 512], P('dp', 'head'), may hold values from -0.1875 to 0.1875
- value_weight: bfloat16 [1024, 512], P('dp', 'head'), may hold values from -0.1875 to 0.1875
- out_weight: bfloat16 [512, 1024], P('head', 'dp'), may hold values from -1 to 1
- up_weight: bfloat16 [1024, 4096], P('dp', 'head'), may hold values from -0.1875 to 0.1875
- down_weight: bfloat16 [4096, 1024], P('head', 'dp'), may hold values from -0.09375 to 0.09375
- cotangent: bfloat16 [12288, 1024], P('dp', 'head'), may hold values from -6 to 6
Outputs:
- latents_out: float32 [12288, 1024], P('dp', 'head')
- latents_grad: float32 [12288, 1024], P('dp')
- time_grad: float32 [5, 1024], replicated
- media_gain_grad: float32 [1024], replicated
- media_bias_grad: float32 [1024], replicated
- latent_gain_grad: float32 [1024], replicated
- latent_bias_grad: float32 [1024], replicated
- feed_gain_grad: float32 [1024], replicated
- feed_bias_grad: float32 [1024], replicated
- query_grad: float32 [1024, 512], P('dp', 'head')
- key_grad: float32 [1024, 512], P('dp', 'head')
- value_grad: float32 [1024, 512], P('dp', 'head')
- out_grad: float32 [512, 1024], P('head', 'dp')
- up_grad: float32 [1024, 4096], P('dp', 'head')
- down_grad: float32 [4096, 1024], P('head', 'dp')
Inputs may be any that keep to these rules, and one draw needn't show every extreme that they name: `image_counts`: each sample holds 1 to 5 images, the counts sum to 192, and some sample holds exactly 5.
All inputs are finite; a program needn't handle non-finite values.
Results may differ from a plain program's by a relative error of at most 0.017.
Values may be sent and summed in bfloat16 or wider, within the bound.
No kernel may reach another device: no remote copies, remote signals or barrier semaphores. Data moves between devices by JAX's collectives and lax.ppermute only.
A program may use at most 192 MiB of HBM per device.

v0:
```python
import math

import jax
import jax.numpy as jnp
from jax import lax
from jax.experimental import pallas as pl
from jax.experimental.pallas import tpu as pltpu
from jax.sharding import PartitionSpec as P


D = 1024
DH = 64
LAT = 64
PATCH = 256
MAX_MEDIA = 5
GROUP = 4

epsilon = 1e-05
highest = lax.Precision.HIGHEST
bf16 = jnp.bfloat16
f32 = jnp.float32


def mm(left, right):
    return lax.dot_general(left, right, (((1,), (0,)), ((), ())), preferred_element_type=f32)


def mm_tn(left, right):
    return lax.dot_general(left, right, (((0,), (0,)), ((), ())), preferred_element_type=f32)


def mm_nt(left, right):
    return lax.dot_general(left, right, (((1,), (1,)), ((), ())), preferred_element_type=f32)


def norm_stats(values_in):
    centre = jnp.mean(values_in, axis=-1, keepdims=True)
    shifted = values_in - centre
    spread = jnp.mean(shifted * shifted, axis=-1, keepdims=True)
    inverse = lax.rsqrt(spread + epsilon)
    return (shifted * inverse, inverse)


def norm_back(grad_in, scaled, inverse, norm_gain):
    weighted = grad_in * norm_gain
    return inverse * (
        weighted
        - jnp.mean(weighted, axis=-1, keepdims=True)
        - scaled * jnp.mean(weighted * scaled, axis=-1, keepdims=True)
    )


def gelu_exact(up_proj):
    return up_proj * 0.5 * (1.0 + lax.erf(up_proj * 0.5**0.5))


def gelu_slope(up_proj):
    normal_cdf = 0.5 * (1.0 + lax.erf(up_proj * 0.5**0.5))
    normal_pdf = jnp.exp(-0.5 * up_proj * up_proj) * (2.0 * math.pi) ** (-0.5)
    return normal_cdf + up_proj * normal_pdf


def own_blocks():
    width = GROUP * DH
    rows = lax.broadcasted_iota(jnp.int32, (GROUP * LAT, width), 0) // LAT
    cols = lax.broadcasted_iota(jnp.int32, (GROUP * LAT, width), 1) // DH
    return rows == cols


def spread_heads(block, mask):
    return jnp.where(mask, jnp.concatenate([block] * GROUP, axis=0), jnp.zeros((), block.dtype))


def gather_heads(blocks, mask):
    kept = jnp.where(mask, blocks, 0.0)
    return sum(kept[g * LAT : (g + 1) * LAT] for g in range(GROUP))


def soft_of(query_diag, keys):
    scores = mm_nt(query_diag, keys) * (DH**-0.5)
    expd = jnp.exp(scores - jnp.max(scores, axis=-1, keepdims=True))
    return expd / jnp.sum(expd, axis=-1, keepdims=True)


def attend_kernel(q_ref, km_ref, kl_ref, vm_ref, vl_ref, mixed_ref):
    mask = own_blocks()
    width = GROUP * DH
    for g in range(q_ref.shape[1] // width):
        cols = slice(g * width, (g + 1) * width)
        keys = jnp.concatenate([km_ref[:, cols], kl_ref[:, cols]], axis=0)
        values = jnp.concatenate([vm_ref[:, cols], vl_ref[:, cols]], axis=0)
        soft = soft_of(spread_heads(q_ref[:, cols], mask), keys)
        mixed_ref[:, cols] = gather_heads(mm(soft.astype(bf16), values), mask).astype(bf16)


def attend_back_kernel(
    q_ref, km_ref, kl_ref, vm_ref, vl_ref, dm_ref, dq_ref, dkvm_ref, dkvl_ref
):
    mask = own_blocks()
    width = GROUP * DH
    inner = q_ref.shape[1]
    for g in range(q_ref.shape[1] // width):
        cols = slice(g * width, (g + 1) * width)
        keys = jnp.concatenate([km_ref[:, cols], kl_ref[:, cols]], axis=0)
        values = jnp.concatenate([vm_ref[:, cols], vl_ref[:, cols]], axis=0)
        query_diag = spread_heads(q_ref[:, cols], mask)
        mixed_diag = spread_heads(dm_ref[:, cols], mask)
        soft = soft_of(query_diag, keys)
        d_prob = mm_nt(mixed_diag, values)
        d_value = mm_tn(soft.astype(bf16), mixed_diag).astype(bf16)
        delta = jnp.sum(soft * d_prob, axis=-1, keepdims=True)
        d_scores = (soft * (d_prob - delta)).astype(bf16)
        d_query = gather_heads(mm(d_scores, keys), mask) * (DH**-0.5)
        d_key = (mm_tn(d_scores, query_diag) * (DH**-0.5)).astype(bf16)
        dq_ref[:, cols] = d_query.astype(bf16)
        value_cols = slice(inner + g * width, inner + (g + 1) * width)
        dkvm_ref[:, cols] = d_key[:PATCH]
        dkvl_ref[:, cols] = d_key[PATCH:]
        dkvm_ref[:, value_cols] = d_value[:PATCH]
        dkvl_ref[:, value_cols] = d_value[PATCH:]


def image_spec(rows, cols, block_col=0):
    return pl.BlockSpec((rows, cols), lambda n: (n, block_col))


def attend(query, media_kv, latent_kv):
    inner = query.shape[1]
    images = query.shape[0] // LAT
    return pl.pallas_call(
        attend_kernel,
        grid=(images,),
        in_specs=[
            image_spec(LAT, inner),
            image_spec(PATCH, inner, 0),
            image_spec(LAT, inner, 0),
            image_spec(PATCH, inner, 1),
            image_spec(LAT, inner, 1),
        ],
        out_specs=image_spec(LAT, inner),
        out_shape=jax.ShapeDtypeStruct(query.shape, bf16),
        name="attend",
    )(query, media_kv, latent_kv, media_kv, latent_kv)


def attend_back(query, media_kv, latent_kv, d_mixed):
    inner = query.shape[1]
    images = query.shape[0] // LAT
    return pl.pallas_call(
        attend_back_kernel,
        grid=(images,),
        in_specs=[
            image_spec(LAT, inner),
            image_spec(PATCH, inner, 0),
            image_spec(LAT, inner, 0),
            image_spec(PATCH, inner, 1),
            image_spec(LAT, inner, 1),
            image_spec(LAT, inner),
        ],
        out_specs=[
            image_spec(LAT, inner),
            image_spec(PATCH, 2 * inner),
            image_spec(LAT, 2 * inner),
        ],
        out_shape=[
            jax.ShapeDtypeStruct(shape, bf16)
            for shape in (query.shape, media_kv.shape, latent_kv.shape)
        ],
        name="attend_back",
    )(query, media_kv, latent_kv, media_kv, latent_kv, d_mixed)


EARLY = 256


def unit_specs(main, extra, side):
    return [
        pl.BlockSpec((D, weights.shape[1] // 2), lambda n: (n, side)) for weights in (main, extra)
    ]


def hidden_kernel(norm_ref, grad_ref, up_ref, up_more, down_ref, down_more, act_ref, d_up_ref):
    start = 0
    for up, down in ((up_ref, down_ref), (up_more, down_more)):
        cols = slice(start, start + up.shape[1])
        start += up.shape[1]
        up_proj = mm(norm_ref[...], up[...])
        d_act = mm(grad_ref[...], down[...])
        act_ref[:, cols] = gelu_exact(up_proj).astype(bf16)
        d_up_ref[:, cols] = (d_act * gelu_slope(up_proj)).astype(bf16)


def hidden_units(feed_norm, grad_out, main, extra):
    rows = feed_norm.shape[0]
    n_head = main.shape[0] // D
    per_head = (main.shape[1] + extra.shape[1]) // 2
    units = per_head * n_head
    whole = pl.BlockSpec((rows, D), lambda n: (0, 0))
    cols = pl.BlockSpec((rows, per_head), lambda n: (0, n))
    shape = jax.ShapeDtypeStruct((rows, units), bf16)
    return pl.pallas_call(
        hidden_kernel,
        grid=(n_head,),
        in_specs=[whole, whole] + unit_specs(main, extra, 0) + unit_specs(main, extra, 1),
        out_specs=[cols, cols],
        out_shape=[shape, shape],
        cost_estimate=pl.CostEstimate(
            flops=4 * rows * D * units, bytes_accessed=4 * D * units, transcendentals=rows * units
        ),
        name="hidden_units",
    )(feed_norm, grad_out, main, extra, main, extra)


def add_features(units_ref, weight_ref, more_ref, total):
    @pl.when(pl.program_id(0) == 0)
    def _():
        total[...] = jnp.zeros_like(total)

    split = weight_ref.shape[1]
    total[...] += mm_nt(units_ref[:, :split], weight_ref[...])
    total[...] += mm_nt(units_ref[:, split:], more_ref[...])


def feed_out_kernel(units_ref, weight_ref, more_ref, hidden_ref, out_ref, total):
    add_features(units_ref, weight_ref, more_ref, total)

    @pl.when(pl.program_id(0) == pl.num_programs(0) - 1)
    def _():
        out_ref[...] = (hidden_ref[...] + total[...]).astype(bf16)


def d_feed_kernel(
    units_ref,
    weight_ref,
    more_ref,
    hidden_ref,
    grad_ref,
    gain_ref,
    out_weight_ref,
    d_hidden_ref,
    d_attention_ref,
    d_mixed_ref,
    gain_out,
    bias_out,
    total,
):
    add_features(units_ref, weight_ref, more_ref, total)

    @pl.when(pl.program_id(0) == pl.num_programs(0) - 1)
    def _():
        d_feed = total[...]
        scaled, inverse = norm_stats(hidden_ref[...])
        gain_out[...] = jnp.sum(d_feed * scaled, axis=0, keepdims=True)
        bias_out[...] = jnp.sum(d_feed, axis=0, keepdims=True)
        d_hidden = grad_ref[...].astype(f32) + norm_back(d_feed, scaled, inverse, gain_ref[...])
        d_hidden_ref[...] = d_hidden
        d_attention_ref[...] = d_hidden.astype(bf16)
        d_mixed_ref[...] = mm(d_hidden.astype(bf16), out_weight_ref[...]).astype(bf16)


def to_features(kernel, units_in, main, extra, side, others, out_shapes):
    rows, units = units_in.shape
    n_head = main.shape[0] // D
    return pl.pallas_call(
        kernel,
        grid=(n_head,),
        in_specs=[pl.BlockSpec((rows, units // n_head), lambda n: (0, n))]
        + unit_specs(main, extra, side)
        + [pl.BlockSpec(other.shape, lambda n: (0, 0)) for other in others],
        out_specs=[pl.BlockSpec(shape.shape, lambda n: (0, 0)) for shape in out_shapes],
        out_shape=out_shapes,
        scratch_shapes=[pltpu.VMEM((rows, D), f32)],
        cost_estimate=pl.CostEstimate(
            flops=2 * rows * D * units, bytes_accessed=2 * D * units, transcendentals=0
        ),
    )(units_in, main, extra, *others)


def media_back_kernel(
    place_ref, tokens_ref, added_ref, gain_ref, d_kv_ref, weight_ref, gain_out, bias_out, sum_out
):
    @pl.when(pl.program_id(0) == 0)
    def _():
        gain_out[...] = jnp.zeros_like(gain_out)
        bias_out[...] = jnp.zeros_like(bias_out)

    scaled, inverse = norm_stats(tokens_ref[...].astype(f32) + added_ref[0])
    d_norm = mm_nt(d_kv_ref[...], weight_ref[...])
    gain_out[...] += jnp.sum(d_norm * scaled, axis=0, keepdims=True)
    bias_out[...] += jnp.sum(d_norm, axis=0, keepdims=True)
    back = norm_back(d_norm, scaled, inverse, gain_ref[...])
    sum_out[0] = jnp.sum(back, axis=0, keepdims=True)


def media_back(media_tokens, per_image, media_gain, d_media_kv, kv_full, here):
    images = per_image.shape[0]
    row = pl.BlockSpec((1, D), lambda n, at: (0, 0))
    own_row = pl.BlockSpec((1, 1, D), lambda n, at: (n, 0, 0))
    cols = d_media_kv.shape[1]
    gain_sum, bias_sum, sums = pl.pallas_call(
        media_back_kernel,
        grid_spec=pltpu.PrefetchScalarGridSpec(
            num_scalar_prefetch=1,
            grid=(images,),
            in_specs=[
                pl.BlockSpec((PATCH, D), lambda n, at: (at[1] * images + n, 0)),
                own_row,
                row,
                pl.BlockSpec((PATCH, cols), lambda n, at: (n, 0)),
                pl.BlockSpec((D, cols), lambda n, at: (0, 0)),
            ],
            out_specs=[row, row, own_row],
        ),
        out_shape=[
            jax.ShapeDtypeStruct((1, D), f32),
            jax.ShapeDtypeStruct((1, D), f32),
            jax.ShapeDtypeStruct((images, 1, D), f32),
        ],
        cost_estimate=pl.CostEstimate(
            flops=2 * images * PATCH * D * cols,
            bytes_accessed=4 * images * PATCH * D,
            transcendentals=0,
        ),
        name="media_back",
    )(here, media_tokens, per_image[:, None, :], media_gain[None, :], d_media_kv, kv_full)
    return (gain_sum[0], bias_sum[0], sums[:, 0, :])


def join(refs):
    return jnp.concatenate([ref[...] for ref in refs], axis=1)


def unit_grad_kernel(place_ref, *refs):
    left, (right_ref, out_ref) = refs[:-2], refs[-2:]
    out_ref[...] = mm_tn(join(left), right_ref[...]).astype(bf16)


def attention_grad_kernel(place_ref, *refs):
    count = (len(refs) - 7) // 3
    latent, media, attention = refs[:count], refs[count : 2 * count], refs[2 * count : 3 * count]
    dq_ref, dkm_ref, dvm_ref, dkl_ref, dvl_ref, mixed_ref, out_ref = refs[3 * count :]
    latent_rows, media_rows = join(latent), join(media)
    query_part = mm_tn(latent_rows, dq_ref[...])
    kv_part = mm_tn(media_rows, join((dkm_ref, dvm_ref))) + mm_tn(
        latent_rows, join((dkl_ref, dvl_ref))
    )
    out_part = mm_tn(join(attention), mixed_ref[...])
    out_ref[...] = jnp.concatenate([query_part, kv_part, out_part], axis=1).astype(bf16)


def make_step(n_dp, n_head):
    def swap(block, bit):
        return lax.ppermute(block, "dp", [(j, j ^ bit) for j in range(n_dp)])

    def shift(block, step):
        return lax.ppermute(block, "head", [(j, (j + step) % n_head) for j in range(n_head)])

    def swap_head(block, bit):
        return lax.ppermute(block, "head", [(j, j ^ bit) for j in range(n_head)])

    ordered = [1 << b for b in range(1, n_dp.bit_length() - 1)]
    paths = (ordered, ordered[::-1])
    evens = list(range(0, n_dp, 2))
    size = D // n_dp
    wide = size % 128 == 0
    half_blocks = D // 2 // max(size, 128)

    def send_order(bits):
        order = [0]
        for bit in bits:
            order = order + [m | bit for m in order]
        return order

    orders = [send_order(bits) for bits in paths]

    def left_blocks(values_in, me, half, steps):
        rows = values_in.shape[0]
        if wide:
            specs = [
                pl.BlockSpec(
                    (rows, size),
                    lambda n, at, m=m, k=k: (0, at[0] ^ jnp.where(n < steps // 2, m, k)),
                )
                for m, k in zip(*[[m | half for m in order] for order in orders])
            ]
        else:
            parts = [
                lax.dynamic_slice_in_dim(values_in, (me ^ (m | odd)) * size, size, 1)
                for order in orders
                for odd in (0, 1)
                for m in order
            ]
            values_in = jnp.concatenate(parts, axis=1)
            specs = [
                pl.BlockSpec(
                    (rows, 128),
                    lambda n, at, b=b: (0, b + jnp.where(n < steps // 2, 0, D // 128)),
                )
                for b in range(half * half_blocks, (half + 1) * half_blocks)
            ]
        return ([values_in] * half_blocks, specs)

    def unit_grad(left, right, here, half):
        rows, units = right.shape
        block = units // n_head
        operands, specs = left_blocks(left, here[0], half, n_head)
        return pl.pallas_call(
            unit_grad_kernel,
            grid_spec=pltpu.PrefetchScalarGridSpec(
                num_scalar_prefetch=1,
                grid=(n_head,),
                in_specs=specs
                + [
                    pl.BlockSpec(
                        (rows, block), lambda n, at: (0, lax.rem(at[1] + n_head - n, n_head))
                    )
                ],
                out_specs=pl.BlockSpec((D // 2, block), lambda n, at: (0, n)),
            ),
            out_shape=jax.ShapeDtypeStruct((D // 2, units), bf16),
            cost_estimate=pl.CostEstimate(
                flops=rows * D * units, bytes_accessed=D * units, transcendentals=0
            ),
            name="unit_grad",
        )(here, *operands, right)

    def attention_grad(
        latent_norm, media_norm, d_attention, d_query, d_media_kv, d_latent_kv, mixed, here, half
    ):
        inner = d_query.shape[1]
        width = inner // n_head
        operands, specs = [], []
        for left in (latent_norm, media_norm, d_attention):
            more, more_specs = left_blocks(left, here[0], half, n_head)
            operands, specs = operands + more, specs + more_specs

        def group(rows, start):
            return pl.BlockSpec(
                (rows, width), lambda n, at: (0, start + lax.rem(at[1] + n_head - n, n_head))
            )

        lat_rows, media_rows = d_query.shape[0], d_media_kv.shape[0]
        return pl.pallas_call(
            attention_grad_kernel,
            grid_spec=pltpu.PrefetchScalarGridSpec(
                num_scalar_prefetch=1,
                grid=(n_head,),
                in_specs=specs
                + [
                    group(lat_rows, 0),
                    group(media_rows, 0),
                    group(media_rows, n_head),
                    group(lat_rows, 0),
                    group(lat_rows, n_head),
                    group(lat_rows, 0),
                ],
                out_specs=pl.BlockSpec((D // 2, 4 * width), lambda n, at: (0, n)),
            ),
            out_shape=jax.ShapeDtypeStruct((D // 2, 4 * inner), bf16),
            cost_estimate=pl.CostEstimate(
                flops=2 * D * inner * (media_rows + 2 * lat_rows),
                bytes_accessed=4 * D * inner,
                transcendentals=0,
            ),
            name="attention_grad",
        )(here, *operands, d_query, d_media_kv, d_media_kv, d_latent_kv, d_latent_kv, mixed)


    def gather(shard):
        columns = [shard] + [shift(shard, s) for s in range(1, n_head)]
        half = n_head // 2
        pieces = {}
        for side, bits in enumerate(paths):
            held = {0: jnp.concatenate(columns[side * half : (side + 1) * half], axis=1)}
            for bit in bits:
                for m in list(held):
                    held[m | bit] = swap(held[m], bit)
            for m in evens:
                pieces[m, side] = held[m]
                pieces[m | 1, side] = swap(held[m], 1)
        return pieces

    def assemble(pieces, here):
        keys = sorted(pieces)
        rows, cols = pieces[keys[0]].shape
        width = cols // (n_head // 2) // 4
        inner = width * n_head

        def kernel(place_ref, *refs):
            sources, (query_ref, kv_ref, out_ref) = refs[:-3], refs[-3:]
            for (m, side), ref in zip(keys, sources):
                at = pl.ds(pl.multiple_of((place_ref[0] ^ m) * rows, rows), rows)
                for k in range(n_head // 2):
                    s = side * (n_head // 2) + k
                    head = lax.rem(place_ref[1] + n_head - s, n_head)
                    base = k * 4 * width
                    to = pl.ds(pl.multiple_of(head * width, width), width)
                    to_value = pl.ds(pl.multiple_of(inner + head * width, width), width)
                    query_ref[at, to] = ref[:, base : base + width]
                    kv_ref[at, to] = ref[:, base + width : base + 2 * width]
                    kv_ref[at, to_value] = ref[:, base + 2 * width : base + 3 * width]
                    out_ref[at, to] = ref[:, base + 3 * width : base + 4 * width]

        return pl.pallas_call(
            kernel,
            grid_spec=pltpu.PrefetchScalarGridSpec(
                num_scalar_prefetch=1,
                grid=(1,),
                in_specs=[pl.BlockSpec((rows, cols), lambda n, at: (0, 0)) for _ in keys],
                out_specs=[
                    pl.BlockSpec((D, inner), lambda n, at: (0, 0)),
                    pl.BlockSpec((D, 2 * inner), lambda n, at: (0, 0)),
                    pl.BlockSpec((D, inner), lambda n, at: (0, 0)),
                ],
            ),
            out_shape=[jax.ShapeDtypeStruct((D, c), bf16) for c in (inner, 2 * inner, inner)],
            name="assemble",
        )(here, *[pieces[key] for key in keys])

    def assemble_units(pieces, here):
        keys = sorted(pieces)
        rows, cols = pieces[keys[0]].shape
        cols = cols // (n_head // 2)

        def kernel(place_ref, *refs):
            sources, out_ref = refs[:-1], refs[-1]
            for (m, side), ref in zip(keys, sources):
                for k in range(n_head // 2):
                    s = side * (n_head // 2) + k
                    head = lax.rem(place_ref[1] + n_head - s, n_head)
                    at = head * D + (place_ref[0] ^ m) * rows
                    out_ref[pl.ds(pl.multiple_of(at, rows), rows), :] = ref[
                        :, k * cols : (k + 1) * cols
                    ]

        return pl.pallas_call(
            kernel,
            grid_spec=pltpu.PrefetchScalarGridSpec(
                num_scalar_prefetch=1,
                grid=(1,),
                in_specs=[
                    pl.BlockSpec(pieces[key].shape, lambda n, at: (0, 0)) for key in keys
                ],
                out_specs=pl.BlockSpec((n_head * D, cols), lambda n, at: (0, 0)),
            ),
            out_shape=jax.ShapeDtypeStruct((n_head * D, cols), bf16),
            name="assemble_units",
        )(here, *[pieces[key] for key in keys])

    def scatter(keep, send):
        arrived = swap(send, 1)
        _, total_cols = keep.shape
        half = total_cols // 2
        sides = []
        for bits, side in zip(paths, (0, 1)):
            cols = slice(side * half, (side + 1) * half)
            terms = [keep[:, cols], arrived[:, cols]]
            for bit in bits[::-1]:
                middle = terms[0].shape[0] // 2
                away = sum(t[middle:].astype(f32) for t in terms).astype(bf16)
                came = swap(away, bit)
                terms = [t[:middle] for t in terms] + [came]
            sides.append(terms)
        width = total_cols // n_head
        per_side = n_head // 2

        def piece(s):
            at = s % per_side
            cols = slice(at * width, (at + 1) * width)
            return sum(t[:, cols].astype(f32) for t in sides[s // per_side])

        total = piece(0)
        for s in range(1, n_head):
            total = total + shift(piece(s).astype(bf16), n_head - s).astype(f32)
        return total

    def sum_everywhere(values_in):
        steps = [(swap, 1 << b) for b in range(n_dp.bit_length() - 1)]
        steps = steps + [(swap_head, 1 << b) for b in range(n_head.bit_length() - 1)]
        for exchange, bit in steps[:-1]:
            values_in = values_in + exchange(values_in, bit)
        exchange, bit = steps[-1]
        return (values_in, exchange(values_in, bit))

    def place_rows(blocks, here):
        rows, cols = blocks[0].shape

        def kernel(place_ref, *refs):
            away = lax.rem(place_ref[1] + n_head - pl.program_id(0), n_head)
            for s in range(n_head):

                @pl.when(away == s)
                def _(s=s):
                    refs[-1][...] = refs[s][...].astype(f32)

        return pl.pallas_call(
            kernel,
            grid_spec=pltpu.PrefetchScalarGridSpec(
                num_scalar_prefetch=1,
                grid=(n_head,),
                in_specs=[pl.BlockSpec((rows, cols), lambda n, at: (0, 0))] * n_head,
                out_specs=pl.BlockSpec((rows, cols), lambda n, at: (n, 0)),
            ),
            out_shape=jax.ShapeDtypeStruct((n_head * rows, cols), f32),
            name="place_rows",
        )(here, *blocks)

    def share_rows(own, here):
        rows = own.shape[0]
        below, above = [own], [own]
        for _ in range(1, n_head):
            below.append(lax.ppermute(below[-1], "head", [(j, j + 1) for j in range(n_head - 1)]))
            above.append(lax.ppermute(above[-1], "head", [(j, j - 1) for j in range(1, n_head)]))

        def kernel(place_ref, own_ref, *refs):
            lower, upper, out_ref = refs[: n_head - 1], refs[n_head - 1 : -1], refs[-1]
            away = pl.program_id(0) - place_ref[1]

            @pl.when(away == 0)
            def _():
                out_ref[...] = own_ref[...].astype(f32)

            for s in range(1, n_head):

                @pl.when(away == -s)
                def _(s=s):
                    out_ref[...] = lower[s - 1][...].astype(f32)

                @pl.when(away == s)
                def _(s=s):
                    out_ref[...] = upper[s - 1][...].astype(f32)

        one = pl.BlockSpec((rows, D), lambda n, at: (0, 0))
        return pl.pallas_call(
            kernel,
            grid_spec=pltpu.PrefetchScalarGridSpec(
                num_scalar_prefetch=1,
                grid=(n_head,),
                in_specs=[one] * (2 * n_head - 1),
                out_specs=pl.BlockSpec((rows, D), lambda n, at: (n, 0)),
            ),
            out_shape=jax.ShapeDtypeStruct((n_head * rows, D), f32),
            name="share_rows",
        )(here, own, *below[1:], *above[1:])

    def per_device(
        latents,
        media_tokens,
        image_counts,
        time_table,
        media_gain,
        media_bias,
        latent_gain,
        latent_bias,
        feed_gain,
        feed_bias,
        query_weight,
        key_weight,
        value_weight,
        out_weight,
        up_weight,
        down_weight,
        cotangent,
    ):
        me = lax.axis_index("dp")
        my_head = lax.axis_index("head")
        here = jnp.stack([me, my_head]).astype(jnp.int32)
        images_dp = latents.shape[0] // LAT
        images = images_dp // n_head
        lat_rows = images * LAT
        media_rows = images * PATCH

        pieces = gather(
            jnp.concatenate([query_weight, key_weight, value_weight, out_weight.T], axis=1)
        )
        down_turned = down_weight.T
        main = lax.all_gather(
            jnp.concatenate([up_weight[:, EARLY:], down_turned[:, EARLY:]], axis=1),
            ("head", "dp"),
            axis=0,
            tiled=True,
        )
        query_full, kv_full, out_full = assemble(pieces, here)
        extra = assemble_units(
            gather(jnp.concatenate([up_weight[:, :EARLY], down_turned[:, :EARLY]], axis=1)), here
        )

        cot_cols = cotangent.shape[1]
        grad_out = jnp.zeros((lat_rows, D), bf16)
        for s in range(n_head):
            target = (my_head + s) % n_head
            block = lax.dynamic_slice_in_dim(cotangent, target * lat_rows, lat_rows, 0)
            if s:
                block = shift(block, s)
            source = (my_head - s) % n_head
            grad_out = lax.dynamic_update_slice_in_dim(grad_out, block, source * cot_cols, 1)

        first_image = me * images_dp + my_head * images
        counts_sum = jnp.cumsum(image_counts)
        starts = counts_sum - image_counts
        image_index = first_image + jnp.arange(images, dtype=jnp.int32)
        latest = jnp.max(
            jnp.where(starts[None, :] <= image_index[:, None], starts[None, :], 0), axis=1
        )
        media_slots = image_index - latest
        slot_match = media_slots[:, None] == jnp.arange(MAX_MEDIA, dtype=jnp.int32)[None, :]
        per_image = jnp.dot(slot_match.astype(bf16), time_table, preferred_element_type=f32)
        media_own = lax.dynamic_slice_in_dim(media_tokens, my_head * media_rows, media_rows, 0)
        latents_own = lax.dynamic_slice_in_dim(latents, my_head * lat_rows, lat_rows, 0)
        latents_own = latents_own.astype(f32)

        media_sum = (
            media_own.reshape(images, PATCH, D).astype(f32) + per_image[:, None, :]
        ).reshape(media_rows, D)
        media_scaled, _ = norm_stats(media_sum)
        media_norm = (media_scaled * media_gain + media_bias).astype(bf16)
        latent_scaled, latent_inverse = norm_stats(latents_own)
        latent_norm = (latent_scaled * latent_gain + latent_bias).astype(bf16)

        query = mm(latent_norm, query_full).astype(bf16)
        media_kv = mm(media_norm, kv_full).astype(bf16)
        latent_kv = mm(latent_norm, kv_full).astype(bf16)
        mixed = attend(query, media_kv, latent_kv)
        hidden = latents_own + mm_nt(mixed, out_full)
        feed_norm = (norm_stats(hidden)[0] * feed_gain + feed_bias).astype(bf16)

        activation, d_up = hidden_units(feed_norm, grad_out, main, extra)
        down_send = unit_grad(grad_out, activation, here, 1)
        down_keep = unit_grad(grad_out, activation, here, 0)
        down_grad = scatter(down_keep, down_send)
        like = jax.ShapeDtypeStruct
        (result,) = to_features(
            feed_out_kernel, activation, main, extra, 1, [hidden], [like((lat_rows, D), bf16)]
        )
        inner = query_full.shape[1]
        d_hidden, d_attention, d_mixed, feed_gain_part, feed_bias_part = to_features(
            d_feed_kernel,
            d_up,
            main,
            extra,
            0,
            [hidden, grad_out, feed_gain[None, :], out_full],
            [
                like((lat_rows, D), f32),
                like((lat_rows, D), bf16),
                like((lat_rows, inner), bf16),
                like((1, D), f32),
                like((1, D), f32),
            ],
        )

        d_query, d_media_kv, d_latent_kv = attend_back(query, media_kv, latent_kv, d_mixed)
        d_latent_norm = mm_nt(d_query, query_full) + mm_nt(d_latent_kv, kv_full)
        latent_gain_part = jnp.sum(d_latent_norm * latent_scaled, axis=0)
        latent_bias_part = jnp.sum(d_latent_norm, axis=0)
        latent_back = d_hidden + norm_back(
            d_latent_norm, latent_scaled, latent_inverse, latent_gain
        )
        latents_grad = share_rows(latent_back.astype(bf16), here)

        media_gain_part, media_bias_part, image_sums = media_back(
            media_tokens, per_image, media_gain, d_media_kv, kv_full, here
        )
        time_part = jnp.dot(slot_match.astype(f32).T, image_sums, precision=highest)
        small = jnp.concatenate(
            [
                time_part,
                jnp.stack(
                    [
                        media_gain_part,
                        media_bias_part,
                        latent_gain_part,
                        latent_bias_part,
                        feed_gain_part[0],
                        feed_bias_part[0],
                    ]
                ),
            ],
            axis=0,
        )
        small, last_small = sum_everywhere(small)

        d_up, _ = lax.optimization_barrier((d_up, media_gain_part))
        up_send = unit_grad(feed_norm, d_up, here, 1)
        up_keep = unit_grad(feed_norm, d_up, here, 0)
        up_grad = scatter(up_keep, up_send)
        sources = (latent_norm, media_norm, d_attention, d_query, d_media_kv, d_latent_kv, mixed)
        attention_send = attention_grad(*sources, here, 1)
        attention_keep = attention_grad(*sources, here, 0)
        attention_grads = scatter(attention_keep, attention_send)
        last_small, attention_grads = lax.optimization_barrier((last_small, attention_grads))
        small = small + last_small
        width = query_weight.shape[1]
        query_grad, key_grad, value_grad, out_grad = [
            attention_grads[:, at * width : (at + 1) * width] for at in range(4)
        ]

        out_cols = D // n_head
        blocks = []
        for s in range(n_head):
            target = (my_head + s) % n_head
            block = lax.dynamic_slice_in_dim(result, target * out_cols, out_cols, 1)
            if s:
                block = shift(block, s)
            blocks.append(block)
        latents_out = place_rows(blocks, here)
        return (
            latents_out,
            latents_grad,
            small[:MAX_MEDIA],
            small[MAX_MEDIA],
            small[MAX_MEDIA + 1],
            small[MAX_MEDIA + 2],
            small[MAX_MEDIA + 3],
            small[MAX_MEDIA + 4],
            small[MAX_MEDIA + 5],
            query_grad,
            key_grad,
            value_grad,
            out_grad.T,
            jnp.roll(up_grad, EARLY, axis=1),
            jnp.roll(down_grad, EARLY, axis=1).T,
        )

    return per_device


def solution(mesh):
    per_device = make_step(mesh.shape["dp"], mesh.shape["head"])
    rows, both, flipped, whole = P("dp", None), P("dp", "head"), P("head", "dp"), P()
    return jax.shard_map(
        per_device,
        mesh=mesh,
        in_specs=(rows, rows)
        + (whole,) * 8
        + (both, both, both, flipped, both, flipped, both),
        out_specs=(both, rows) + (whole,) * 7 + (both, both, both, flipped, both, flipped),
        check_vma=False,
    )
```

profile of v0, /device:TPU:8, one launch (start us, length us, event | category | flops | bytes accessed | tf_op | source)
XLA Modules:
  0.0 429.8 jit_solution(203067811610853875)
XLA Ops:
  11.0 3.0 collective-permute-start.1
  23.3 3.8 multiply_reduce_fusion
  40.0 3.4 collective-permute-start.17
  48.6 4.3 collective-permute-done.20
  52.9 7.7 %collective-permute-done.19 = bf16[384,256]{1,0:T(8,128)(2,1)S(1)} collective-permute-done((bf16[384,256]{1,0:T(8,128)(2,1)S(1)}, bf16[384,256]{1,0:T(8,128)(2,1)S(1)}, u32[]{:S(2)}, u32[]{:S(2)}) %collective-permute-start.19) | collective-permute-done | bytes 196640 | tf_op jit(solution)/shard_map/ppermute | solution.py:356
  63.4 3.3 add_convert_fusion.refs_4_.refs_5_.refs_6_.refs_7_
  66.8 3.4 fusion.9.refs_0_.refs_1_.refs_2_.refs_3_
  70.2 8.3 %collective-permute-done.18 = bf16[384,256]{1,0:T(8,128)(2,1)S(1)} collective-permute-done((bf16[384,256]{1,0:T(8,128)(2,1)S(1)}, bf16[384,256]{1,0:T(8,128)(2,1)S(1)}, u32[]{:S(2)}, u32[]{:S(2)}) %collective-permute-start.18) | collective-permute-done | bytes 196640 | tf_op jit(solution)/shard_map/ppermute | solution.py:356
  85.8 2.7 collective-permute-done.6.refs_5_
  91.7 6.6 %collective-permute-done.14.refs_13_ = bf16[128,1024]{1,0:T(8,128)(2,1)S(1)} collective-permute-done((bf16[128,1024]{1,0:T(8,128)(2,1)}, bf16[128,1024]{1,0:T(8,128)(2,1)S(1)}, u32[]{:S(2)}, u32[]{:S(2)}) %collective-permute-start.14) | collective-permute-done | bytes 262176 | tf_op jit(solution)/shard_map/ppermute | solution.py:353
  107.2 5.7 %assemble.1 = (bf16[1024,512]{1,0:T(8,128)(2,1)}, bf16[1024,1024]{1,0:T(8,128)(2,1)}, bf16[1024,512]{1,0:T(8,128)(2,1)}) custom-call(s32[2]{0:T(128)} %pad_add_fusion.place_ref, bf16[128,1024]{1,0:T(8,128)(2,1)} %constant_dynamic-update-slice_fusion.refs_0_, bf16[128,1024]{1,0:T(8,128)(2,1)} %constant_dynamic-update-slice_fusion.5.refs_1_, ...), custom_call_target="tpu_custom_call" | custom-call | tf_op jit(solution)/shard_map/assemble/pallas_call | solution.py:504
  112.9 7.1 %convolution_convert_fusion.km_ref.vm_ref = bf16[1536,1024]{1,0:T(8,128)(2,1)} fusion(bf16[1536,1024]{1,0:T(8,128)(2,1)S(1)} %add_convert_fusion.refs_4_.refs_5_.refs_6_.refs_7_, bf16[1024,1024]{1,0:T(8,128)(2,1)} %get-tuple-element.34.weight_ref), kind=kOutput, calls=%fused_computation.5 | convolution fusion | flops 3222798336 | bytes 8388608 | tf_op jit(solution)/shard_map/dot_general | solution.py:25
  126.4 2.8 collective-permute-done.33.refs_12_
  132.6 7.3 %attend.1.refs_17_ = bf16[384,512]{1,0:T(8,128)(2,1)} custom-call(bf16[384,512]{1,0:T(8,128)(2,1)} %convolution_convert_fusion.2.q_ref, bf16[1536,1024]{1,0:T(8,128)(2,1)} %convolution_convert_fusion.km_ref.vm_ref, bf16[384,1024]{1,0:T(8,128)(2,1)} %convolution_convert_fusion.1.kl_ref.vl_ref, bf16[1536,1024]{1,0:T(8,128)(2,1)} %convolution_convert_fusion.km_ref.vm_ref, ...), custom_call_target="tpu_custom_call" | custom-call | tf_op jit(solution)/shard_map/attend/pallas_call | solution.py:130
  141.0 5.1 %assemble_units.1.up_more.down_more.more_ref = bf16[4096,512]{1,0:T(8,128)(2,1)} custom-call(s32[2]{0:T(128)} %pad_add_fusion.place_ref, bf16[128,1024]{1,0:T(8,128)(2,1)} %copy-done.17, bf16[128,1024]{1,0:T(8,128)(2,1)} %constant_dynamic-update-slice_fusion.7.refs_1_, bf16[128,1024]{1,0:T(8,128)(2,1)} %collective-permute-done.23.refs_2_, ...), custom_call_target="tpu_custom_call" | custom-call | tf_op jit(solution)/shard_map/assemble_units/pallas_call | solution.py:536
  149.5 12.6 %hidden_units.1 = (bf16[384,4096]{1,0:T(8,128)(2,1)}, bf16[384,4096]{1,0:T(8,128)(2,1)}) custom-call(bf16[384,1024]{1,0:T(8,128)(2,1)} %add_convert_fusion.5.norm_ref.refs_0_.refs_1_.refs_2_.refs_3_, bf16[384,1024]{1,0:T(8,128)(2,1)} %constant_dynamic-update-slice_fusion.9.grad_ref.refs_0_.refs_1_.refs_2_.refs_3_, ...), custom_call_target="tpu_custom_call" | custom-call | flops 6442450944 | bytes 16777216 | tf_op jit(solution)/shard_map/hidden_units/pallas_call | solution.py:201
  162.1 11.5 %shard_map.281 = (f32[384,1024]{1,0:T(8,128)}, bf16[384,1024]{1,0:T(8,128)(2,1)}, bf16[384,512]{1,0:T(8,128)(2,1)}, f32[1,1024]{1,0:T(1,128)}, f32[1,1024]{1,0:T(1,128)}) custom-call(bf16[384,4096]{1,0:T(8,128)(2,1)} %get-tuple-element.37.units_ref.refs_4_, bf16[4096,1536]{1,0:T(8,128)(2,1)} %all-gather.2.cloned.1.call-done.up_ref.down_ref.weight_ref, ...), custom_call_target="tpu_custom_call" | custom-call | flops 3221225472 | bytes 8388608 | tf_op jit(solution)/shard_map/pallas_call | solution.py:264
  173.6 11.4 %attend_back.1 = (bf16[384,512]{1,0:T(8,128)(2,1)}, bf16[1536,1024]{1,0:T(8,128)(2,1)}, bf16[384,1024]{1,0:T(8,128)(2,1)}) custom-call(bf16[384,512]{1,0:T(8,128)(2,1)} %convolution_convert_fusion.2.q_ref, bf16[1536,1024]{1,0:T(8,128)(2,1)} %convolution_convert_fusion.km_ref.vm_ref, bf16[384,1024]{1,0:T(8,128)(2,1)} %convolution_convert_fusion.1.kl_ref.vl_ref, ...), custom_call_target="tpu_custom_call" | custom-call | tf_op jit(solution)/shard_map/attend_back/pallas_call | solution.py:149
  185.0 6.9 %unit_grad.7 = bf16[512,4096]{1,0:T(8,128)(2,1)} custom-call(s32[2]{0:T(128)} %pad_add_fusion.place_ref, bf16[384,1024]{1,0:T(8,128)(2,1)} %constant_dynamic-update-slice_fusion.9.grad_ref.refs_0_.refs_1_.refs_2_.refs_3_, bf16[384,1024]{1,0:T(8,128)(2,1)} %constant_dynamic-update-slice_fusion.9.grad_ref.refs_0_.refs_1_.refs_2_.refs_3_, ...), custom_call_target="tpu_custom_call" | custom-call | flops 1610612736 | bytes 4194304 | tf_op jit(solution)/shard_map/unit_grad/pallas_call | solution.py:407
  192.6 8.9 %attention_grad.3 = bf16[512,2048]{1,0:T(8,128)(2,1)} custom-call(s32[2]{0:T(128)} %pad_add_fusion.place_ref, bf16[384,1024]{1,0:T(8,128)(2,1)} %fusion.9.refs_0_.refs_1_.refs_2_.refs_3_, bf16[384,1024]{1,0:T(8,128)(2,1)} %fusion.9.refs_0_.refs_1_.refs_2_.refs_3_, bf16[384,1024]{1,0:T(8,128)(2,1)} %fusion.9.refs_0_.refs_1_.refs_2_.refs_3_, ...), custom_call_target="tpu_custom_call" | custom-call | flops 2415919104 | bytes 2097152 | tf_op jit(solution)/shard_map/attention_grad/pallas_call | solution.py:443
  201.5 7.0 %unit_grad.5 = bf16[512,4096]{1,0:T(8,128)(2,1)} custom-call(s32[2]{0:T(128)} %pad_add_fusion.place_ref, bf16[384,1024]{1,0:T(8,128)(2,1)} %add_convert_fusion.5.norm_ref.refs_0_.refs_1_.refs_2_.refs_3_, bf16[384,1024]{1,0:T(8,128)(2,1)} %add_convert_fusion.5.norm_ref.refs_0_.refs_1_.refs_2_.refs_3_, ...), custom_call_target="tpu_custom_call" | custom-call | flops 1610612736 | bytes 4194304 | tf_op jit(solution)/shard_map/unit_grad/pallas_call | solution.py:407
  212.9 4.8 %collective-permute-start.43 = (bf16[384,1024]{1,0:T(8,128)(2,1)S(1)}, bf16[384,1024]{1,0:T(8,128)(2,1)S(1)}, u32[]{:S(2)}, u32[]{:S(2)}) collective-permute-start(bf16[384,1024]{1,0:T(8,128)(2,1)S(1)} %fusion.14.own_ref), channel_id=1, source_target_pairs={{1,0},{2,1},{3,2},{5,4},{6,5},{7,6},{9,8},{10,9},{11,10},{13,12},{... | collective-permute-start | bytes 2359304 | tf_op jit(solution)/shard_map/ppermute | solution.py:613
  217.8 11.0 %media_back.1 = (f32[1,1024]{1,0:T(1,128)}, f32[1,1024]{1,0:T(1,128)}, f32[6,1,1024]{2,1,0:T(1,128)}) custom-call(s32[2]{0:T(128)} %pad_add_fusion.place_ref, bf16[6144,1024]{1,0:T(8,128)(2,1)} %tokens_ref.1, f32[6,1,1024]{2,1,0:T(1,128)} %broadcast_in_dim.21.added_ref, f32[1,1024]{1,0:T(1,128)} %bitcast.50, ...), custom_call_target="tpu_custom_call" | custom-call | flops 3221225472 | bytes 6291456 | tf_op jit(solution)/shard_map/media_back/pallas_call | solution.py:300
  233.5 8.7 %attention_grad.2 = bf16[512,2048]{1,0:T(8,128)(2,1)} custom-call(s32[2]{0:T(128)} %pad_add_fusion.place_ref, bf16[384,1024]{1,0:T(8,128)(2,1)} %fusion.9.refs_0_.refs_1_.refs_2_.refs_3_, bf16[384,1024]{1,0:T(8,128)(2,1)} %fusion.9.refs_0_.refs_1_.refs_2_.refs_3_, bf16[384,1024]{1,0:T(8,128)(2,1)} %fusion.9.refs_0_.refs_1_.refs_2_.refs_3_, ...), custom_call_target="tpu_custom_call" | custom-call | flops 2415919104 | bytes 2097152 | tf_op jit(solution)/shard_map/attention_grad/pallas_call | solution.py:443
  245.1 2.9 add_convert_fusion.11
  250.3 7.1 %unit_grad.4 = bf16[512,4096]{1,0:T(8,128)(2,1)} custom-call(s32[2]{0:T(128)} %pad_add_fusion.place_ref, bf16[384,1024]{1,0:T(8,128)(2,1)} %add_convert_fusion.5.norm_ref.refs_0_.refs_1_.refs_2_.refs_3_, bf16[384,1024]{1,0:T(8,128)(2,1)} %add_convert_fusion.5.norm_ref.refs_0_.refs_1_.refs_2_.refs_3_, ...), custom_call_target="tpu_custom_call" | custom-call | flops 1610612736 | bytes 4194304 | tf_op jit(solution)/shard_map/unit_grad/pallas_call | solution.py:407
  258.2 5.4 %collective-permute-done.40.refs_0_ = bf16[384,1024]{1,0:T(8,128)(2,1)} collective-permute-done((bf16[384,1024]{1,0:T(8,128)(2,1)S(1)}, bf16[384,1024]{1,0:T(8,128)(2,1)}, u32[]{:S(2)}, u32[]{:S(2)}) %collective-permute-start.40) | collective-permute-done | bytes 786464 | tf_op jit(solution)/shard_map/ppermute | solution.py:612
  263.6 3.9 collective-permute-start.44
  272.1 8.9 %shard_map.280 = bf16[384,1024]{1,0:T(8,128)(2,1)} custom-call(bf16[384,4096]{1,0:T(8,128)(2,1)} %get-tuple-element.36.units_ref.refs_4_, bf16[4096,1536]{1,0:T(8,128)(2,1)} %all-gather.2.cloned.1.call-done.up_ref.down_ref.weight_ref, bf16[4096,512]{1,0:T(8,128)(2,1)} %assemble_units.1.up_more.down_more.more_ref, f32[384,1024]{1,0:T(8,128)} %copy-done.4), custom_call_target="tpu_custom_call" | custom-call | flops 3221225472 | bytes 8388608 | tf_op jit(solution)/shard_map/pallas_call | solution.py:264
  284.0 6.9 %unit_grad.6 = bf16[512,4096]{1,0:T(8,128)(2,1)} custom-call(s32[2]{0:T(128)} %pad_add_fusion.place_ref, bf16[384,1024]{1,0:T(8,128)(2,1)} %constant_dynamic-update-slice_fusion.9.grad_ref.refs_0_.refs_1_.refs_2_.refs_3_, bf16[384,1024]{1,0:T(8,128)(2,1)} %constant_dynamic-update-slice_fusion.9.grad_ref.refs_0_.refs_1_.refs_2_.refs_3_, ...), custom_call_target="tpu_custom_call" | custom-call | flops 1610612736 | bytes 4194304 | tf_op jit(solution)/shard_map/unit_grad/pallas_call | solution.py:407
  290.9 2.9 collective-permute-start.39
  297.3 3.2 collective-permute-start.38
  301.2 3.3 collective-permute-start.45
  304.5 3.1 collective-permute-start.42
  307.5 4.4 %add_convert_fusion.2 = (bf16[256,2048]{1,0:T(8,128)(2,1)}, bf16[256,2048]{1,0:T(8,128)(2,1)}) fusion(bf16[512,4096]{1,0:T(8,128)(2,1)} %collective-permute-done.67, bf16[512,4096]{1,0:T(8,128)(2,1)} %unit_grad.6), kind=kLoop, calls=%fused_computation.10 | loop fusion | flops 4194304 | bytes 6291456 | tf_op jit(solution)/shard_map/convert_element_type | solution.py:560
  314.8 3.7 add_convert_fusion.4
  318.6 12.1 %collective-permute-done.45.refs_5_ = bf16[384,1024]{1,0:T(8,128)(2,1)S(1)} collective-permute-done((bf16[384,1024]{1,0:T(8,128)(2,1)S(1)}, bf16[384,1024]{1,0:T(8,128)(2,1)S(1)}, u32[]{:S(2)}, u32[]{:S(2)}) %collective-permute-start.45) | collective-permute-done | bytes 786464 | tf_op jit(solution)/shard_map/ppermute | solution.py:613
  335.2 4.0 collective-permute-done.58
  341.9 3.6 place_rows.1
  345.5 6.4 %share_rows.1 = f32[1536,1024]{1,0:T(8,128)} custom-call(s32[2]{0:T(128)} %pad_add_fusion.place_ref, bf16[384,1024]{1,0:T(8,128)(2,1)} %copy-done.12, bf16[384,1024]{1,0:T(8,128)(2,1)} %collective-permute-done.40.refs_0_, bf16[384,1024]{1,0:T(8,128)(2,1)} %collective-permute-done.41.refs_1_, bf16[384,1024]{1,0:T(8,128)(2,1)} %copy-done.21, ...), custom_call_target="tpu_custom_call" | custom-call | tf_op jit(solution)/shard_map/share_rows/pallas_call | solution.py:634
  353.6 3.5 collective-permute-done.50
  357.1 3.4 add_convert_fusion.7
  363.3 3.2 add_convert_fusion.9
  370.4 5.1 %collective-permute-done.69 = bf16[128,2048]{1,0:T(8,128)(2,1)S(1)} collective-permute-done((bf16[128,2048]{1,0:T(8,128)(2,1)}, bf16[128,2048]{1,0:T(8,128)(2,1)S(1)}, u32[]{:S(2)}, u32[]{:S(2)}) %collective-permute-start.69) | collective-permute-done | bytes 524320 | tf_op jit(solution)/shard_map/ppermute | solution.py:353
  388.5 6.0 %collective-permute-done.73 = bf16[128,1024]{1,0:T(8,128)(2,1)S(1)} collective-permute-done((bf16[128,1024]{1,0:T(8,128)(2,1)S(1)}, bf16[128,1024]{1,0:T(8,128)(2,1)S(1)}, u32[]{:S(2)}, u32[]{:S(2)}) %collective-permute-start.73) | collective-permute-done | bytes 262176 | tf_op jit(solution)/shard_map/ppermute | solution.py:356
  394.5 7.7 %collective-permute-start.62 = (bf16[128,1024]{1,0:T(8,128)(2,1)S(1)}, bf16[128,1024]{1,0:T(8,128)(2,1)S(1)}, u32[]{:S(2)}, u32[]{:S(2)}) collective-permute-start(bf16[128,1024]{1,0:T(8,128)(2,1)S(1)} %get-tuple-element.109), channel_id=1, source_target_pairs={{0,3},{1,0},{2,1},{3,2},{4,7},{5,4},{6,5},{7,6},{8,11},{9,8},{10,9... | collective-permute-start | bytes 786440 | tf_op jit(solution)/shard_map/ppermute | solution.py:356
  402.2 6.8 %collective-permute-done.74 = bf16[128,1024]{1,0:T(8,128)(2,1)S(1)} collective-permute-done((bf16[128,1024]{1,0:T(8,128)(2,1)S(1)}, bf16[128,1024]{1,0:T(8,128)(2,1)S(1)}, u32[]{:S(2)}, u32[]{:S(2)}) %collective-permute-start.74) | collective-permute-done | bytes 262176 | tf_op jit(solution)/shard_map/ppermute | solution.py:356
  414.6 2.8 collective-permute-done.66
  (358 shorter events, 136.9 us)
Async XLA Ops:
  7.3 142.3 %all-gather.2.cloned.1.call-start = ((), (), s32[]{:S(2)}) async-start(), calls=%async_computation | async-start | bytes 12976128 | tf_op jit(solution)/shard_map/all_gather | solution.py:677
  11.0 26.3 %collective-permute-start.2 = (bf16[128,512]{1,0:T(8,128)(2,1)}, bf16[128,512]{1,0:T(8,128)(2,1)S(1)}, u32[]{:S(2)}, u32[]{:S(2)}) collective-permute-start(bf16[128,512]{1,0:T(8,128)(2,1)} %pad_maximum_fusion.3), channel_id=1, source_target_pairs={{0,3},{1,0},{2,1},{3,2},{4,7},{5,4},{6,5},{7,6},{8,11},{9,8},{10,9... | collective-permute-start | bytes 393224 | tf_op jit(solution)/shard_map/ppermute | solution.py:356
  11.0 22.4 %collective-permute-start.1 = (bf16[128,512]{1,0:T(8,128)(2,1)}, bf16[128,512]{1,0:T(8,128)(2,1)}, u32[]{:S(2)}, u32[]{:S(2)}) collective-permute-start(bf16[128,512]{1,0:T(8,128)(2,1)} %pad_maximum_fusion.3), channel_id=1, source_target_pairs={{0,2},{1,3},{2,0},{3,1},{4,6},{5,7},{6,4},{7,5},{8,10},{9,11},{10,... | collective-permute-start | bytes 393224 | tf_op jit(solution)/shard_map/ppermute | solution.py:356
  14.0 26.0 %collective-permute-start = (bf16[128,512]{1,0:T(8,128)(2,1)}, bf16[128,512]{1,0:T(8,128)(2,1)}, u32[]{:S(2)}, u32[]{:S(2)}) collective-permute-start(bf16[128,512]{1,0:T(8,128)(2,1)} %pad_maximum_fusion.3), channel_id=1, source_target_pairs={{0,1},{1,2},{2,3},{3,0},{4,5},{5,6},{6,7},{7,4},{8,9},{9,10},{10,1... | collective-permute-start | bytes 393224 | tf_op jit(solution)/shard_map/ppermute | solution.py:356
  18.0 27.0 %collective-permute-start.22 = (bf16[128,512]{1,0:T(8,128)(2,1)}, bf16[128,512]{1,0:T(8,128)(2,1)}, u32[]{:S(2)}, u32[]{:S(2)}) collective-permute-start(bf16[128,512]{1,0:T(8,128)(2,1)} %pad_maximum_fusion.4), channel_id=1, source_target_pairs={{0,3},{1,0},{2,1},{3,2},{4,7},{5,4},{6,5},{7,6},{8,11},{9,8},{10,9... | collective-permute-start | bytes 393224 | tf_op jit(solution)/shard_map/ppermute | solution.py:356
  18.0 29.1 %collective-permute-start.21 = (bf16[128,512]{1,0:T(8,128)(2,1)}, bf16[128,512]{1,0:T(8,128)(2,1)}, u32[]{:S(2)}, u32[]{:S(2)}) collective-permute-start(bf16[128,512]{1,0:T(8,128)(2,1)} %pad_maximum_fusion.4), channel_id=1, source_target_pairs={{0,2},{1,3},{2,0},{3,1},{4,6},{5,7},{6,4},{7,5},{8,10},{9,11},{10,... | collective-permute-start | bytes 393224 | tf_op jit(solution)/shard_map/ppermute | solution.py:356
  33.4 19.5 %collective-permute-start.20 = (bf16[128,512]{1,0:T(8,128)(2,1)}, bf16[128,512]{1,0:T(8,128)(2,1)S(1)}, u32[]{:S(2)}, u32[]{:S(2)}) collective-permute-start(bf16[128,512]{1,0:T(8,128)(2,1)} %pad_maximum_fusion.4), channel_id=1, source_target_pairs={{0,1},{1,2},{2,3},{3,0},{4,5},{5,6},{6,7},{7,4},{8,9},{9,10},{10,1... | collective-permute-start | bytes 393224 | tf_op jit(solution)/shard_map/ppermute | solution.py:356
  37.9 22.6 %collective-permute-start.19 = (bf16[384,256]{1,0:T(8,128)(2,1)S(1)}, bf16[384,256]{1,0:T(8,128)(2,1)S(1)}, u32[]{:S(2)}, u32[]{:S(2)}) collective-permute-start(bf16[384,256]{1,0:T(8,128)(2,1)S(1)} %get-tuple-element.125), channel_id=1, source_target_pairs={{0,3},{1,0},{2,1},{3,2},{4,7},{5,4},{6,5},{7,6},{8,11},{9,8},{10,9... | collective-permute-start | bytes 589832 | tf_op jit(solution)/shard_map/ppermute | solution.py:356
  40.0 26.7 %collective-permute-start.17 = (bf16[384,256]{1,0:T(8,128)(2,1)}, bf16[384,256]{1,0:T(8,128)(2,1)}, u32[]{:S(2)}, u32[]{:S(2)}) collective-permute-start(bf16[384,256]{1,0:T(8,128)(2,1)} %get-tuple-element.126), channel_id=1, source_target_pairs={{0,1},{1,2},{2,3},{3,0},{4,5},{5,6},{6,7},{7,4},{8,9},{9,10},{10,1... | collective-permute-start | bytes 589832 | tf_op jit(solution)/shard_map/ppermute | solution.py:356
  45.0 35.0 %collective-permute-start.9 = (bf16[128,1024]{1,0:T(8,128)(2,1)}, bf16[128,1024]{1,0:T(8,128)(2,1)}, u32[]{:S(2)}, u32[]{:S(2)}) collective-permute-start(bf16[128,1024]{1,0:T(8,128)(2,1)} %constant_dynamic-update-slice_fusion.refs_0_), channel_id=1, source_target_pairs={{0,16},{4,20},{8,24},{12,28},{16,0},{20,4},{24,8},{28,12},{1,17},{... | collective-permute-start | bytes 786440 | tf_op jit(solution)/shard_map/ppermute | solution.py:353
  47.1 32.9 %collective-permute-start.5 = (bf16[128,1024]{1,0:T(8,128)(2,1)}, bf16[128,1024]{1,0:T(8,128)(2,1)}, u32[]{:S(2)}, u32[]{:S(2)}) collective-permute-start(bf16[128,1024]{1,0:T(8,128)(2,1)} %constant_dynamic-update-slice_fusion.refs_0_), channel_id=1, source_target_pairs={{0,8},{4,12},{8,0},{12,4},{16,24},{20,28},{24,16},{28,20},{1,9},{5... | collective-permute-start | bytes 786440 | tf_op jit(solution)/shard_map/ppermute | solution.py:353
  52.9 27.6 %collective-permute-start.3 = (bf16[128,1024]{1,0:T(8,128)(2,1)}, bf16[128,1024]{1,0:T(8,128)(2,1)}, u32[]{:S(2)}, u32[]{:S(2)}) collective-permute-start(bf16[128,1024]{1,0:T(8,128)(2,1)} %constant_dynamic-update-slice_fusion.refs_0_), channel_id=1, source_target_pairs={{0,4},{4,0},{8,12},{12,8},{16,20},{20,16},{24,28},{28,24},{1,5},{5... | collective-permute-start | bytes 786440 | tf_op jit(solution)/shard_map/ppermute | solution.py:353
  60.6 21.5 %collective-permute-start.10 = (bf16[128,1024]{1,0:T(8,128)(2,1)}, bf16[128,1024]{1,0:T(8,128)(2,1)}, u32[]{:S(2)}, u32[]{:S(2)}) collective-permute-start(bf16[128,1024]{1,0:T(8,128)(2,1)} %constant_dynamic-update-slice_fusion.5.refs_1_), channel_id=1, source_target_pairs={{0,16},{4,20},{8,24},{12,28},{16,0},{20,4},{24,8},{28,12},{1,17},{... | collective-permute-start | bytes 786440 | tf_op jit(solution)/shard_map/ppermute | solution.py:353
  82.1 16.2 %collective-permute-start.14 = (bf16[128,1024]{1,0:T(8,128)(2,1)}, bf16[128,1024]{1,0:T(8,128)(2,1)S(1)}, u32[]{:S(2)}, u32[]{:S(2)}) collective-permute-start(bf16[128,1024]{1,0:T(8,128)(2,1)} %collective-permute-done.10.refs_9_), channel_id=1, source_target_pairs={{0,8},{4,12},{8,0},{12,4},{16,24},{20,28},{24,16},{28,20},{1,9},{5... | collective-permute-start | bytes 786440 | tf_op jit(solution)/shard_map/ppermute | solution.py:353
  88.5 14.6 %collective-permute-start.12 = (bf16[128,1024]{1,0:T(8,128)(2,1)}, bf16[128,1024]{1,0:T(8,128)(2,1)S(1)}, u32[]{:S(2)}, u32[]{:S(2)}) collective-permute-start(bf16[128,1024]{1,0:T(8,128)(2,1)} %collective-permute-done.10.refs_9_), channel_id=1, source_target_pairs={{0,4},{4,0},{8,12},{12,8},{16,20},{20,16},{24,28},{28,24},{1,5},{5... | collective-permute-start | bytes 786440 | tf_op jit(solution)/shard_map/ppermute | solution.py:353
  89.0 16.5 %collective-permute-start.8 = (bf16[128,1024]{1,0:T(8,128)(2,1)S(1)}, bf16[128,1024]{1,0:T(8,128)(2,1)S(1)}, u32[]{:S(2)}, u32[]{:S(2)}) collective-permute-start(bf16[128,1024]{1,0:T(8,128)(2,1)S(1)} %collective-permute-done.6.refs_5_), channel_id=1, source_target_pairs={{0,4},{4,0},{8,12},{12,8},{16,20},{20,16},{24,28},{28,24},{1,5},{5... | collective-permute-start | bytes 786440 | tf_op jit(solution)/shard_map/ppermute | solution.py:353
  101.5 18.5 %collective-permute-start.29 = (bf16[128,1024]{1,0:T(8,128)(2,1)S(1)}, bf16[128,1024]{1,0:T(8,128)(2,1)}, u32[]{:S(2)}, u32[]{:S(2)}) collective-permute-start(bf16[128,1024]{1,0:T(8,128)(2,1)S(1)} %pad_maximum_fusion.2.refs_0_), channel_id=1, source_target_pairs={{0,16},{4,20},{8,24},{12,28},{16,0},{20,4},{24,8},{28,12},{1,17},{... | collective-permute-start | bytes 786440 | tf_op jit(solution)/shard_map/ppermute | solution.py:353
  103.1 17.2 %collective-permute-start.25 = (bf16[128,1024]{1,0:T(8,128)(2,1)S(1)}, bf16[128,1024]{1,0:T(8,128)(2,1)}, u32[]{:S(2)}, u32[]{:S(2)}) collective-permute-start(bf16[128,1024]{1,0:T(8,128)(2,1)S(1)} %pad_maximum_fusion.2.refs_0_), channel_id=1, source_target_pairs={{0,8},{4,12},{8,0},{12,4},{16,24},{20,28},{24,16},{28,20},{1,9},{5... | collective-permute-start | bytes 786440 | tf_op jit(solution)/shard_map/ppermute | solution.py:353
  105.5 15.0 %collective-permute-start.23 = (bf16[128,1024]{1,0:T(8,128)(2,1)S(1)}, bf16[128,1024]{1,0:T(8,128)(2,1)}, u32[]{:S(2)}, u32[]{:S(2)}) collective-permute-start(bf16[128,1024]{1,0:T(8,128)(2,1)S(1)} %pad_maximum_fusion.2.refs_0_), channel_id=1, source_target_pairs={{0,4},{4,0},{8,12},{12,8},{16,20},{20,16},{24,28},{28,24},{1,5},{5... | collective-permute-start | bytes 786440 | tf_op jit(solution)/shard_map/ppermute | solution.py:353
  105.6 17.2 %collective-permute-start.30 = (bf16[128,1024]{1,0:T(8,128)(2,1)}, bf16[128,1024]{1,0:T(8,128)(2,1)}, u32[]{:S(2)}, u32[]{:S(2)}) collective-permute-start(bf16[128,1024]{1,0:T(8,128)(2,1)} %constant_dynamic-update-slice_fusion.7.refs_1_), channel_id=1, source_target_pairs={{0,16},{4,20},{8,24},{12,28},{16,0},{20,4},{24,8},{28,12},{1,17},{... | collective-permute-start | bytes 786440 | tf_op jit(solution)/shard_map/ppermute | solution.py:353
  107.1 18.7 %collective-permute-start.26 = (bf16[128,1024]{1,0:T(8,128)(2,1)}, bf16[128,1024]{1,0:T(8,128)(2,1)}, u32[]{:S(2)}, u32[]{:S(2)}) collective-permute-start(bf16[128,1024]{1,0:T(8,128)(2,1)} %constant_dynamic-update-slice_fusion.7.refs_1_), channel_id=1, source_target_pairs={{0,8},{4,12},{8,0},{12,4},{16,24},{20,28},{24,16},{28,20},{1,9},{5... | collective-permute-start | bytes 786440 | tf_op jit(solution)/shard_map/ppermute | solution.py:353
  191.9 112.5 %collective-permute-start.67 = (bf16[512,4096]{1,0:T(8,128)(2,1)}, bf16[512,4096]{1,0:T(8,128)(2,1)}, u32[]{:S(2)}, u32[]{:S(2)}) collective-permute-start(bf16[512,4096]{1,0:T(8,128)(2,1)} %unit_grad.7), channel_id=1, source_target_pairs={{0,4},{4,0},{8,12},{12,8},{16,20},{20,16},{24,28},{28,24},{1,5},{5... | collective-permute-start | bytes 12582920 | tf_op jit(solution)/shard_map/ppermute | solution.py:353
  201.5 42.7 %collective-permute-start.51 = (bf16[512,2048]{1,0:T(8,128)(2,1)}, bf16[512,2048]{1,0:T(8,128)(2,1)}, u32[]{:S(2)}, u32[]{:S(2)}) collective-permute-start(bf16[512,2048]{1,0:T(8,128)(2,1)} %attention_grad.3), channel_id=1, source_target_pairs={{0,4},{4,0},{8,12},{12,8},{16,20},{20,16},{24,28},{28,24},{1,5},{5... | collective-permute-start | bytes 6291464 | tf_op jit(solution)/shard_map/ppermute | solution.py:353
  208.6 104.7 %collective-permute-start.59 = (bf16[512,4096]{1,0:T(8,128)(2,1)}, bf16[512,4096]{1,0:T(8,128)(2,1)}, u32[]{:S(2)}, u32[]{:S(2)}) collective-permute-start(bf16[512,4096]{1,0:T(8,128)(2,1)} %unit_grad.5), channel_id=1, source_target_pairs={{0,4},{4,0},{8,12},{12,8},{16,20},{20,16},{24,28},{28,24},{1,5},{5... | collective-permute-start | bytes 12582920 | tf_op jit(solution)/shard_map/ppermute | solution.py:353
  212.9 36.5 %collective-permute-start.43 = (bf16[384,1024]{1,0:T(8,128)(2,1)S(1)}, bf16[384,1024]{1,0:T(8,128)(2,1)S(1)}, u32[]{:S(2)}, u32[]{:S(2)}) collective-permute-start(bf16[384,1024]{1,0:T(8,128)(2,1)S(1)} %fusion.14.own_ref), channel_id=1, source_target_pairs={{1,0},{2,1},{3,2},{5,4},{6,5},{7,6},{9,8},{10,9},{11,10},{13,12},{... | collective-permute-start | bytes 2359304 | tf_op jit(solution)/shard_map/ppermute | solution.py:613
  242.2 21.4 %collective-permute-start.40 = (bf16[384,1024]{1,0:T(8,128)(2,1)S(1)}, bf16[384,1024]{1,0:T(8,128)(2,1)}, u32[]{:S(2)}, u32[]{:S(2)}) collective-permute-start(bf16[384,1024]{1,0:T(8,128)(2,1)S(1)} %fusion.14.own_ref), channel_id=1, source_target_pairs={{0,1},{1,2},{2,3},{4,5},{5,6},{6,7},{8,9},{9,10},{10,11},{12,13},{... | collective-permute-start | bytes 2359304 | tf_op jit(solution)/shard_map/ppermute | solution.py:612
  248.5 15.1 %collective-permute-start.52 = (bf16[256,1024]{1,0:T(8,128)(2,1)}, bf16[256,1024]{1,0:T(8,128)(2,1)}, u32[]{:S(2)}, u32[]{:S(2)}) collective-permute-start(bf16[256,1024]{1,0:T(8,128)(2,1)} %get-tuple-element.119), channel_id=1, source_target_pairs={{0,16},{4,20},{8,24},{12,28},{16,0},{20,4},{24,8},{28,12},{1,17},{... | collective-permute-start | bytes 1572872 | tf_op jit(solution)/shard_map/ppermute | solution.py:353
  249.3 18.2 %collective-permute-start.55 = (bf16[256,1024]{1,0:T(8,128)(2,1)}, bf16[256,1024]{1,0:T(8,128)(2,1)S(1)}, u32[]{:S(2)}, u32[]{:S(2)}) collective-permute-start(bf16[256,1024]{1,0:T(8,128)(2,1)} %get-tuple-element.120), channel_id=1, source_target_pairs={{0,8},{4,12},{8,0},{12,4},{16,24},{20,28},{24,16},{28,20},{1,9},{5... | collective-permute-start | bytes 1572872 | tf_op jit(solution)/shard_map/ppermute | solution.py:353
  263.6 36.9 %collective-permute-start.44 = (bf16[384,1024]{1,0:T(8,128)(2,1)}, bf16[384,1024]{1,0:T(8,128)(2,1)S(1)}, u32[]{:S(2)}, u32[]{:S(2)}) collective-permute-start(bf16[384,1024]{1,0:T(8,128)(2,1)} %copy-done.18), channel_id=1, source_target_pairs={{1,0},{2,1},{3,2},{5,4},{6,5},{7,6},{9,8},{10,9},{11,10},{13,12},{... | collective-permute-start | bytes 2359304 | tf_op jit(solution)/shard_map/ppermute | solution.py:613
  267.5 33.6 %collective-permute-start.41 = (bf16[384,1024]{1,0:T(8,128)(2,1)}, bf16[384,1024]{1,0:T(8,128)(2,1)}, u32[]{:S(2)}, u32[]{:S(2)}) collective-permute-start(bf16[384,1024]{1,0:T(8,128)(2,1)} %collective-permute-done.40.refs_0_), channel_id=1, source_target_pairs={{0,1},{1,2},{2,3},{4,5},{5,6},{6,7},{8,9},{9,10},{10,11},{12,13},{... | collective-permute-start | bytes 2359304 | tf_op jit(solution)/shard_map/ppermute | solution.py:612
  297.3 14.6 %collective-permute-start.38 = (bf16[384,256]{1,0:T(8,128)(2,1)}, bf16[384,256]{1,0:T(8,128)(2,1)S(1)}, u32[]{:S(2)}, u32[]{:S(2)}) collective-permute-start(bf16[384,256]{1,0:T(8,128)(2,1)} %get-tuple-element.122), channel_id=1, source_target_pairs={{0,2},{1,3},{2,0},{3,1},{4,6},{5,7},{6,4},{7,5},{8,10},{9,11},{10,... | collective-permute-start | bytes 589832 | tf_op jit(solution)/shard_map/ppermute | solution.py:356
  301.2 29.5 %collective-permute-start.45 = (bf16[384,1024]{1,0:T(8,128)(2,1)S(1)}, bf16[384,1024]{1,0:T(8,128)(2,1)S(1)}, u32[]{:S(2)}, u32[]{:S(2)}) collective-permute-start(bf16[384,1024]{1,0:T(8,128)(2,1)S(1)} %collective-permute-done.44.refs_4_), channel_id=1, source_target_pairs={{1,0},{2,1},{3,2},{5,4},{6,5},{7,6},{9,8},{10,9},{11,10},{13,12},{... | collective-permute-start | bytes 2359304 | tf_op jit(solution)/shard_map/ppermute | solution.py:613
  304.5 27.3 %collective-permute-start.42 = (bf16[384,1024]{1,0:T(8,128)(2,1)}, bf16[384,1024]{1,0:T(8,128)(2,1)S(1)}, u32[]{:S(2)}, u32[]{:S(2)}) collective-permute-start(bf16[384,1024]{1,0:T(8,128)(2,1)} %collective-permute-done.41.refs_1_), channel_id=1, source_target_pairs={{0,1},{1,2},{2,3},{4,5},{5,6},{6,7},{8,9},{9,10},{10,11},{12,13},{... | collective-permute-start | bytes 2359304 | tf_op jit(solution)/shard_map/ppermute | solution.py:612
  311.9 22.3 %collective-permute-start.57 = (bf16[128,512]{1,0:T(8,128)(2,1)S(1)}, bf16[128,512]{1,0:T(8,128)(2,1)S(1)}, u32[]{:S(2)}, u32[]{:S(2)}) collective-permute-start(bf16[128,512]{1,0:T(8,128)(2,1)S(1)} %get-tuple-element.114), channel_id=1, source_target_pairs={{0,2},{1,3},{2,0},{3,1},{4,6},{5,7},{6,4},{7,5},{8,10},{9,11},{10,... | collective-permute-start | bytes 393224 | tf_op jit(solution)/shard_map/ppermute | solution.py:356
  312.0 45.0 %collective-permute-start.68 = (bf16[256,2048]{1,0:T(8,128)(2,1)}, bf16[256,2048]{1,0:T(8,128)(2,1)}, u32[]{:S(2)}, u32[]{:S(2)}) collective-permute-start(bf16[256,2048]{1,0:T(8,128)(2,1)} %get-tuple-element.107), channel_id=1, source_target_pairs={{0,16},{4,20},{8,24},{12,28},{16,0},{20,4},{24,8},{28,12},{1,17},{... | collective-permute-start | bytes 3145736 | tf_op jit(solution)/shard_map/ppermute | solution.py:353
  313.3 43.8 %collective-permute-start.71 = (bf16[256,2048]{1,0:T(8,128)(2,1)}, bf16[256,2048]{1,0:T(8,128)(2,1)}, u32[]{:S(2)}, u32[]{:S(2)}) collective-permute-start(bf16[256,2048]{1,0:T(8,128)(2,1)} %get-tuple-element.108), channel_id=1, source_target_pairs={{0,8},{4,12},{8,0},{12,4},{16,24},{20,28},{24,16},{28,20},{1,9},{5... | collective-permute-start | bytes 3145736 | tf_op jit(solution)/shard_map/ppermute | solution.py:353
  330.7 32.7 %collective-permute-start.60 = (bf16[256,2048]{1,0:T(8,128)(2,1)}, bf16[256,2048]{1,0:T(8,128)(2,1)}, u32[]{:S(2)}, u32[]{:S(2)}) collective-permute-start(bf16[256,2048]{1,0:T(8,128)(2,1)} %get-tuple-element.112), channel_id=1, source_target_pairs={{0,16},{4,20},{8,24},{12,28},{16,0},{20,4},{24,8},{28,12},{1,17},{... | collective-permute-start | bytes 3145736 | tf_op jit(solution)/shard_map/ppermute | solution.py:353
  332.7 30.6 %collective-permute-start.63 = (bf16[256,2048]{1,0:T(8,128)(2,1)}, bf16[256,2048]{1,0:T(8,128)(2,1)S(1)}, u32[]{:S(2)}, u32[]{:S(2)}) collective-permute-start(bf16[256,2048]{1,0:T(8,128)(2,1)} %get-tuple-element.113), channel_id=1, source_target_pairs={{0,8},{4,12},{8,0},{12,4},{16,24},{20,28},{24,16},{28,20},{1,9},{5... | collective-permute-start | bytes 3145736 | tf_op jit(solution)/shard_map/ppermute | solution.py:353
  360.5 15.0 %collective-permute-start.69 = (bf16[128,2048]{1,0:T(8,128)(2,1)}, bf16[128,2048]{1,0:T(8,128)(2,1)S(1)}, u32[]{:S(2)}, u32[]{:S(2)}) collective-permute-start(bf16[128,2048]{1,0:T(8,128)(2,1)} %get-tuple-element.105), channel_id=1, source_target_pairs={{0,8},{4,12},{8,0},{12,4},{16,24},{20,28},{24,16},{28,20},{1,9},{5... | collective-permute-start | bytes 1572872 | tf_op jit(solution)/shard_map/ppermute | solution.py:353
  362.1 15.0 %collective-permute-start.72 = (bf16[128,2048]{1,0:T(8,128)(2,1)}, bf16[128,2048]{1,0:T(8,128)(2,1)S(1)}, u32[]{:S(2)}, u32[]{:S(2)}) collective-permute-start(bf16[128,2048]{1,0:T(8,128)(2,1)} %get-tuple-element.106), channel_id=1, source_target_pairs={{0,16},{4,20},{8,24},{12,28},{16,0},{20,4},{24,8},{28,12},{1,17},{... | collective-permute-start | bytes 1572872 | tf_op jit(solution)/shard_map/ppermute | solution.py:353
  366.5 16.6 %collective-permute-start.61 = (bf16[128,2048]{1,0:T(8,128)(2,1)}, bf16[128,2048]{1,0:T(8,128)(2,1)S(1)}, u32[]{:S(2)}, u32[]{:S(2)}) collective-permute-start(bf16[128,2048]{1,0:T(8,128)(2,1)} %get-tuple-element.110), channel_id=1, source_target_pairs={{0,8},{4,12},{8,0},{12,4},{16,24},{20,28},{24,16},{28,20},{1,9},{5... | collective-permute-start | bytes 1572872 | tf_op jit(solution)/shard_map/ppermute | solution.py:353
  367.1 17.5 %collective-permute-start.64 = (bf16[128,2048]{1,0:T(8,128)(2,1)}, bf16[128,2048]{1,0:T(8,128)(2,1)S(1)}, u32[]{:S(2)}, u32[]{:S(2)}) collective-permute-start(bf16[128,2048]{1,0:T(8,128)(2,1)} %get-tuple-element.111), channel_id=1, source_target_pairs={{0,16},{4,20},{8,24},{12,28},{16,0},{20,4},{24,8},{28,12},{1,17},{... | collective-permute-start | bytes 1572872 | tf_op jit(solution)/shard_map/ppermute | solution.py:353
  379.4 15.1 %collective-permute-start.73 = (bf16[128,1024]{1,0:T(8,128)(2,1)S(1)}, bf16[128,1024]{1,0:T(8,128)(2,1)S(1)}, u32[]{:S(2)}, u32[]{:S(2)}) collective-permute-start(bf16[128,1024]{1,0:T(8,128)(2,1)S(1)} %get-tuple-element.100), channel_id=1, source_target_pairs={{0,2},{1,3},{2,0},{3,1},{4,6},{5,7},{6,4},{7,5},{8,10},{9,11},{10,... | collective-permute-start | bytes 786440 | tf_op jit(solution)/shard_map/ppermute | solution.py:356
  379.9 29.2 %collective-permute-start.74 = (bf16[128,1024]{1,0:T(8,128)(2,1)S(1)}, bf16[128,1024]{1,0:T(8,128)(2,1)S(1)}, u32[]{:S(2)}, u32[]{:S(2)}) collective-permute-start(bf16[128,1024]{1,0:T(8,128)(2,1)S(1)} %get-tuple-element.101), channel_id=1, source_target_pairs={{0,1},{1,2},{2,3},{3,0},{4,5},{5,6},{6,7},{7,4},{8,9},{9,10},{10,1... | collective-permute-start | bytes 786440 | tf_op jit(solution)/shard_map/ppermute | solution.py:356
  381.1 29.7 %collective-permute-start.70 = (bf16[128,1024]{1,0:T(8,128)(2,1)S(1)}, bf16[128,1024]{1,0:T(8,128)(2,1)S(1)}, u32[]{:S(2)}, u32[]{:S(2)}) collective-permute-start(bf16[128,1024]{1,0:T(8,128)(2,1)S(1)} %get-tuple-element.104), channel_id=1, source_target_pairs={{0,3},{1,0},{2,1},{3,2},{4,7},{5,4},{6,5},{7,6},{8,11},{9,8},{10,9... | collective-permute-start | bytes 786440 | tf_op jit(solution)/shard_map/ppermute | solution.py:356
  386.6 27.9 %collective-permute-start.65 = (bf16[128,1024]{1,0:T(8,128)(2,1)S(1)}, bf16[128,1024]{1,0:T(8,128)(2,1)S(1)}, u32[]{:S(2)}, u32[]{:S(2)}) collective-permute-start(bf16[128,1024]{1,0:T(8,128)(2,1)S(1)} %get-tuple-element.102), channel_id=1, source_target_pairs={{0,2},{1,3},{2,0},{3,1},{4,6},{5,7},{6,4},{7,5},{8,10},{9,11},{10,... | collective-permute-start | bytes 786440 | tf_op jit(solution)/shard_map/ppermute | solution.py:356
  387.4 30.0 %collective-permute-start.66 = (bf16[128,1024]{1,0:T(8,128)(2,1)S(1)}, bf16[128,1024]{1,0:T(8,128)(2,1)S(1)}, u32[]{:S(2)}, u32[]{:S(2)}) collective-permute-start(bf16[128,1024]{1,0:T(8,128)(2,1)S(1)} %get-tuple-element.103), channel_id=1, source_target_pairs={{0,1},{1,2},{2,3},{3,0},{4,5},{5,6},{6,7},{7,4},{8,9},{9,10},{10,1... | collective-permute-start | bytes 786440 | tf_op jit(solution)/shard_map/ppermute | solution.py:356
  394.5 24.8 %collective-permute-start.62 = (bf16[128,1024]{1,0:T(8,128)(2,1)S(1)}, bf16[128,1024]{1,0:T(8,128)(2,1)S(1)}, u32[]{:S(2)}, u32[]{:S(2)}) collective-permute-start(bf16[128,1024]{1,0:T(8,128)(2,1)S(1)} %get-tuple-element.109), channel_id=1, source_target_pairs={{0,3},{1,0},{2,1},{3,2},{4,7},{5,4},{6,5},{7,6},{8,11},{9,8},{10,9... | collective-permute-start | bytes 786440 | tf_op jit(solution)/shard_map/ppermute | solution.py:356
  (103 other events, 912.5 us)
Sparse Core Ops, SparseCore 0:
  10.9 127.7 all-gather.1
where the time goes:
time: 438 us; the launch traced here: 430 us
  Pallas kernels  129 us (29%)
  waiting for transfers between devices  98.4 us (22%)
  starting transfers between devices  87.7 us (20%)
  other arithmetic  51.6 us (12%)
  local copies, waits for them, and re-layouts  32.4 us (7%)
  matrix products  15.3 us (3%)
  between operations  15.3 us (3%)
    ppermute x21, waiting for transfers between devices, shift(): lax.ppermute(block, 'head', [(j, (j + step) % n_head) for j in range(n_he...  48.5 us
    ppermute x21, starting transfers between devices, shift(): lax.ppermute(block, 'head', [(j, (j + step) % n_head) for j in range(n_he...  34.6 us
    ppermute x46, starting transfers between devices, swap(): return lax.ppermute(block, 'dp', [(j, j ^ bit) for j in range(n_dp)])  33.7 us
    ppermute x46, waiting for transfers between devices, swap(): return lax.ppermute(block, 'dp', [(j, j ^ bit) for j in range(n_dp)])  29 us
    pallas_call x4, Pallas kernels, unit_grad(): pl.pallas_call(unit_grad_kernel, grid_spec=pltpu.PrefetchScalarGridSpec(n...  28 us
    pallas_call x2, Pallas kernels, to_features(): pl.pallas_call(kernel, grid=(n_head,), in_specs=[pl.BlockSpec((rows, unit...  20.4 us
    convert_element_type x6, other arithmetic, scatter(): away = sum((t[middle:].astype(f32) for t in terms)).astype(bf16)  19.8 us
    pallas_call x2, Pallas kernels, attention_grad(): pl.pallas_call(attention_grad_kernel, grid_spec=pltpu.PrefetchScalarGridS...  17.6 us
  transfers between devices with their start and end apart: 76, of which 29 were waited for; matrix products, arithmetic and copies ran while one was open for 20% of the time, Pallas kernels for 20%

commit v1 on v0

--- a/solution.py
+++ b/solution.py
@@ -13,6 +13,7 @@
 LAT = 64
 PATCH = 256
 MAX_MEDIA = 5
+CHUNK = 64
 GROUP = 4
 
 epsilon = 1e-05
@@ -248,14 +249,24 @@
 
     @pl.when(pl.program_id(0) == pl.num_programs(0) - 1)
     def _():
-        d_feed = total[...]
-        scaled, inverse = norm_stats(hidden_ref[...])
-        gain_out[...] = jnp.sum(d_feed * scaled, axis=0, keepdims=True)
-        bias_out[...] = jnp.sum(d_feed, axis=0, keepdims=True)
-        d_hidden = grad_ref[...].astype(f32) + norm_back(d_feed, scaled, inverse, gain_ref[...])
-        d_hidden_ref[...] = d_hidden
-        d_attention_ref[...] = d_hidden.astype(bf16)
-        d_mixed_ref[...] = mm(d_hidden.astype(bf16), out_weight_ref[...]).astype(bf16)
+        gain_out[...] = jnp.zeros_like(gain_out)
+        bias_out[...] = jnp.zeros_like(bias_out)
+
+        def step(at, carry):
+            rows = pl.ds(pl.multiple_of(at * CHUNK, CHUNK), CHUNK)
+            d_feed = total[rows, :]
+            scaled, inverse = norm_stats(hidden_ref[rows, :])
+            gain_out[...] += jnp.sum(d_feed * scaled, axis=0, keepdims=True)
+            bias_out[...] += jnp.sum(d_feed, axis=0, keepdims=True)
+            d_hidden = grad_ref[rows, :].astype(f32) + norm_back(
+                d_feed, scaled, inverse, gain_ref[...]
+            )
+            d_hidden_ref[rows, :] = d_hidden
+            d_attention_ref[rows, :] = d_hidden.astype(bf16)
+            return carry
+
+        lax.fori_loop(0, total.shape[0] // CHUNK, step, 0)
+        d_mixed_ref[...] = mm(d_attention_ref[...], out_weight_ref[...]).astype(bf16)
 
 
 def to_features(kernel, units_in, main, extra, side, others, out_shapes):
@@ -276,8 +287,52 @@
     )(units_in, main, extra, *others)
 
 
+def media_norm_kernel(place_ref, tokens_ref, added_ref, gain_ref, bias_ref, out_ref):
+    def step(at, carry):
+        rows = pl.ds(pl.multiple_of(at * CHUNK, CHUNK), CHUNK)
+        scaled = norm_stats(tokens_ref[rows, :].astype(f32) + added_ref[0])[0]
+        out_ref[rows, :] = (scaled * gain_ref[...] + bias_ref[...]).astype(bf16)
+        return carry
+
+    lax.fori_loop(0, PATCH // CHUNK, step, 0)
+
+
+def media_norm_of(media_tokens, per_image, media_gain, media_bias, here):
+    images = per_image.shape[0]
+    row = pl.BlockSpec((1, D), lambda n, at: (0, 0))
+    return pl.pallas_call(
+        media_norm_kernel,
+        grid_spec=pltpu.PrefetchScalarGridSpec(
+            num_scalar_prefetch=1,
+            grid=(images,),
+            in_specs=[
+                pl.BlockSpec((PATCH, D), lambda n, at: (at[1] * images + n, 0)),
+                pl.BlockSpec((1, 1, D), lambda n, at: (n, 0, 0)),
+                row,
+                row,
+            ],
+            out_specs=pl.BlockSpec((PATCH, D), lambda n, at: (n, 0)),
+        ),
+        out_shape=jax.ShapeDtypeStruct((images * PATCH, D), bf16),
+        cost_estimate=pl.CostEstimate(
+            flops=20 * images * PATCH * D,
+            bytes_accessed=4 * images * PATCH * D,
+            transcendentals=0,
+        ),
+        name="media_norm",
+    )(here, media_tokens, per_image[:, None, :], media_gain[None, :], media_bias[None, :])
+
+
 def media_back_kernel(
-    place_ref, tokens_ref, added_ref, gain_ref, d_kv_ref, weight_ref, gain_out, bias_out, sum_out
+    place_ref,
+    tokens_ref,
+    added_ref,
+    gain_ref,
+    d_kv_ref,
+    weight_ref,
+    gain_out,
+    bias_out,
+    sum_out,
 ):
     @pl.when(pl.program_id(0) == 0)
     def _():
@@ -574,13 +629,15 @@
             total = total + shift(piece(s).astype(bf16), n_head - s).astype(f32)
         return total
 
-    def sum_everywhere(values_in):
+    def sum_everywhere(values_in, after):
         steps = [(swap, 1 << b) for b in range(n_dp.bit_length() - 1)]
         steps = steps + [(swap_head, 1 << b) for b in range(n_head.bit_length() - 1)]
-        for exchange, bit in steps[:-1]:
-            values_in = values_in + exchange(values_in, bit)
-        exchange, bit = steps[-1]
-        return (values_in, exchange(values_in, bit))
+        for k, (exchange, bit) in enumerate(steps):
+            came = exchange(values_in, bit)
+            if k >= len(steps) - len(after):
+                came, _ = lax.optimization_barrier((came, after[k - len(steps)]))
+            values_in = values_in + came
+        return values_in
 
     def place_rows(blocks, here):
         rows, cols = blocks[0].shape
@@ -604,44 +661,6 @@
             out_shape=jax.ShapeDtypeStruct((n_head * rows, cols), f32),
             name="place_rows",
         )(here, *blocks)
-
-    def share_rows(own, here):
-        rows = own.shape[0]
-        below, above = [own], [own]
-        for _ in range(1, n_head):
-            below.append(lax.ppermute(below[-1], "head", [(j, j + 1) for j in range(n_head - 1)]))
-            above.append(lax.ppermute(above[-1], "head", [(j, j - 1) for j in range(1, n_head)]))
-
-        def kernel(place_ref, own_ref, *refs):
-            lower, upper, out_ref = refs[: n_head - 1], refs[n_head - 1 : -1], refs[-1]
-            away = pl.program_id(0) - place_ref[1]
-
-            @pl.when(away == 0)
-            def _():
-                out_ref[...] = own_ref[...].astype(f32)
-
-            for s in range(1, n_head):
-
-                @pl.when(away == -s)
-                def _(s=s):
-                    out_ref[...] = lower[s - 1][...].astype(f32)
-
-                @pl.when(away == s)
-                def _(s=s):
-                    out_ref[...] = upper[s - 1][...].astype(f32)
-
-        one = pl.BlockSpec((rows, D), lambda n, at: (0, 0))
-        return pl.pallas_call(
-            kernel,
-            grid_spec=pltpu.PrefetchScalarGridSpec(
-                num_scalar_prefetch=1,
-                grid=(n_head,),
-                in_specs=[one] * (2 * n_head - 1),
-                out_specs=pl.BlockSpec((rows, D), lambda n, at: (n, 0)),
-            ),
-            out_shape=jax.ShapeDtypeStruct((n_head * rows, D), f32),
-            name="share_rows",
-        )(here, own, *below[1:], *above[1:])
 
     def per_device(
         latents,
@@ -668,7 +687,6 @@
         images_dp = latents.shape[0] // LAT
         images = images_dp // n_head
         lat_rows = images * LAT
-        media_rows = images * PATCH
 
         pieces = gather(
             jnp.concatenate([query_weight, key_weight, value_weight, out_weight.T], axis=1)
@@ -682,7 +700,8 @@
         )
         query_full, kv_full, out_full = assemble(pieces, here)
         extra = assemble_units(
-            gather(jnp.concatenate([up_weight[:, :EARLY], down_turned[:, :EARLY]], axis=1)), here
+            gather(jnp.concatenate([up_weight[:, :EARLY], down_turned[:, :EARLY]], axis=1)),
+            here,
         )
 
         cot_cols = cotangent.shape[1]
@@ -705,15 +724,10 @@
         media_slots = image_index - latest
         slot_match = media_slots[:, None] == jnp.arange(MAX_MEDIA, dtype=jnp.int32)[None, :]
         per_image = jnp.dot(slot_match.astype(bf16), time_table, preferred_element_type=f32)
-        media_own = lax.dynamic_slice_in_dim(media_tokens, my_head * media_rows, media_rows, 0)
         latents_own = lax.dynamic_slice_in_dim(latents, my_head * lat_rows, lat_rows, 0)
         latents_own = latents_own.astype(f32)
 
-        media_sum = (
-            media_own.reshape(images, PATCH, D).astype(f32) + per_image[:, None, :]
-        ).reshape(media_rows, D)
-        media_scaled, _ = norm_stats(media_sum)
-        media_norm = (media_scaled * media_gain + media_bias).astype(bf16)
+        media_norm = media_norm_of(media_tokens, per_image, media_gain, media_bias, here)
         latent_scaled, latent_inverse = norm_stats(latents_own)
         latent_norm = (latent_scaled * latent_gain + latent_bias).astype(bf16)
 
@@ -729,9 +743,6 @@
         down_keep = unit_grad(grad_out, activation, here, 0)
         down_grad = scatter(down_keep, down_send)
         like = jax.ShapeDtypeStruct
-        (result,) = to_features(
-            feed_out_kernel, activation, main, extra, 1, [hidden], [like((lat_rows, D), bf16)]
-        )
         inner = query_full.shape[1]
         d_hidden, d_attention, d_mixed, feed_gain_part, feed_bias_part = to_features(
             d_feed_kernel,
@@ -756,7 +767,16 @@
         latent_back = d_hidden + norm_back(
             d_latent_norm, latent_scaled, latent_inverse, latent_gain
         )
-        latents_grad = share_rows(latent_back.astype(bf16), here)
+        own_grad = latent_back.astype(bf16)
+        latents_grad = lax.all_gather(own_grad, "head", axis=0, tiled=True)
+        d_up, _ = lax.optimization_barrier((d_up, own_grad))
+        up_send = unit_grad(feed_norm, d_up, here, 1)
+        up_keep = unit_grad(feed_norm, d_up, here, 0)
+        up_grad = scatter(up_keep, up_send)
+        activation, _ = lax.optimization_barrier((activation, up_keep))
+        (result,) = to_features(
+            feed_out_kernel, activation, main, extra, 1, [hidden], [like((lat_rows, D), bf16)]
+        )
 
         media_gain_part, media_bias_part, image_sums = media_back(
             media_tokens, per_image, media_gain, d_media_kv, kv_full, here
@@ -778,18 +798,14 @@
             ],
             axis=0,
         )
-        small, last_small = sum_everywhere(small)
-
-        d_up, _ = lax.optimization_barrier((d_up, media_gain_part))
-        up_send = unit_grad(feed_norm, d_up, here, 1)
-        up_keep = unit_grad(feed_norm, d_up, here, 0)
-        up_grad = scatter(up_keep, up_send)
+
         sources = (latent_norm, media_norm, d_attention, d_query, d_media_kv, d_latent_kv, mixed)
         attention_send = attention_grad(*sources, here, 1)
         attention_keep = attention_grad(*sources, here, 0)
         attention_grads = scatter(attention_keep, attention_send)
-        last_small, attention_grads = lax.optimization_barrier((last_small, attention_grads))
-        small = small + last_small
+        small = sum_everywhere(small, (up_grad, attention_grads))
+        latents_grad, _ = lax.optimization_barrier((latents_grad, up_grad))
+        latents_grad = latents_grad.astype(f32)
         width = query_weight.shape[1]
         query_grad, key_grad, value_grad, out_grad = [
             attention_grads[:, at * width : (at + 1) * width] for at in range(4)

time: 438 us -> 448 us (1.023)
  the two profiles are of different devices: /device:TPU:8 before, /device:TPU:0 now
where the time goes in v1:
time: 448 us; the launch traced here: 446 us
  Pallas kernels  133 us (30%)
  waiting for transfers between devices  116 us (26%)
  starting transfers between devices  82.7 us (18%)
  other arithmetic  48.3 us (11%)
  local copies, waits for them, and re-layouts  31.5 us (7%)
  matrix products  20.2 us (5%)
  between operations  14.9 us (3%)
    ppermute x46, waiting for transfers between devices, swap(): return lax.ppermute(block, 'dp', [(j, j ^ bit) for j in range(n_dp)])  63.4 us
    ppermute x21, waiting for transfers between devices, shift(): lax.ppermute(block, 'head', [(j, (j + step) % n_head) for j in range(n_he...  52.2 us
    ppermute x21, starting transfers between devices, shift(): lax.ppermute(block, 'head', [(j, (j + step) % n_head) for j in range(n_he...  47.6 us
    ppermute x46, starting transfers between devices, swap(): return lax.ppermute(block, 'dp', [(j, j ^ bit) for j in range(n_dp)])  30.8 us
    pallas_call x4, Pallas kernels, unit_grad(): pl.pallas_call(unit_grad_kernel, grid_spec=pltpu.PrefetchScalarGridSpec(n...  28.2 us
    pallas_call x2, Pallas kernels, to_features(): pl.pallas_call(kernel, grid=(n_head,), in_specs=[pl.BlockSpec((rows, unit...  21.4 us
    convert_element_type x6, other arithmetic, scatter(): away = sum((t[middle:].astype(f32) for t in terms)).astype(bf16)  20.4 us
    pallas_call x2, Pallas kernels, attention_grad(): pl.pallas_call(attention_grad_kernel, grid_spec=pltpu.PrefetchScalarGridS...  17.5 us
  transfers between devices with their start and end apart: 71, of which 16 were waited for; matrix products, arithmetic and copies ran while one was open for 20% of the time, Pallas kernels for 20%

profile of v1, /device:TPU:0, one launch (start us, length us, event | category | flops | bytes accessed | tf_op | source)
XLA Modules:
  0.0 446.2 jit_solution(6132881032154957766)
XLA Ops:
  13.6 5.1 %collective-permute-start.2 = (bf16[128,512]{1,0:T(8,128)(2,1)}, bf16[128,512]{1,0:T(8,128)(2,1)}, u32[]{:S(2)}, u32[]{:S(2)}) collective-permute-start(bf16[128,512]{1,0:T(8,128)(2,1)} %pad_maximum_fusion.3), channel_id=1, source_target_pairs={{0,3},{1,0},{2,1},{3,2},{4,7},{5,4},{6,5},{7,6},{8,11},{9,8},{10,9... | collective-permute-start | bytes 393224 | tf_op jit(solution)/shard_map/ppermute | solution.py:411
  21.2 2.8 collective-permute-start.22
  35.0 2.7 collective-permute-done.1
  39.2 3.8 collective-permute-start.19
  48.9 6.4 %collective-permute-done.21 = bf16[128,512]{1,0:T(8,128)(2,1)} collective-permute-done((bf16[128,512]{1,0:T(8,128)(2,1)}, bf16[128,512]{1,0:T(8,128)(2,1)}, u32[]{:S(2)}, u32[]{:S(2)}) %collective-permute-start.21) | collective-permute-done | bytes 131104 | tf_op jit(solution)/shard_map/ppermute | solution.py:411
  61.5 8.9 %media_norm.1.refs_4_.refs_5_.refs_6_.refs_7_ = bf16[1536,1024]{1,0:T(8,128)(2,1)} custom-call(s32[2]{0:T(128)} %pad_add_fusion.place_ref, bf16[6144,1024]{1,0:T(8,128)(2,1)} %tokens_ref.3, f32[6,1,1024]{2,1,0:T(1,128)} %broadcast_in_dim.21.added_ref, f32[1,1024]{1,0:T(1,128)} %bitcast.41, f32[1,1024]{1,0:T(1,128)} %bitcast.43), custom_call_target="tpu_custom_call" | custom-call | flops 31457280 | bytes 6291456 | tf_op jit(solution)/shard_map/media_norm/pallas_call | solution.py:303
  70.5 8.7 %collective-permute-start.18 = (bf16[384,256]{1,0:T(8,128)(2,1)}, bf16[384,256]{1,0:T(8,128)(2,1)S(1)}, u32[]{:S(2)}, u32[]{:S(2)}) collective-permute-start(bf16[384,256]{1,0:T(8,128)(2,1)} %get-tuple-element.134), channel_id=1, source_target_pairs={{0,2},{1,3},{2,0},{3,1},{4,6},{5,7},{6,4},{7,5},{8,10},{9,11},{10,... | collective-permute-start | bytes 589832 | tf_op jit(solution)/shard_map/ppermute | solution.py:411
  80.5 11.9 %collective-permute-done.18 = bf16[384,256]{1,0:T(8,128)(2,1)S(1)} collective-permute-done((bf16[384,256]{1,0:T(8,128)(2,1)}, bf16[384,256]{1,0:T(8,128)(2,1)S(1)}, u32[]{:S(2)}, u32[]{:S(2)}) %collective-permute-start.18) | collective-permute-done | bytes 196640 | tf_op jit(solution)/shard_map/ppermute | solution.py:411
  92.9 2.1 collective-permute-start.14
  98.2 9.3 %collective-permute-done.6.refs_5_ = bf16[128,1024]{1,0:T(8,128)(2,1)S(1)} collective-permute-done((bf16[128,1024]{1,0:T(8,128)(2,1)}, bf16[128,1024]{1,0:T(8,128)(2,1)S(1)}, u32[]{:S(2)}, u32[]{:S(2)}) %collective-permute-start.6) | collective-permute-done | bytes 262176 | tf_op jit(solution)/shard_map/ppermute | solution.py:408
  108.5 7.4 %collective-permute-done.14.refs_13_ = bf16[128,1024]{1,0:T(8,128)(2,1)S(1)} collective-permute-done((bf16[128,1024]{1,0:T(8,128)(2,1)}, bf16[128,1024]{1,0:T(8,128)(2,1)S(1)}, u32[]{:S(2)}, u32[]{:S(2)}) %collective-permute-start.14) | collective-permute-done | bytes 262176 | tf_op jit(solution)/shard_map/ppermute | solution.py:408
  125.1 5.6 %assemble.1 = (bf16[1024,512]{1,0:T(8,128)(2,1)}, bf16[1024,1024]{1,0:T(8,128)(2,1)}, bf16[1024,512]{1,0:T(8,128)(2,1)}) custom-call(s32[2]{0:T(128)} %pad_add_fusion.place_ref, bf16[128,1024]{1,0:T(8,128)(2,1)} %copy-done.20, bf16[128,1024]{1,0:T(8,128)(2,1)} %constant_dynamic-update-slice_fusion.5.refs_1_, ...), custom_call_target="tpu_custom_call" | custom-call | tf_op jit(solution)/shard_map/assemble/pallas_call | solution.py:559
  130.7 6.7 %convolution_convert_fusion.km_ref.vm_ref = bf16[1536,1024]{1,0:T(8,128)(2,1)} fusion(bf16[1536,1024]{1,0:T(8,128)(2,1)S(1)} %copy-done.2, bf16[1024,1024]{1,0:T(8,128)(2,1)} %get-tuple-element.37.weight_ref), kind=kOutput, calls=%fused_computation | convolution fusion | flops 3222798336 | bytes 8388608 | tf_op jit(solution)/shard_map/dot_general | solution.py:26
  141.2 5.2 %collective-permute-done.33.refs_12_ = bf16[128,1024]{1,0:T(8,128)(2,1)S(1)} collective-permute-done((bf16[128,1024]{1,0:T(8,128)(2,1)}, bf16[128,1024]{1,0:T(8,128)(2,1)S(1)}, u32[]{:S(2)}, u32[]{:S(2)}) %collective-permute-start.33) | collective-permute-done | bytes 262176 | tf_op jit(solution)/shard_map/ppermute | solution.py:408
  148.4 7.3 %attend.1.refs_17_ = bf16[384,512]{1,0:T(8,128)(2,1)} custom-call(bf16[384,512]{1,0:T(8,128)(2,1)} %convolution_convert_fusion.2.q_ref, bf16[1536,1024]{1,0:T(8,128)(2,1)} %convolution_convert_fusion.km_ref.vm_ref, bf16[384,1024]{1,0:T(8,128)(2,1)} %convolution_convert_fusion.1.kl_ref.vl_ref, bf16[1536,1024]{1,0:T(8,128)(2,1)} %convolution_convert_fusion.km_ref.vm_ref, ...), custom_call_target="tpu_custom_call" | custom-call | tf_op jit(solution)/shard_map/attend/pallas_call | solution.py:131
  156.8 5.1 %assemble_units.1.up_more.down_more.more_ref = bf16[4096,512]{1,0:T(8,128)(2,1)} custom-call(s32[2]{0:T(128)} %pad_add_fusion.place_ref, bf16[128,1024]{1,0:T(8,128)(2,1)} %copy-done.17, bf16[128,1024]{1,0:T(8,128)(2,1)} %constant_dynamic-update-slice_fusion.7.refs_1_, bf16[128,1024]{1,0:T(8,128)(2,1)} %collective-permute-done.23.refs_2_, ...), custom_call_target="tpu_custom_call" | custom-call | tf_op jit(solution)/shard_map/assemble_units/pallas_call | solution.py:591
  165.3 12.6 %hidden_units.1 = (bf16[384,4096]{1,0:T(8,128)(2,1)}, bf16[384,4096]{1,0:T(8,128)(2,1)}) custom-call(bf16[384,1024]{1,0:T(8,128)(2,1)} %add_convert_fusion.4.norm_ref.refs_0_.refs_1_.refs_2_.refs_3_, bf16[384,1024]{1,0:T(8,128)(2,1)} %constant_dynamic-update-slice_fusion.9.grad_ref.refs_0_.refs_1_.refs_2_.refs_3_, ...), custom_call_target="tpu_custom_call" | custom-call | flops 6442450944 | bytes 16777216 | tf_op jit(solution)/shard_map/hidden_units/pallas_call | solution.py:202
  178.0 12.5 %shard_map.280 = (f32[384,1024]{1,0:T(8,128)}, bf16[384,1024]{1,0:T(8,128)(2,1)}, bf16[384,512]{1,0:T(8,128)(2,1)}, f32[1,1024]{1,0:T(1,128)}, f32[1,1024]{1,0:T(1,128)}) custom-call(bf16[384,4096]{1,0:T(8,128)(2,1)} %get-tuple-element.45.units_ref.refs_4_, bf16[4096,1536]{1,0:T(8,128)(2,1)} %all-gather.3.cloned.1.call-done.up_ref.down_ref.weight_ref, ...), custom_call_target="tpu_custom_call" | custom-call | flops 3221225472 | bytes 8388608 | tf_op jit(solution)/shard_map/pallas_call | solution.py:275
  190.4 11.8 %attend_back.1 = (bf16[384,512]{1,0:T(8,128)(2,1)}, bf16[1536,1024]{1,0:T(8,128)(2,1)}, bf16[384,1024]{1,0:T(8,128)(2,1)}) custom-call(bf16[384,512]{1,0:T(8,128)(2,1)} %convolution_convert_fusion.2.q_ref, bf16[1536,1024]{1,0:T(8,128)(2,1)} %convolution_convert_fusion.km_ref.vm_ref, bf16[384,1024]{1,0:T(8,128)(2,1)} %convolution_convert_fusion.1.kl_ref.vl_ref, ...), custom_call_target="tpu_custom_call" | custom-call | tf_op jit(solution)/shard_map/attend_back/pallas_call | solution.py:150
  202.2 3.3 fusion.24
  205.5 7.3 %unit_grad.7 = bf16[512,4096]{1,0:T(8,128)(2,1)} custom-call(s32[2]{0:T(128)} %pad_add_fusion.place_ref, bf16[384,1024]{1,0:T(8,128)(2,1)} %constant_dynamic-update-slice_fusion.9.grad_ref.refs_0_.refs_1_.refs_2_.refs_3_, bf16[384,1024]{1,0:T(8,128)(2,1)} %constant_dynamic-update-slice_fusion.9.grad_ref.refs_0_.refs_1_.refs_2_.refs_3_, ...), custom_call_target="tpu_custom_call" | custom-call | flops 1610612736 | bytes 4194304 | tf_op jit(solution)/shard_map/unit_grad/pallas_call | solution.py:462
  213.3 3.4 fusion.13
  218.2 6.9 %unit_grad.5 = bf16[512,4096]{1,0:T(8,128)(2,1)} custom-call(s32[2]{0:T(128)} %pad_add_fusion.place_ref, bf16[384,1024]{1,0:T(8,128)(2,1)} %add_convert_fusion.4.norm_ref.refs_0_.refs_1_.refs_2_.refs_3_, bf16[384,1024]{1,0:T(8,128)(2,1)} %add_convert_fusion.4.norm_ref.refs_0_.refs_1_.refs_2_.refs_3_, ...), custom_call_target="tpu_custom_call" | custom-call | flops 1610612736 | bytes 4194304 | tf_op jit(solution)/shard_map/unit_grad/pallas_call | solution.py:462
  225.2 8.7 %attention_grad.3 = bf16[512,2048]{1,0:T(8,128)(2,1)} custom-call(s32[2]{0:T(128)} %pad_add_fusion.place_ref, bf16[384,1024]{1,0:T(8,128)(2,1)} %fusion.7.refs_0_.refs_1_.refs_2_.refs_3_, bf16[384,1024]{1,0:T(8,128)(2,1)} %fusion.7.refs_0_.refs_1_.refs_2_.refs_3_, bf16[384,1024]{1,0:T(8,128)(2,1)} %fusion.7.refs_0_.refs_1_.refs_2_.refs_3_, ...), custom_call_target="tpu_custom_call" | custom-call | flops 2415919104 | bytes 2097152 | tf_op jit(solution)/shard_map/attention_grad/pallas_call | solution.py:498
  234.5 11.0 %media_back.1 = (f32[1,1024]{1,0:T(1,128)}, f32[1,1024]{1,0:T(1,128)}, f32[6,1,1024]{2,1,0:T(1,128)}) custom-call(s32[2]{0:T(128)} %pad_add_fusion.place_ref, bf16[6144,1024]{1,0:T(8,128)(2,1)} %tokens_ref.3, f32[6,1,1024]{2,1,0:T(1,128)} %broadcast_in_dim.21.added_ref, f32[1,1024]{1,0:T(1,128)} %bitcast.42, ...), custom_call_target="tpu_custom_call" | custom-call | flops 3221225472 | bytes 6291456 | tf_op jit(solution)/shard_map/media_back/pallas_call | solution.py:355
  247.4 6.9 %unit_grad.4 = bf16[512,4096]{1,0:T(8,128)(2,1)} custom-call(s32[2]{0:T(128)} %pad_add_fusion.place_ref, bf16[384,1024]{1,0:T(8,128)(2,1)} %add_convert_fusion.4.norm_ref.refs_0_.refs_1_.refs_2_.refs_3_, bf16[384,1024]{1,0:T(8,128)(2,1)} %add_convert_fusion.4.norm_ref.refs_0_.refs_1_.refs_2_.refs_3_, ...), custom_call_target="tpu_custom_call" | custom-call | flops 1610612736 | bytes 4194304 | tf_op jit(solution)/shard_map/unit_grad/pallas_call | solution.py:462
  254.3 8.7 %attention_grad.2 = bf16[512,2048]{1,0:T(8,128)(2,1)} custom-call(s32[2]{0:T(128)} %pad_add_fusion.place_ref, bf16[384,1024]{1,0:T(8,128)(2,1)} %fusion.7.refs_0_.refs_1_.refs_2_.refs_3_, bf16[384,1024]{1,0:T(8,128)(2,1)} %fusion.7.refs_0_.refs_1_.refs_2_.refs_3_, bf16[384,1024]{1,0:T(8,128)(2,1)} %fusion.7.refs_0_.refs_1_.refs_2_.refs_3_, ...), custom_call_target="tpu_custom_call" | custom-call | flops 2415919104 | bytes 2097152 | tf_op jit(solution)/shard_map/attention_grad/pallas_call | solution.py:498
  263.1 3.3 add_convert_fusion.8
  267.9 9.0 %shard_map.281 = bf16[384,1024]{1,0:T(8,128)(2,1)} custom-call(bf16[384,4096]{1,0:T(8,128)(2,1)} %get-tuple-element.46.units_ref.refs_4_, bf16[4096,1536]{1,0:T(8,128)(2,1)} %all-gather.3.cloned.1.call-done.up_ref.down_ref.weight_ref, bf16[4096,512]{1,0:T(8,128)(2,1)} %assemble_units.1.up_more.down_more.more_ref, f32[384,1024]{1,0:T(8,128)} %copy-done.4), custom_call_target="tpu_custom_call" | custom-call | flops 3221225472 | bytes 8388608 | tf_op jit(solution)/shard_map/pallas_call | solution.py:275
  276.9 7.1 %unit_grad.6 = bf16[512,4096]{1,0:T(8,128)(2,1)} custom-call(s32[2]{0:T(128)} %pad_add_fusion.place_ref, bf16[384,1024]{1,0:T(8,128)(2,1)} %constant_dynamic-update-slice_fusion.9.grad_ref.refs_0_.refs_1_.refs_2_.refs_3_, bf16[384,1024]{1,0:T(8,128)(2,1)} %constant_dynamic-update-slice_fusion.9.grad_ref.refs_0_.refs_1_.refs_2_.refs_3_, ...), custom_call_target="tpu_custom_call" | custom-call | flops 1610612736 | bytes 4194304 | tf_op jit(solution)/shard_map/unit_grad/pallas_call | solution.py:462
  288.3 6.6 %collective-permute-start.39 = (bf16[384,256]{1,0:T(8,128)(2,1)S(1)}, bf16[384,256]{1,0:T(8,128)(2,1)S(1)}, u32[]{:S(2)}, u32[]{:S(2)}) collective-permute-start(bf16[384,256]{1,0:T(8,128)(2,1)S(1)} %get-tuple-element.127), channel_id=1, source_target_pairs={{0,3},{1,0},{2,1},{3,2},{4,7},{5,4},{6,5},{7,6},{8,11},{9,8},{10,9... | collective-permute-start | bytes 589832 | tf_op jit(solution)/shard_map/ppermute | solution.py:411
  298.3 4.8 %add_convert_fusion.1 = (bf16[256,2048]{1,0:T(8,128)(2,1)}, bf16[256,2048]{1,0:T(8,128)(2,1)}) fusion(bf16[512,4096]{1,0:T(8,128)(2,1)} %collective-permute-done.61, bf16[512,4096]{1,0:T(8,128)(2,1)} %unit_grad.6), kind=kLoop, calls=%fused_computation.5 | loop fusion | flops 4194304 | bytes 6291456 | tf_op jit(solution)/shard_map/convert_element_type | solution.py:615
  306.1 3.6 add_convert_fusion.3
  309.8 7.5 %collective-permute-done.38.refs_2_ = bf16[384,256]{1,0:T(8,128)(2,1)S(1)} collective-permute-done((bf16[384,256]{1,0:T(8,128)(2,1)S(1)}, bf16[384,256]{1,0:T(8,128)(2,1)S(1)}, u32[]{:S(2)}, u32[]{:S(2)}) %collective-permute-start.38) | collective-permute-done | bytes 196640 | tf_op jit(solution)/shard_map/ppermute | solution.py:411
  321.6 3.6 place_rows.1
  325.2 30.7 %collective-permute-done.58 = bf16[128,1024]{1,0:T(8,128)(2,1)S(1)} collective-permute-done((bf16[128,1024]{1,0:T(8,128)(2,1)}, bf16[128,1024]{1,0:T(8,128)(2,1)S(1)}, u32[]{:S(2)}, u32[]{:S(2)}) %collective-permute-start.58) | collective-permute-done | bytes 262176 | tf_op jit(solution)/shard_map/ppermute | solution.py:408
  357.4 2.6 collective-permute-start.59
  361.3 2.5 collective-permute-start.56
  363.8 3.4 add_convert_fusion.6
  370.3 3.2 add_convert_fusion.10
  377.1 5.3 %collective-permute-done.63 = bf16[128,2048]{1,0:T(8,128)(2,1)} collective-permute-done((bf16[128,2048]{1,0:T(8,128)(2,1)}, bf16[128,2048]{1,0:T(8,128)(2,1)}, u32[]{:S(2)}, u32[]{:S(2)}) %collective-permute-start.63) | collective-permute-done | bytes 524320 | tf_op jit(solution)/shard_map/ppermute | solution.py:408
  383.6 2.4 add_convert_fusion.12
  392.1 2.3 add_convert_fusion.17
  394.7 14.9 %collective-permute-done.67 = bf16[128,1024]{1,0:T(8,128)(2,1)S(1)} collective-permute-done((bf16[128,1024]{1,0:T(8,128)(2,1)S(1)}, bf16[128,1024]{1,0:T(8,128)(2,1)S(1)}, u32[]{:S(2)}, u32[]{:S(2)}) %collective-permute-start.67) | collective-permute-done | bytes 262176 | tf_op jit(solution)/shard_map/ppermute | solution.py:411
  409.6 5.0 %collective-permute-start.43 = (bf16[128,1024]{1,0:T(8,128)(2,1)S(1)}, bf16[128,1024]{1,0:T(8,128)(2,1)S(1)}, u32[]{:S(2)}, u32[]{:S(2)}) collective-permute-start(bf16[128,1024]{1,0:T(8,128)(2,1)S(1)} %get-tuple-element.115), channel_id=1, source_target_pairs={{0,3},{1,0},{2,1},{3,2},{4,7},{5,4},{6,5},{7,6},{8,11},{9,8},{10,9... | collective-permute-start | bytes 786440 | tf_op jit(solution)/shard_map/ppermute | solution.py:411
  416.1 7.6 %collective-permute-done.46 = bf16[128,1024]{1,0:T(8,128)(2,1)S(1)} collective-permute-done((bf16[128,1024]{1,0:T(8,128)(2,1)S(1)}, bf16[128,1024]{1,0:T(8,128)(2,1)S(1)}, u32[]{:S(2)}, u32[]{:S(2)}) %collective-permute-start.46) | collective-permute-done | bytes 262176 | tf_op jit(solution)/shard_map/ppermute | solution.py:411
  426.6 4.3 collective-permute-start.52
  432.8 5.4 %convert_element_type.393 = f32[1536,1024]{1,0:T(8,128)} convert(bf16[1536,1024]{1,0:T(8,128)(2,1)} %all-gather.5.cloned.1.call-done) | non-fusion elementwise | flops 1572864 | bytes 9437184 | tf_op jit(solution)/shard_map/convert_element_type | solution.py:808
  (325 shorter events, 104.3 us)
Async XLA Ops:
  7.2 158.1 %all-gather.3.cloned.1.call-start = ((), (), s32[]{:S(2)}) async-start(), calls=%async_computation | async-start | bytes 12976128 | tf_op jit(solution)/shard_map/all_gather | solution.py:695
  11.9 420.8 %all-gather.5.cloned.1.call-start = ((), (), s32[]{:S(2)}) async-start(), calls=%async_computation.1 | async-start | bytes 3932160 | tf_op jit(solution)/shard_map/all_gather | solution.py:771
  13.6 25.7 %collective-permute-start.2 = (bf16[128,512]{1,0:T(8,128)(2,1)}, bf16[128,512]{1,0:T(8,128)(2,1)}, u32[]{:S(2)}, u32[]{:S(2)}) collective-permute-start(bf16[128,512]{1,0:T(8,128)(2,1)} %pad_maximum_fusion.3), channel_id=1, source_target_pairs={{0,3},{1,0},{2,1},{3,2},{4,7},{5,4},{6,5},{7,6},{8,11},{9,8},{10,9... | collective-permute-start | bytes 393224 | tf_op jit(solution)/shard_map/ppermute | solution.py:411
  18.6 19.0 %collective-permute-start.1 = (bf16[128,512]{1,0:T(8,128)(2,1)}, bf16[128,512]{1,0:T(8,128)(2,1)}, u32[]{:S(2)}, u32[]{:S(2)}) collective-permute-start(bf16[128,512]{1,0:T(8,128)(2,1)} %pad_maximum_fusion.3), channel_id=1, source_target_pairs={{0,2},{1,3},{2,0},{3,1},{4,6},{5,7},{6,4},{7,5},{8,10},{9,11},{10,... | collective-permute-start | bytes 393224 | tf_op jit(solution)/shard_map/ppermute | solution.py:411
  18.6 26.0 %collective-permute-start = (bf16[128,512]{1,0:T(8,128)(2,1)}, bf16[128,512]{1,0:T(8,128)(2,1)}, u32[]{:S(2)}, u32[]{:S(2)}) collective-permute-start(bf16[128,512]{1,0:T(8,128)(2,1)} %pad_maximum_fusion.3), channel_id=1, source_target_pairs={{0,1},{1,2},{2,3},{3,0},{4,5},{5,6},{6,7},{7,4},{8,9},{9,10},{10,1... | collective-permute-start | bytes 393224 | tf_op jit(solution)/shard_map/ppermute | solution.py:411
  21.2 26.1 %collective-permute-start.22 = (bf16[128,512]{1,0:T(8,128)(2,1)}, bf16[128,512]{1,0:T(8,128)(2,1)}, u32[]{:S(2)}, u32[]{:S(2)}) collective-permute-start(bf16[128,512]{1,0:T(8,128)(2,1)} %pad_maximum_fusion.4), channel_id=1, source_target_pairs={{0,3},{1,0},{2,1},{3,2},{4,7},{5,4},{6,5},{7,6},{8,11},{9,8},{10,9... | collective-permute-start | bytes 393224 | tf_op jit(solution)/shard_map/ppermute | solution.py:411
  24.0 31.3 %collective-permute-start.21 = (bf16[128,512]{1,0:T(8,128)(2,1)}, bf16[128,512]{1,0:T(8,128)(2,1)}, u32[]{:S(2)}, u32[]{:S(2)}) collective-permute-start(bf16[128,512]{1,0:T(8,128)(2,1)} %pad_maximum_fusion.4), channel_id=1, source_target_pairs={{0,2},{1,3},{2,0},{3,1},{4,6},{5,7},{6,4},{7,5},{8,10},{9,11},{10,... | collective-permute-start | bytes 393224 | tf_op jit(solution)/shard_map/ppermute | solution.py:411
  37.6 19.6 %collective-permute-start.20 = (bf16[128,512]{1,0:T(8,128)(2,1)}, bf16[128,512]{1,0:T(8,128)(2,1)S(1)}, u32[]{:S(2)}, u32[]{:S(2)}) collective-permute-start(bf16[128,512]{1,0:T(8,128)(2,1)} %pad_maximum_fusion.4), channel_id=1, source_target_pairs={{0,1},{1,2},{2,3},{3,0},{4,5},{5,6},{6,7},{7,4},{8,9},{9,10},{10,1... | collective-permute-start | bytes 393224 | tf_op jit(solution)/shard_map/ppermute | solution.py:411
  39.2 18.0 %collective-permute-start.19 = (bf16[384,256]{1,0:T(8,128)(2,1)S(1)}, bf16[384,256]{1,0:T(8,128)(2,1)}, u32[]{:S(2)}, u32[]{:S(2)}) collective-permute-start(bf16[384,256]{1,0:T(8,128)(2,1)S(1)} %get-tuple-element.131), channel_id=1, source_target_pairs={{0,3},{1,0},{2,1},{3,2},{4,7},{5,4},{6,5},{7,6},{8,11},{9,8},{10,9... | collective-permute-start | bytes 589832 | tf_op jit(solution)/shard_map/ppermute | solution.py:411
  44.6 25.9 %collective-permute-start.17 = (bf16[384,256]{1,0:T(8,128)(2,1)}, bf16[384,256]{1,0:T(8,128)(2,1)}, u32[]{:S(2)}, u32[]{:S(2)}) collective-permute-start(bf16[384,256]{1,0:T(8,128)(2,1)} %get-tuple-element.132), channel_id=1, source_target_pairs={{0,1},{1,2},{2,3},{3,0},{4,5},{5,6},{6,7},{7,4},{8,9},{9,10},{10,1... | collective-permute-start | bytes 589832 | tf_op jit(solution)/shard_map/ppermute | solution.py:411
  47.3 45.1 %collective-permute-start.9 = (bf16[128,1024]{1,0:T(8,128)(2,1)S(1)}, bf16[128,1024]{1,0:T(8,128)(2,1)}, u32[]{:S(2)}, u32[]{:S(2)}) collective-permute-start(bf16[128,1024]{1,0:T(8,128)(2,1)S(1)} %constant_dynamic-update-slice_fusion.refs_0_), channel_id=1, source_target_pairs={{0,16},{4,20},{8,24},{12,28},{16,0},{20,4},{24,8},{28,12},{1,17},{... | collective-permute-start | bytes 786440 | tf_op jit(solution)/shard_map/ppermute | solution.py:408
  55.3 37.1 %collective-permute-start.5 = (bf16[128,1024]{1,0:T(8,128)(2,1)S(1)}, bf16[128,1024]{1,0:T(8,128)(2,1)}, u32[]{:S(2)}, u32[]{:S(2)}) collective-permute-start(bf16[128,1024]{1,0:T(8,128)(2,1)S(1)} %constant_dynamic-update-slice_fusion.refs_0_), channel_id=1, source_target_pairs={{0,8},{4,12},{8,0},{12,4},{16,24},{20,28},{24,16},{28,20},{1,9},{5... | collective-permute-start | bytes 786440 | tf_op jit(solution)/shard_map/ppermute | solution.py:408
  57.2 35.7 %collective-permute-start.3 = (bf16[128,1024]{1,0:T(8,128)(2,1)S(1)}, bf16[128,1024]{1,0:T(8,128)(2,1)}, u32[]{:S(2)}, u32[]{:S(2)}) collective-permute-start(bf16[128,1024]{1,0:T(8,128)(2,1)S(1)} %constant_dynamic-update-slice_fusion.refs_0_), channel_id=1, source_target_pairs={{0,4},{4,0},{8,12},{12,8},{16,20},{20,16},{24,28},{28,24},{1,5},{5... | collective-permute-start | bytes 786440 | tf_op jit(solution)/shard_map/ppermute | solution.py:408
  57.9 35.0 %collective-permute-start.10 = (bf16[128,1024]{1,0:T(8,128)(2,1)}, bf16[128,1024]{1,0:T(8,128)(2,1)}, u32[]{:S(2)}, u32[]{:S(2)}) collective-permute-start(bf16[128,1024]{1,0:T(8,128)(2,1)} %constant_dynamic-update-slice_fusion.5.refs_1_), channel_id=1, source_target_pairs={{0,16},{4,20},{8,24},{12,28},{16,0},{20,4},{24,8},{28,12},{1,17},{... | collective-permute-start | bytes 786440 | tf_op jit(solution)/shard_map/ppermute | solution.py:408
  70.5 21.9 %collective-permute-start.18 = (bf16[384,256]{1,0:T(8,128)(2,1)}, bf16[384,256]{1,0:T(8,128)(2,1)S(1)}, u32[]{:S(2)}, u32[]{:S(2)}) collective-permute-start(bf16[384,256]{1,0:T(8,128)(2,1)} %get-tuple-element.134), channel_id=1, source_target_pairs={{0,2},{1,3},{2,0},{3,1},{4,6},{5,7},{6,4},{7,5},{8,10},{9,11},{10,... | collective-permute-start | bytes 589832 | tf_op jit(solution)/shard_map/ppermute | solution.py:411
  92.4 15.6 %collective-permute-start.11 = (bf16[128,1024]{1,0:T(8,128)(2,1)}, bf16[128,1024]{1,0:T(8,128)(2,1)S(1)}, u32[]{:S(2)}, u32[]{:S(2)}) collective-permute-start(bf16[128,1024]{1,0:T(8,128)(2,1)} %collective-permute-done.9.refs_8_), channel_id=1, source_target_pairs={{0,4},{4,0},{8,12},{12,8},{16,20},{20,16},{24,28},{28,24},{1,5},{5... | collective-permute-start | bytes 786440 | tf_op jit(solution)/shard_map/ppermute | solution.py:408
  92.9 15.2 %collective-permute-start.13 = (bf16[128,1024]{1,0:T(8,128)(2,1)}, bf16[128,1024]{1,0:T(8,128)(2,1)S(1)}, u32[]{:S(2)}, u32[]{:S(2)}) collective-permute-start(bf16[128,1024]{1,0:T(8,128)(2,1)} %collective-permute-done.5.refs_4_), channel_id=1, source_target_pairs={{0,16},{4,20},{8,24},{12,28},{16,0},{20,4},{24,8},{28,12},{1,17},{... | collective-permute-start | bytes 786440 | tf_op jit(solution)/shard_map/ppermute | solution.py:408
  92.9 23.0 %collective-permute-start.14 = (bf16[128,1024]{1,0:T(8,128)(2,1)}, bf16[128,1024]{1,0:T(8,128)(2,1)S(1)}, u32[]{:S(2)}, u32[]{:S(2)}) collective-permute-start(bf16[128,1024]{1,0:T(8,128)(2,1)} %collective-permute-done.10.refs_9_), channel_id=1, source_target_pairs={{0,8},{4,12},{8,0},{12,4},{16,24},{20,28},{24,16},{28,20},{1,9},{5... | collective-permute-start | bytes 786440 | tf_op jit(solution)/shard_map/ppermute | solution.py:408
  120.0 17.4 %collective-permute-start.29 = (bf16[128,1024]{1,0:T(8,128)(2,1)S(1)}, bf16[128,1024]{1,0:T(8,128)(2,1)}, u32[]{:S(2)}, u32[]{:S(2)}) collective-permute-start(bf16[128,1024]{1,0:T(8,128)(2,1)S(1)} %pad_maximum_fusion.2.refs_0_), channel_id=1, source_target_pairs={{0,16},{4,20},{8,24},{12,28},{16,0},{20,4},{24,8},{28,12},{1,17},{... | collective-permute-start | bytes 786440 | tf_op jit(solution)/shard_map/ppermute | solution.py:408
  120.1 17.3 %collective-permute-start.25 = (bf16[128,1024]{1,0:T(8,128)(2,1)S(1)}, bf16[128,1024]{1,0:T(8,128)(2,1)}, u32[]{:S(2)}, u32[]{:S(2)}) collective-permute-start(bf16[128,1024]{1,0:T(8,128)(2,1)S(1)} %pad_maximum_fusion.2.refs_0_), channel_id=1, source_target_pairs={{0,8},{4,12},{8,0},{12,4},{16,24},{20,28},{24,16},{28,20},{1,9},{5... | collective-permute-start | bytes 786440 | tf_op jit(solution)/shard_map/ppermute | solution.py:408
  120.2 17.7 %collective-permute-start.23 = (bf16[128,1024]{1,0:T(8,128)(2,1)S(1)}, bf16[128,1024]{1,0:T(8,128)(2,1)}, u32[]{:S(2)}, u32[]{:S(2)}) collective-permute-start(bf16[128,1024]{1,0:T(8,128)(2,1)S(1)} %pad_maximum_fusion.2.refs_0_), channel_id=1, source_target_pairs={{0,4},{4,0},{8,12},{12,8},{16,20},{20,16},{24,28},{28,24},{1,5},{5... | collective-permute-start | bytes 786440 | tf_op jit(solution)/shard_map/ppermute | solution.py:408
  120.7 17.8 %collective-permute-start.30 = (bf16[128,1024]{1,0:T(8,128)(2,1)}, bf16[128,1024]{1,0:T(8,128)(2,1)}, u32[]{:S(2)}, u32[]{:S(2)}) collective-permute-start(bf16[128,1024]{1,0:T(8,128)(2,1)} %constant_dynamic-update-slice_fusion.7.refs_1_), channel_id=1, source_target_pairs={{0,16},{4,20},{8,24},{12,28},{16,0},{20,4},{24,8},{28,12},{1,17},{... | collective-permute-start | bytes 786440 | tf_op jit(solution)/shard_map/ppermute | solution.py:408
  123.2 17.4 %collective-permute-start.26 = (bf16[128,1024]{1,0:T(8,128)(2,1)}, bf16[128,1024]{1,0:T(8,128)(2,1)}, u32[]{:S(2)}, u32[]{:S(2)}) collective-permute-start(bf16[128,1024]{1,0:T(8,128)(2,1)} %constant_dynamic-update-slice_fusion.7.refs_1_), channel_id=1, source_target_pairs={{0,8},{4,12},{8,0},{12,4},{16,24},{20,28},{24,16},{28,20},{1,9},{5... | collective-permute-start | bytes 786440 | tf_op jit(solution)/shard_map/ppermute | solution.py:408
  140.6 15.1 %collective-permute-start.27 = (bf16[128,1024]{1,0:T(8,128)(2,1)}, bf16[128,1024]{1,0:T(8,128)(2,1)S(1)}, u32[]{:S(2)}, u32[]{:S(2)}) collective-permute-start(bf16[128,1024]{1,0:T(8,128)(2,1)} %collective-permute-done.25.refs_4_), channel_id=1, source_target_pairs={{0,4},{4,0},{8,12},{12,8},{16,20},{20,16},{24,28},{28,24},{1,5},{5... | collective-permute-start | bytes 786440 | tf_op jit(solution)/shard_map/ppermute | solution.py:408
  212.7 84.8 %collective-permute-start.61 = (bf16[512,4096]{1,0:T(8,128)(2,1)}, bf16[512,4096]{1,0:T(8,128)(2,1)}, u32[]{:S(2)}, u32[]{:S(2)}) collective-permute-start(bf16[512,4096]{1,0:T(8,128)(2,1)} %unit_grad.7), channel_id=1, source_target_pairs={{0,4},{4,0},{8,12},{12,8},{16,20},{20,16},{24,28},{28,24},{1,5},{5... | collective-permute-start | bytes 12582920 | tf_op jit(solution)/shard_map/ppermute | solution.py:408
  225.1 80.4 %collective-permute-start.40 = (bf16[512,4096]{1,0:T(8,128)(2,1)}, bf16[512,4096]{1,0:T(8,128)(2,1)}, u32[]{:S(2)}, u32[]{:S(2)}) collective-permute-start(bf16[512,4096]{1,0:T(8,128)(2,1)} %unit_grad.5), channel_id=1, source_target_pairs={{0,4},{4,0},{8,12},{12,8},{16,20},{20,16},{24,28},{28,24},{1,5},{5... | collective-permute-start | bytes 12582920 | tf_op jit(solution)/shard_map/ppermute | solution.py:408
  233.9 29.2 %collective-permute-start.53 = (bf16[512,2048]{1,0:T(8,128)(2,1)}, bf16[512,2048]{1,0:T(8,128)(2,1)S(1)}, u32[]{:S(2)}, u32[]{:S(2)}) collective-permute-start(bf16[512,2048]{1,0:T(8,128)(2,1)} %attention_grad.3), channel_id=1, source_target_pairs={{0,4},{4,0},{8,12},{12,8},{16,20},{20,16},{24,28},{28,24},{1,5},{5... | collective-permute-start | bytes 6291464 | tf_op jit(solution)/shard_map/ppermute | solution.py:408
  247.3 36.6 %collective-permute-start.48 = (f32[11,1024]{1,0:T(8,128)S(1)}, f32[11,1024]{1,0:T(8,128)S(1)}, u32[]{:S(2)}, u32[]{:S(2)}) collective-permute-start(f32[11,1024]{1,0:T(8,128)S(1)} %concatenate.40), channel_id=1, source_target_pairs={{0,4},{4,0},{8,12},{12,8},{16,20},{20,16},{24,28},{28,24},{1,5},{5... | collective-permute-start | bytes 135176 | tf_op jit(solution)/shard_map/ppermute | solution.py:408
  266.4 28.4 %collective-permute-start.54 = (bf16[256,1024]{1,0:T(8,128)(2,1)}, bf16[256,1024]{1,0:T(8,128)(2,1)}, u32[]{:S(2)}, u32[]{:S(2)}) collective-permute-start(bf16[256,1024]{1,0:T(8,128)(2,1)} %get-tuple-element.125), channel_id=1, source_target_pairs={{0,16},{4,20},{8,24},{12,28},{16,0},{20,4},{24,8},{28,12},{1,17},{... | collective-permute-start | bytes 1572872 | tf_op jit(solution)/shard_map/ppermute | solution.py:408
  267.5 27.4 %collective-permute-start.57 = (bf16[256,1024]{1,0:T(8,128)(2,1)}, bf16[256,1024]{1,0:T(8,128)(2,1)S(1)}, u32[]{:S(2)}, u32[]{:S(2)}) collective-permute-start(bf16[256,1024]{1,0:T(8,128)(2,1)} %get-tuple-element.126), channel_id=1, source_target_pairs={{0,8},{4,12},{8,0},{12,4},{16,24},{20,28},{24,16},{28,20},{1,9},{5... | collective-permute-start | bytes 1572872 | tf_op jit(solution)/shard_map/ppermute | solution.py:408
  288.3 16.3 %collective-permute-start.39 = (bf16[384,256]{1,0:T(8,128)(2,1)S(1)}, bf16[384,256]{1,0:T(8,128)(2,1)S(1)}, u32[]{:S(2)}, u32[]{:S(2)}) collective-permute-start(bf16[384,256]{1,0:T(8,128)(2,1)S(1)} %get-tuple-element.127), channel_id=1, source_target_pairs={{0,3},{1,0},{2,1},{3,2},{4,7},{5,4},{6,5},{7,6},{8,11},{9,8},{10,9... | collective-permute-start | bytes 589832 | tf_op jit(solution)/shard_map/ppermute | solution.py:411
  294.8 22.5 %collective-permute-start.38 = (bf16[384,256]{1,0:T(8,128)(2,1)S(1)}, bf16[384,256]{1,0:T(8,128)(2,1)S(1)}, u32[]{:S(2)}, u32[]{:S(2)}) collective-permute-start(bf16[384,256]{1,0:T(8,128)(2,1)S(1)} %get-tuple-element.128), channel_id=1, source_target_pairs={{0,2},{1,3},{2,0},{3,1},{4,6},{5,7},{6,4},{7,5},{8,10},{9,11},{10,... | collective-permute-start | bytes 589832 | tf_op jit(solution)/shard_map/ppermute | solution.py:411
  294.9 23.8 %collective-permute-start.37 = (bf16[384,256]{1,0:T(8,128)(2,1)S(1)}, bf16[384,256]{1,0:T(8,128)(2,1)S(1)}, u32[]{:S(2)}, u32[]{:S(2)}) collective-permute-start(bf16[384,256]{1,0:T(8,128)(2,1)S(1)} %get-tuple-element.129), channel_id=1, source_target_pairs={{0,1},{1,2},{2,3},{3,0},{4,5},{5,6},{6,7},{7,4},{8,9},{9,10},{10,1... | collective-permute-start | bytes 589832 | tf_op jit(solution)/shard_map/ppermute | solution.py:411
  303.2 17.8 %collective-permute-start.55 = (bf16[128,1024]{1,0:T(8,128)(2,1)S(1)}, bf16[128,1024]{1,0:T(8,128)(2,1)S(1)}, u32[]{:S(2)}, u32[]{:S(2)}) collective-permute-start(bf16[128,1024]{1,0:T(8,128)(2,1)S(1)} %get-tuple-element.123), channel_id=1, source_target_pairs={{0,8},{4,12},{8,0},{12,4},{16,24},{20,28},{24,16},{28,20},{1,9},{5... | collective-permute-start | bytes 786440 | tf_op jit(solution)/shard_map/ppermute | solution.py:408
  304.6 55.4 %collective-permute-start.62 = (bf16[256,2048]{1,0:T(8,128)(2,1)}, bf16[256,2048]{1,0:T(8,128)(2,1)}, u32[]{:S(2)}, u32[]{:S(2)}) collective-permute-start(bf16[256,2048]{1,0:T(8,128)(2,1)} %get-tuple-element.113), channel_id=1, source_target_pairs={{0,16},{4,20},{8,24},{12,28},{16,0},{20,4},{24,8},{28,12},{1,17},{... | collective-permute-start | bytes 3145736 | tf_op jit(solution)/shard_map/ppermute | solution.py:408
  305.6 55.8 %collective-permute-start.65 = (bf16[256,2048]{1,0:T(8,128)(2,1)}, bf16[256,2048]{1,0:T(8,128)(2,1)}, u32[]{:S(2)}, u32[]{:S(2)}) collective-permute-start(bf16[256,2048]{1,0:T(8,128)(2,1)} %get-tuple-element.114), channel_id=1, source_target_pairs={{0,8},{4,12},{8,0},{12,4},{16,24},{20,28},{24,16},{28,20},{1,9},{5... | collective-permute-start | bytes 3145736 | tf_op jit(solution)/shard_map/ppermute | solution.py:408
  317.3 49.9 %collective-permute-start.41 = (bf16[256,2048]{1,0:T(8,128)(2,1)}, bf16[256,2048]{1,0:T(8,128)(2,1)}, u32[]{:S(2)}, u32[]{:S(2)}) collective-permute-start(bf16[256,2048]{1,0:T(8,128)(2,1)} %get-tuple-element.118), channel_id=1, source_target_pairs={{0,16},{4,20},{8,24},{12,28},{16,0},{20,4},{24,8},{28,12},{1,17},{... | collective-permute-start | bytes 3145736 | tf_op jit(solution)/shard_map/ppermute | solution.py:408
  319.4 49.1 %collective-permute-start.44 = (bf16[256,2048]{1,0:T(8,128)(2,1)}, bf16[256,2048]{1,0:T(8,128)(2,1)S(1)}, u32[]{:S(2)}, u32[]{:S(2)}) collective-permute-start(bf16[256,2048]{1,0:T(8,128)(2,1)} %get-tuple-element.119), channel_id=1, source_target_pairs={{0,8},{4,12},{8,0},{12,4},{16,24},{20,28},{24,16},{28,20},{1,9},{5... | collective-permute-start | bytes 3145736 | tf_op jit(solution)/shard_map/ppermute | solution.py:408
  320.9 35.0 %collective-permute-start.58 = (bf16[128,1024]{1,0:T(8,128)(2,1)}, bf16[128,1024]{1,0:T(8,128)(2,1)S(1)}, u32[]{:S(2)}, u32[]{:S(2)}) collective-permute-start(bf16[128,1024]{1,0:T(8,128)(2,1)} %get-tuple-element.124), channel_id=1, source_target_pairs={{0,16},{4,20},{8,24},{12,28},{16,0},{20,4},{24,8},{28,12},{1,17},{... | collective-permute-start | bytes 786440 | tf_op jit(solution)/shard_map/ppermute | solution.py:408
  357.4 16.1 %collective-permute-start.59 = (bf16[128,512]{1,0:T(8,128)(2,1)S(1)}, bf16[128,512]{1,0:T(8,128)(2,1)S(1)}, u32[]{:S(2)}, u32[]{:S(2)}) collective-permute-start(bf16[128,512]{1,0:T(8,128)(2,1)S(1)} %get-tuple-element.120), channel_id=1, source_target_pairs={{0,2},{1,3},{2,0},{3,1},{4,6},{5,7},{6,4},{7,5},{8,10},{9,11},{10,... | collective-permute-start | bytes 393224 | tf_op jit(solution)/shard_map/ppermute | solution.py:411
  373.5 53.1 %collective-permute-start.51 = (f32[11,1024]{1,0:T(8,128)S(1)}, f32[11,1024]{1,0:T(8,128)S(1)}, u32[]{:S(2)}, u32[]{:S(2)}) collective-permute-start(f32[11,1024]{1,0:T(8,128)S(1)} %add.397), channel_id=1, source_target_pairs={{0,1},{1,0},{2,3},{3,2},{4,5},{5,4},{6,7},{7,6},{8,9},{9,8},{10,11... | collective-permute-start | bytes 135176 | tf_op jit(solution)/shard_map/ppermute | solution.py:414
  373.5 16.9 %collective-permute-start.42 = (bf16[128,2048]{1,0:T(8,128)(2,1)}, bf16[128,2048]{1,0:T(8,128)(2,1)}, u32[]{:S(2)}, u32[]{:S(2)}) collective-permute-start(bf16[128,2048]{1,0:T(8,128)(2,1)} %get-tuple-element.116), channel_id=1, source_target_pairs={{0,8},{4,12},{8,0},{12,4},{16,24},{20,28},{24,16},{28,20},{1,9},{5... | collective-permute-start | bytes 1572872 | tf_op jit(solution)/shard_map/ppermute | solution.py:408
  373.9 18.1 %collective-permute-start.45 = (bf16[128,2048]{1,0:T(8,128)(2,1)}, bf16[128,2048]{1,0:T(8,128)(2,1)}, u32[]{:S(2)}, u32[]{:S(2)}) collective-permute-start(bf16[128,2048]{1,0:T(8,128)(2,1)} %get-tuple-element.117), channel_id=1, source_target_pairs={{0,16},{4,20},{8,24},{12,28},{16,0},{20,4},{24,8},{28,12},{1,17},{... | collective-permute-start | bytes 1572872 | tf_op jit(solution)/shard_map/ppermute | solution.py:408
  386.1 23.5 %collective-permute-start.67 = (bf16[128,1024]{1,0:T(8,128)(2,1)S(1)}, bf16[128,1024]{1,0:T(8,128)(2,1)S(1)}, u32[]{:S(2)}, u32[]{:S(2)}) collective-permute-start(bf16[128,1024]{1,0:T(8,128)(2,1)S(1)} %get-tuple-element.106), channel_id=1, source_target_pairs={{0,2},{1,3},{2,0},{3,1},{4,6},{5,7},{6,4},{7,5},{8,10},{9,11},{10,... | collective-permute-start | bytes 786440 | tf_op jit(solution)/shard_map/ppermute | solution.py:411
  386.7 22.9 %collective-permute-start.68 = (bf16[128,1024]{1,0:T(8,128)(2,1)S(1)}, bf16[128,1024]{1,0:T(8,128)(2,1)S(1)}, u32[]{:S(2)}, u32[]{:S(2)}) collective-permute-start(bf16[128,1024]{1,0:T(8,128)(2,1)S(1)} %get-tuple-element.107), channel_id=1, source_target_pairs={{0,1},{1,2},{2,3},{3,0},{4,5},{5,6},{6,7},{7,4},{8,9},{9,10},{10,1... | collective-permute-start | bytes 786440 | tf_op jit(solution)/shard_map/ppermute | solution.py:411
  390.4 24.2 %collective-permute-start.64 = (bf16[128,1024]{1,0:T(8,128)(2,1)S(1)}, bf16[128,1024]{1,0:T(8,128)(2,1)S(1)}, u32[]{:S(2)}, u32[]{:S(2)}) collective-permute-start(bf16[128,1024]{1,0:T(8,128)(2,1)S(1)} %get-tuple-element.110), channel_id=1, source_target_pairs={{0,3},{1,0},{2,1},{3,2},{4,7},{5,4},{6,5},{7,6},{8,11},{9,8},{10,9... | collective-permute-start | bytes 786440 | tf_op jit(solution)/shard_map/ppermute | solution.py:411
  394.4 29.3 %collective-permute-start.46 = (bf16[128,1024]{1,0:T(8,128)(2,1)S(1)}, bf16[128,1024]{1,0:T(8,128)(2,1)S(1)}, u32[]{:S(2)}, u32[]{:S(2)}) collective-permute-start(bf16[128,1024]{1,0:T(8,128)(2,1)S(1)} %get-tuple-element.108), channel_id=1, source_target_pairs={{0,2},{1,3},{2,0},{3,1},{4,6},{5,7},{6,4},{7,5},{8,10},{9,11},{10,... | collective-permute-start | bytes 786440 | tf_op jit(solution)/shard_map/ppermute | solution.py:411
  409.6 15.4 %collective-permute-start.43 = (bf16[128,1024]{1,0:T(8,128)(2,1)S(1)}, bf16[128,1024]{1,0:T(8,128)(2,1)S(1)}, u32[]{:S(2)}, u32[]{:S(2)}) collective-permute-start(bf16[128,1024]{1,0:T(8,128)(2,1)S(1)} %get-tuple-element.115), channel_id=1, source_target_pairs={{0,3},{1,0},{2,1},{3,2},{4,7},{5,4},{6,5},{7,6},{8,11},{9,8},{10,9... | collective-permute-start | bytes 786440 | tf_op jit(solution)/shard_map/ppermute | solution.py:411
  (88 other events, 834.7 us)
Sparse Core Ops, SparseCore 0:
  12.0 122.1 all-gather.2
  234.6 69.9 all-gather.4

commit v2 on v1

--- a/solution.py
+++ b/solution.py
@@ -739,9 +739,6 @@
         feed_norm = (norm_stats(hidden)[0] * feed_gain + feed_bias).astype(bf16)
 
         activation, d_up = hidden_units(feed_norm, grad_out, main, extra)
-        down_send = unit_grad(grad_out, activation, here, 1)
-        down_keep = unit_grad(grad_out, activation, here, 0)
-        down_grad = scatter(down_keep, down_send)
         like = jax.ShapeDtypeStruct
         inner = query_full.shape[1]
         d_hidden, d_attention, d_mixed, feed_gain_part, feed_bias_part = to_features(
@@ -769,7 +766,10 @@
         )
         own_grad = latent_back.astype(bf16)
         latents_grad = lax.all_gather(own_grad, "head", axis=0, tiled=True)
-        d_up, _ = lax.optimization_barrier((d_up, own_grad))
+        activation, d_up, _ = lax.optimization_barrier((activation, d_up, own_grad))
+        down_send = unit_grad(grad_out, activation, here, 1)
+        down_keep = unit_grad(grad_out, activation, here, 0)
+        down_grad = scatter(down_keep, down_send)
         up_send = unit_grad(feed_norm, d_up, here, 1)
         up_keep = unit_grad(feed_norm, d_up, here, 0)
         up_grad = scatter(up_keep, up_send)
@@ -804,7 +804,7 @@
         attention_keep = attention_grad(*sources, here, 0)
         attention_grads = scatter(attention_keep, attention_send)
         small = sum_everywhere(small, (up_grad, attention_grads))
-        latents_grad, _ = lax.optimization_barrier((latents_grad, up_grad))
+        latents_grad, _ = lax.optimization_barrier((latents_grad, down_grad))
         latents_grad = latents_grad.astype(f32)
         width = query_weight.shape[1]
         query_grad, key_grad, value_grad, out_grad = [
@@ -819,6 +819,7 @@
             if s:
                 block = shift(block, s)
             blocks.append(block)
+        blocks, _ = lax.optimization_barrier((blocks, down_grad))
         latents_out = place_rows(blocks, here)
         return (
             latents_out,

time: 448 us -> 426 us (0.951)
  waiting for transfers between devices: 116 us -> 87 us
  starting transfers between devices: 82.7 us -> 92.5 us
    ppermute x46, waiting for transfers between devices: 63.4 us -> 40 us  [swap(): return lax.ppermute(block, 'dp', [(j, j ^ bit) for j in range(n_dp)])]
    ppermute x21, starting transfers between devices: 47.6 us -> 57.9 us  [shift(): lax.ppermute(block, 'head', [(j, (j + step) % n_head) for j in range(n_he...]
    ppermute x21, waiting for transfers between devices: 52.2 us -> 46.9 us  [shift(): lax.ppermute(block, 'head', [(j, (j + step) % n_head) for j in range(n_he...]
    unnamed x140 -> x142, local copies, waits for them, and re-layouts: 13.2 us -> 13.7 us
  transfers between devices with their start and end apart: 71 -> 71, of which waited for: 16 -> 13; matrix products, arithmetic and copies ran while one was open for 20% -> 19% of each run, Pallas kernels for 20% -> 21%
where the time goes in v2:
time: 426 us; the launch traced here: 424 us
  Pallas kernels  133 us (31%)
  starting transfers between devices  92.5 us (22%)
  waiting for transfers between devices  87 us (20%)
  other arithmetic  48.1 us (11%)
  local copies, waits for them, and re-layouts  32.7 us (8%)
  matrix products  16.2 us (4%)
  between operations  15 us (4%)
    ppermute x21, starting transfers between devices, shift(): lax.ppermute(block, 'head', [(j, (j + step) % n_head) for j in range(n_he...  57.9 us
    ppermute x21, waiting for transfers between devices, shift(): lax.ppermute(block, 'head', [(j, (j + step) % n_head) for j in range(n_he...  46.9 us
    ppermute x46, waiting for transfers between devices, swap(): return lax.ppermute(block, 'dp', [(j, j ^ bit) for j in range(n_dp)])  40 us
    ppermute x46, starting transfers between devices, swap(): return lax.ppermute(block, 'dp', [(j, j ^ bit) for j in range(n_dp)])  29.9 us
    pallas_call x4, Pallas kernels, unit_grad(): pl.pallas_call(unit_grad_kernel, grid_spec=pltpu.PrefetchScalarGridSpec(n...  27.7 us
    pallas_call x2, Pallas kernels, to_features(): pl.pallas_call(kernel, grid=(n_head,), in_specs=[pl.BlockSpec((rows, unit...  21.3 us
    convert_element_type x6, other arithmetic, scatter(): away = sum((t[middle:].astype(f32) for t in terms)).astype(bf16)  19.5 us
    pallas_call x2, Pallas kernels, attention_grad(): pl.pallas_call(attention_grad_kernel, grid_spec=pltpu.PrefetchScalarGridS...  17.4 us
  transfers between devices with their start and end apart: 71, of which 13 were waited for; matrix products, arithmetic and copies ran while one was open for 19% of the time, Pallas kernels for 21%

profile of v2, /device:TPU:0, one launch (start us, length us, event | category | flops | bytes accessed | tf_op | source)
XLA Modules:
  0.0 424.1 jit_solution(11016897910166968258)
XLA Ops:
  13.5 5.1 %collective-permute-start.2 = (bf16[128,512]{1,0:T(8,128)(2,1)}, bf16[128,512]{1,0:T(8,128)(2,1)}, u32[]{:S(2)}, u32[]{:S(2)}) collective-permute-start(bf16[128,512]{1,0:T(8,128)(2,1)} %pad_maximum_fusion.3), channel_id=1, source_target_pairs={{0,3},{1,0},{2,1},{3,2},{4,7},{5,4},{6,5},{7,6},{8,11},{9,8},{10,9... | collective-permute-start | bytes 393224 | tf_op jit(solution)/shard_map/ppermute | solution.py:411
  21.2 2.8 collective-permute-start.22
  35.0 2.6 collective-permute-done.1
  39.2 3.8 collective-permute-start.19
  48.9 6.4 %collective-permute-done.21 = bf16[128,512]{1,0:T(8,128)(2,1)} collective-permute-done((bf16[128,512]{1,0:T(8,128)(2,1)}, bf16[128,512]{1,0:T(8,128)(2,1)}, u32[]{:S(2)}, u32[]{:S(2)}) %collective-permute-start.21) | collective-permute-done | bytes 131104 | tf_op jit(solution)/shard_map/ppermute | solution.py:411
  61.5 9.0 %media_norm.1.refs_4_.refs_5_.refs_6_.refs_7_ = bf16[1536,1024]{1,0:T(8,128)(2,1)} custom-call(s32[2]{0:T(128)} %pad_add_fusion.place_ref, bf16[6144,1024]{1,0:T(8,128)(2,1)} %tokens_ref.3, f32[6,1,1024]{2,1,0:T(1,128)} %broadcast_in_dim.21.added_ref, f32[1,1024]{1,0:T(1,128)} %bitcast.41, f32[1,1024]{1,0:T(1,128)} %bitcast.43), custom_call_target="tpu_custom_call" | custom-call | flops 31457280 | bytes 6291456 | tf_op jit(solution)/shard_map/media_norm/pallas_call | solution.py:303
  70.5 8.7 %collective-permute-start.18 = (bf16[384,256]{1,0:T(8,128)(2,1)}, bf16[384,256]{1,0:T(8,128)(2,1)S(1)}, u32[]{:S(2)}, u32[]{:S(2)}) collective-permute-start(bf16[384,256]{1,0:T(8,128)(2,1)} %get-tuple-element.144), channel_id=1, source_target_pairs={{0,2},{1,3},{2,0},{3,1},{4,6},{5,7},{6,4},{7,5},{8,10},{9,11},{10,... | collective-permute-start | bytes 589832 | tf_op jit(solution)/shard_map/ppermute | solution.py:411
  80.5 11.9 %collective-permute-done.18 = bf16[384,256]{1,0:T(8,128)(2,1)S(1)} collective-permute-done((bf16[384,256]{1,0:T(8,128)(2,1)}, bf16[384,256]{1,0:T(8,128)(2,1)S(1)}, u32[]{:S(2)}, u32[]{:S(2)}) %collective-permute-start.18) | collective-permute-done | bytes 196640 | tf_op jit(solution)/shard_map/ppermute | solution.py:411
  98.2 9.3 %collective-permute-done.6.refs_5_ = bf16[128,1024]{1,0:T(8,128)(2,1)S(1)} collective-permute-done((bf16[128,1024]{1,0:T(8,128)(2,1)}, bf16[128,1024]{1,0:T(8,128)(2,1)S(1)}, u32[]{:S(2)}, u32[]{:S(2)}) %collective-permute-start.6) | collective-permute-done | bytes 262176 | tf_op jit(solution)/shard_map/ppermute | solution.py:408
  108.5 7.4 %collective-permute-done.14.refs_13_ = bf16[128,1024]{1,0:T(8,128)(2,1)S(1)} collective-permute-done((bf16[128,1024]{1,0:T(8,128)(2,1)}, bf16[128,1024]{1,0:T(8,128)(2,1)S(1)}, u32[]{:S(2)}, u32[]{:S(2)}) %collective-permute-start.14) | collective-permute-done | bytes 262176 | tf_op jit(solution)/shard_map/ppermute | solution.py:408
  125.1 5.6 %assemble.1 = (bf16[1024,512]{1,0:T(8,128)(2,1)}, bf16[1024,1024]{1,0:T(8,128)(2,1)}, bf16[1024,512]{1,0:T(8,128)(2,1)}) custom-call(s32[2]{0:T(128)} %pad_add_fusion.place_ref, bf16[128,1024]{1,0:T(8,128)(2,1)} %copy-done.18, bf16[128,1024]{1,0:T(8,128)(2,1)} %constant_dynamic-update-slice_fusion.5.refs_1_, ...), custom_call_target="tpu_custom_call" | custom-call | tf_op jit(solution)/shard_map/assemble/pallas_call | solution.py:559
  130.7 6.7 %convolution_convert_fusion.km_ref.vm_ref = bf16[1536,1024]{1,0:T(8,128)(2,1)} fusion(bf16[1536,1024]{1,0:T(8,128)(2,1)S(1)} %copy-done.2, bf16[1024,1024]{1,0:T(8,128)(2,1)} %get-tuple-element.42.weight_ref), kind=kOutput, calls=%fused_computation | convolution fusion | flops 3222798336 | bytes 8388608 | tf_op jit(solution)/shard_map/dot_general | solution.py:26
  141.1 5.4 %collective-permute-done.33.refs_12_ = bf16[128,1024]{1,0:T(8,128)(2,1)S(1)} collective-permute-done((bf16[128,1024]{1,0:T(8,128)(2,1)}, bf16[128,1024]{1,0:T(8,128)(2,1)S(1)}, u32[]{:S(2)}, u32[]{:S(2)}) %collective-permute-start.33) | collective-permute-done | bytes 262176 | tf_op jit(solution)/shard_map/ppermute | solution.py:408
  148.3 7.3 %attend.1.refs_17_ = bf16[384,512]{1,0:T(8,128)(2,1)} custom-call(bf16[384,512]{1,0:T(8,128)(2,1)} %convolution_convert_fusion.2.q_ref, bf16[1536,1024]{1,0:T(8,128)(2,1)} %convolution_convert_fusion.km_ref.vm_ref, bf16[384,1024]{1,0:T(8,128)(2,1)} %convolution_convert_fusion.1.kl_ref.vl_ref, bf16[1536,1024]{1,0:T(8,128)(2,1)} %convolution_convert_fusion.km_ref.vm_ref, ...), custom_call_target="tpu_custom_call" | custom-call | tf_op jit(solution)/shard_map/attend/pallas_call | solution.py:131
  156.7 5.1 %assemble_units.1.up_more.down_more.more_ref = bf16[4096,512]{1,0:T(8,128)(2,1)} custom-call(s32[2]{0:T(128)} %pad_add_fusion.place_ref, bf16[128,1024]{1,0:T(8,128)(2,1)} %copy-done.15, bf16[128,1024]{1,0:T(8,128)(2,1)} %constant_dynamic-update-slice_fusion.7.refs_1_, bf16[128,1024]{1,0:T(8,128)(2,1)} %collective-permute-done.23.refs_2_, ...), custom_call_target="tpu_custom_call" | custom-call | tf_op jit(solution)/shard_map/assemble_units/pallas_call | solution.py:591
  165.2 12.7 %hidden_units.1 = (bf16[384,4096]{1,0:T(8,128)(2,1)}, bf16[384,4096]{1,0:T(8,128)(2,1)}) custom-call(bf16[384,1024]{1,0:T(8,128)(2,1)} %add_convert_fusion.4.norm_ref.refs_0_.refs_1_.refs_2_.refs_3_, bf16[384,1024]{1,0:T(8,128)(2,1)} %constant_dynamic-update-slice_fusion.9.grad_ref.refs_0_.refs_1_.refs_2_.refs_3_, ...), custom_call_target="tpu_custom_call" | custom-call | flops 6442450944 | bytes 16777216 | tf_op jit(solution)/shard_map/hidden_units/pallas_call | solution.py:202
  177.9 12.5 %shard_map.280 = (f32[384,1024]{1,0:T(8,128)}, bf16[384,1024]{1,0:T(8,128)(2,1)}, bf16[384,512]{1,0:T(8,128)(2,1)}, f32[1,1024]{1,0:T(1,128)}, f32[1,1024]{1,0:T(1,128)}) custom-call(bf16[384,4096]{1,0:T(8,128)(2,1)} %get-tuple-element.51.units_ref.refs_4_, bf16[4096,1536]{1,0:T(8,128)(2,1)} %all-gather.3.cloned.1.call-done.up_ref.down_ref.weight_ref, ...), custom_call_target="tpu_custom_call" | custom-call | flops 3221225472 | bytes 8388608 | tf_op jit(solution)/shard_map/pallas_call | solution.py:275
  190.3 11.7 %attend_back.1 = (bf16[384,512]{1,0:T(8,128)(2,1)}, bf16[1536,1024]{1,0:T(8,128)(2,1)}, bf16[384,1024]{1,0:T(8,128)(2,1)}) custom-call(bf16[384,512]{1,0:T(8,128)(2,1)} %convolution_convert_fusion.2.q_ref, bf16[1536,1024]{1,0:T(8,128)(2,1)} %convolution_convert_fusion.km_ref.vm_ref, bf16[384,1024]{1,0:T(8,128)(2,1)} %convolution_convert_fusion.1.kl_ref.vl_ref, ...), custom_call_target="tpu_custom_call" | custom-call | tf_op jit(solution)/shard_map/attend_back/pallas_call | solution.py:150
  207.5 6.9 %unit_grad.6 = bf16[512,4096]{1,0:T(8,128)(2,1)} custom-call(s32[2]{0:T(128)} %pad_add_fusion.place_ref, bf16[384,1024]{1,0:T(8,128)(2,1)} %constant_dynamic-update-slice_fusion.9.grad_ref.refs_0_.refs_1_.refs_2_.refs_3_, bf16[384,1024]{1,0:T(8,128)(2,1)} %constant_dynamic-update-slice_fusion.9.grad_ref.refs_0_.refs_1_.refs_2_.refs_3_, ...), custom_call_target="tpu_custom_call" | custom-call | flops 1610612736 | bytes 4194304 | tf_op jit(solution)/shard_map/unit_grad/pallas_call | solution.py:462
  214.9 6.9 %unit_grad.7 = bf16[512,4096]{1,0:T(8,128)(2,1)} custom-call(s32[2]{0:T(128)} %pad_add_fusion.place_ref, bf16[384,1024]{1,0:T(8,128)(2,1)} %add_convert_fusion.4.norm_ref.refs_0_.refs_1_.refs_2_.refs_3_, bf16[384,1024]{1,0:T(8,128)(2,1)} %add_convert_fusion.4.norm_ref.refs_0_.refs_1_.refs_2_.refs_3_, ...), custom_call_target="tpu_custom_call" | custom-call | flops 1610612736 | bytes 4194304 | tf_op jit(solution)/shard_map/unit_grad/pallas_call | solution.py:462
  221.9 8.7 %attention_grad.3 = bf16[512,2048]{1,0:T(8,128)(2,1)} custom-call(s32[2]{0:T(128)} %pad_add_fusion.place_ref, bf16[384,1024]{1,0:T(8,128)(2,1)} %fusion.7.refs_0_.refs_1_.refs_2_.refs_3_, bf16[384,1024]{1,0:T(8,128)(2,1)} %fusion.7.refs_0_.refs_1_.refs_2_.refs_3_, bf16[384,1024]{1,0:T(8,128)(2,1)} %fusion.7.refs_0_.refs_1_.refs_2_.refs_3_, ...), custom_call_target="tpu_custom_call" | custom-call | flops 2415919104 | bytes 2097152 | tf_op jit(solution)/shard_map/attention_grad/pallas_call | solution.py:498
  231.2 8.7 %attention_grad.2 = bf16[512,2048]{1,0:T(8,128)(2,1)} custom-call(s32[2]{0:T(128)} %pad_add_fusion.place_ref, bf16[384,1024]{1,0:T(8,128)(2,1)} %fusion.7.refs_0_.refs_1_.refs_2_.refs_3_, bf16[384,1024]{1,0:T(8,128)(2,1)} %fusion.7.refs_0_.refs_1_.refs_2_.refs_3_, bf16[384,1024]{1,0:T(8,128)(2,1)} %fusion.7.refs_0_.refs_1_.refs_2_.refs_3_, ...), custom_call_target="tpu_custom_call" | custom-call | flops 2415919104 | bytes 2097152 | tf_op jit(solution)/shard_map/attention_grad/pallas_call | solution.py:498
  239.9 11.2 %media_back.1 = (f32[1,1024]{1,0:T(1,128)}, f32[1,1024]{1,0:T(1,128)}, f32[6,1,1024]{2,1,0:T(1,128)}) custom-call(s32[2]{0:T(128)} %pad_add_fusion.place_ref, bf16[6144,1024]{1,0:T(8,128)(2,1)} %tokens_ref.3, f32[6,1,1024]{2,1,0:T(1,128)} %broadcast_in_dim.21.added_ref, f32[1,1024]{1,0:T(1,128)} %bitcast.42, ...), custom_call_target="tpu_custom_call" | custom-call | flops 3221225472 | bytes 6291456 | tf_op jit(solution)/shard_map/media_back/pallas_call | solution.py:355
  251.2 2.4 add_convert_fusion.6
  255.4 6.9 %unit_grad.4 = bf16[512,4096]{1,0:T(8,128)(2,1)} custom-call(s32[2]{0:T(128)} %pad_add_fusion.place_ref, bf16[384,1024]{1,0:T(8,128)(2,1)} %add_convert_fusion.4.norm_ref.refs_0_.refs_1_.refs_2_.refs_3_, bf16[384,1024]{1,0:T(8,128)(2,1)} %add_convert_fusion.4.norm_ref.refs_0_.refs_1_.refs_2_.refs_3_, ...), custom_call_target="tpu_custom_call" | custom-call | flops 1610612736 | bytes 4194304 | tf_op jit(solution)/shard_map/unit_grad/pallas_call | solution.py:462
  264.3 6.9 %unit_grad.5 = bf16[512,4096]{1,0:T(8,128)(2,1)} custom-call(s32[2]{0:T(128)} %pad_add_fusion.place_ref, bf16[384,1024]{1,0:T(8,128)(2,1)} %constant_dynamic-update-slice_fusion.9.grad_ref.refs_0_.refs_1_.refs_2_.refs_3_, bf16[384,1024]{1,0:T(8,128)(2,1)} %constant_dynamic-update-slice_fusion.9.grad_ref.refs_0_.refs_1_.refs_2_.refs_3_, ...), custom_call_target="tpu_custom_call" | custom-call | flops 1610612736 | bytes 4194304 | tf_op jit(solution)/shard_map/unit_grad/pallas_call | solution.py:462
  275.8 4.5 %add_convert_fusion.3 = (bf16[256,2048]{1,0:T(8,128)(2,1)}, bf16[256,2048]{1,0:T(8,128)(2,1)}) fusion(bf16[512,4096]{1,0:T(8,128)(2,1)} %collective-permute-done.40, bf16[512,4096]{1,0:T(8,128)(2,1)} %unit_grad.5), kind=kLoop, calls=%fused_computation.7 | loop fusion | flops 4194304 | bytes 6291456 | tf_op jit(solution)/shard_map/convert_element_type | solution.py:615
  283.3 3.7 add_convert_fusion.1
  288.8 8.9 %shard_map.281 = bf16[384,1024]{1,0:T(8,128)(2,1)} custom-call(bf16[384,4096]{1,0:T(8,128)(2,1)} %get-tuple-element.52.units_ref.refs_4_, bf16[4096,1536]{1,0:T(8,128)(2,1)} %all-gather.3.cloned.1.call-done.up_ref.down_ref.weight_ref, bf16[4096,512]{1,0:T(8,128)(2,1)} %assemble_units.1.up_more.down_more.more_ref, f32[384,1024]{1,0:T(8,128)} %copy-done.4), custom_call_target="tpu_custom_call" | custom-call | flops 3221225472 | bytes 8388608 | tf_op jit(solution)/shard_map/pallas_call | solution.py:275
  302.2 4.4 %collective-permute-done.41 = bf16[256,2048]{1,0:T(8,128)(2,1)} collective-permute-done((bf16[256,2048]{1,0:T(8,128)(2,1)}, bf16[256,2048]{1,0:T(8,128)(2,1)}, u32[]{:S(2)}, u32[]{:S(2)}) %collective-permute-start.41) | collective-permute-done | bytes 1048608 | tf_op jit(solution)/shard_map/ppermute | solution.py:408
  306.6 5.0 %collective-permute-start.68 = (bf16[128,512]{1,0:T(8,128)(2,1)S(1)}, bf16[128,512]{1,0:T(8,128)(2,1)S(1)}, u32[]{:S(2)}, u32[]{:S(2)}) collective-permute-start(bf16[128,512]{1,0:T(8,128)(2,1)S(1)} %get-tuple-element.131), channel_id=1, source_target_pairs={{0,1},{1,2},{2,3},{3,0},{4,5},{5,6},{6,7},{7,4},{8,9},{9,10},{10,1... | collective-permute-start | bytes 393224 | tf_op jit(solution)/shard_map/ppermute | solution.py:411
  311.7 2.8 collective-permute-start.64
  314.5 3.4 add_convert_fusion.10
  317.8 10.1 %collective-permute-done.53 = bf16[256,2048]{1,0:T(8,128)(2,1)} collective-permute-done((bf16[256,2048]{1,0:T(8,128)(2,1)}, bf16[256,2048]{1,0:T(8,128)(2,1)}, u32[]{:S(2)}, u32[]{:S(2)}) %collective-permute-start.53) | collective-permute-done | bytes 1048608 | tf_op jit(solution)/shard_map/ppermute | solution.py:408
  330.8 3.2 add_convert_fusion.8
  334.0 6.2 %collective-permute-start.39 = (bf16[384,256]{1,0:T(8,128)(2,1)}, bf16[384,256]{1,0:T(8,128)(2,1)}, u32[]{:S(2)}, u32[]{:S(2)}) collective-permute-start(bf16[384,256]{1,0:T(8,128)(2,1)} %get-tuple-element.137), channel_id=1, source_target_pairs={{0,3},{1,0},{2,1},{3,2},{4,7},{5,4},{6,5},{7,6},{8,11},{9,8},{10,9... | collective-permute-start | bytes 589832 | tf_op jit(solution)/shard_map/ppermute | solution.py:411
  344.3 2.5 add_convert_fusion.17
  346.7 3.0 collective-permute-start.46
  349.7 2.8 collective-permute-done.54
  352.5 4.3 %collective-permute-start.47 = (bf16[128,1024]{1,0:T(8,128)(2,1)S(1)}, bf16[128,1024]{1,0:T(8,128)(2,1)S(1)}, u32[]{:S(2)}, u32[]{:S(2)}) collective-permute-start(bf16[128,1024]{1,0:T(8,128)(2,1)S(1)} %get-tuple-element.119), channel_id=1, source_target_pairs={{0,1},{1,2},{2,3},{3,0},{4,5},{5,6},{6,7},{7,4},{8,9},{9,10},{10,1... | collective-permute-start | bytes 786440 | tf_op jit(solution)/shard_map/ppermute | solution.py:411
  356.8 2.7 collective-permute-start.43
  361.8 10.4 %collective-permute-done.46 = bf16[128,1024]{1,0:T(8,128)(2,1)S(1)} collective-permute-done((bf16[128,1024]{1,0:T(8,128)(2,1)S(1)}, bf16[128,1024]{1,0:T(8,128)(2,1)S(1)}, u32[]{:S(2)}, u32[]{:S(2)}) %collective-permute-start.46) | collective-permute-done | bytes 262176 | tf_op jit(solution)/shard_map/ppermute | solution.py:411
  372.2 9.6 %collective-permute-start.59 = (bf16[128,1024]{1,0:T(8,128)(2,1)S(1)}, bf16[128,1024]{1,0:T(8,128)(2,1)S(1)}, u32[]{:S(2)}, u32[]{:S(2)}) collective-permute-start(bf16[128,1024]{1,0:T(8,128)(2,1)S(1)} %get-tuple-element.117), channel_id=1, source_target_pairs={{0,1},{1,2},{2,3},{3,0},{4,5},{5,6},{6,7},{7,4},{8,9},{9,10},{10,1... | collective-permute-start | bytes 786440 | tf_op jit(solution)/shard_map/ppermute | solution.py:411
  383.2 11.5 %collective-permute-done.58 = bf16[128,1024]{1,0:T(8,128)(2,1)S(1)} collective-permute-done((bf16[128,1024]{1,0:T(8,128)(2,1)S(1)}, bf16[128,1024]{1,0:T(8,128)(2,1)S(1)}, u32[]{:S(2)}, u32[]{:S(2)}) %collective-permute-start.58) | collective-permute-done | bytes 262176 | tf_op jit(solution)/shard_map/ppermute | solution.py:411
  394.7 3.9 collective-permute-start.51
  398.6 4.2 collective-permute-done.55
  407.0 5.4 %convert_element_type.393 = f32[1536,1024]{1,0:T(8,128)} convert(bf16[1536,1024]{1,0:T(8,128)(2,1)} %all-gather.5.cloned.1.call-done) | non-fusion elementwise | flops 1572864 | bytes 9437184 | tf_op jit(solution)/shard_map/convert_element_type | solution.py:808
  412.4 3.6 place_rows.1
  (327 shorter events, 100.4 us)
Async XLA Ops:
  7.2 157.9 %all-gather.3.cloned.1.call-start = ((), (), s32[]{:S(2)}) async-start(), calls=%async_computation | async-start | bytes 12976128 | tf_op jit(solution)/shard_map/all_gather | solution.py:695
  11.9 394.1 %all-gather.5.cloned.1.call-start = ((), (), s32[]{:S(2)}) async-start(), calls=%async_computation.1 | async-start | bytes 3932160 | tf_op jit(solution)/shard_map/all_gather | solution.py:768
  13.5 25.7 %collective-permute-start.2 = (bf16[128,512]{1,0:T(8,128)(2,1)}, bf16[128,512]{1,0:T(8,128)(2,1)}, u32[]{:S(2)}, u32[]{:S(2)}) collective-permute-start(bf16[128,512]{1,0:T(8,128)(2,1)} %pad_maximum_fusion.3), channel_id=1, source_target_pairs={{0,3},{1,0},{2,1},{3,2},{4,7},{5,4},{6,5},{7,6},{8,11},{9,8},{10,9... | collective-permute-start | bytes 393224 | tf_op jit(solution)/shard_map/ppermute | solution.py:411
  18.6 19.0 %collective-permute-start.1 = (bf16[128,512]{1,0:T(8,128)(2,1)}, bf16[128,512]{1,0:T(8,128)(2,1)}, u32[]{:S(2)}, u32[]{:S(2)}) collective-permute-start(bf16[128,512]{1,0:T(8,128)(2,1)} %pad_maximum_fusion.3), channel_id=1, source_target_pairs={{0,2},{1,3},{2,0},{3,1},{4,6},{5,7},{6,4},{7,5},{8,10},{9,11},{10,... | collective-permute-start | bytes 393224 | tf_op jit(solution)/shard_map/ppermute | solution.py:411
  18.6 26.0 %collective-permute-start = (bf16[128,512]{1,0:T(8,128)(2,1)}, bf16[128,512]{1,0:T(8,128)(2,1)}, u32[]{:S(2)}, u32[]{:S(2)}) collective-permute-start(bf16[128,512]{1,0:T(8,128)(2,1)} %pad_maximum_fusion.3), channel_id=1, source_target_pairs={{0,1},{1,2},{2,3},{3,0},{4,5},{5,6},{6,7},{7,4},{8,9},{9,10},{10,1... | collective-permute-start | bytes 393224 | tf_op jit(solution)/shard_map/ppermute | solution.py:411
  21.2 26.1 %collective-permute-start.22 = (bf16[128,512]{1,0:T(8,128)(2,1)}, bf16[128,512]{1,0:T(8,128)(2,1)}, u32[]{:S(2)}, u32[]{:S(2)}) collective-permute-start(bf16[128,512]{1,0:T(8,128)(2,1)} %pad_maximum_fusion.4), channel_id=1, source_target_pairs={{0,3},{1,0},{2,1},{3,2},{4,7},{5,4},{6,5},{7,6},{8,11},{9,8},{10,9... | collective-permute-start | bytes 393224 | tf_op jit(solution)/shard_map/ppermute | solution.py:411
  24.0 31.3 %collective-permute-start.21 = (bf16[128,512]{1,0:T(8,128)(2,1)}, bf16[128,512]{1,0:T(8,128)(2,1)}, u32[]{:S(2)}, u32[]{:S(2)}) collective-permute-start(bf16[128,512]{1,0:T(8,128)(2,1)} %pad_maximum_fusion.4), channel_id=1, source_target_pairs={{0,2},{1,3},{2,0},{3,1},{4,6},{5,7},{6,4},{7,5},{8,10},{9,11},{10,... | collective-permute-start | bytes 393224 | tf_op jit(solution)/shard_map/ppermute | solution.py:411
  37.6 19.6 %collective-permute-start.20 = (bf16[128,512]{1,0:T(8,128)(2,1)}, bf16[128,512]{1,0:T(8,128)(2,1)S(1)}, u32[]{:S(2)}, u32[]{:S(2)}) collective-permute-start(bf16[128,512]{1,0:T(8,128)(2,1)} %pad_maximum_fusion.4), channel_id=1, source_target_pairs={{0,1},{1,2},{2,3},{3,0},{4,5},{5,6},{6,7},{7,4},{8,9},{9,10},{10,1... | collective-permute-start | bytes 393224 | tf_op jit(solution)/shard_map/ppermute | solution.py:411
  39.2 18.0 %collective-permute-start.19 = (bf16[384,256]{1,0:T(8,128)(2,1)S(1)}, bf16[384,256]{1,0:T(8,128)(2,1)}, u32[]{:S(2)}, u32[]{:S(2)}) collective-permute-start(bf16[384,256]{1,0:T(8,128)(2,1)S(1)} %get-tuple-element.141), channel_id=1, source_target_pairs={{0,3},{1,0},{2,1},{3,2},{4,7},{5,4},{6,5},{7,6},{8,11},{9,8},{10,9... | collective-permute-start | bytes 589832 | tf_op jit(solution)/shard_map/ppermute | solution.py:411
  44.6 25.9 %collective-permute-start.17 = (bf16[384,256]{1,0:T(8,128)(2,1)}, bf16[384,256]{1,0:T(8,128)(2,1)}, u32[]{:S(2)}, u32[]{:S(2)}) collective-permute-start(bf16[384,256]{1,0:T(8,128)(2,1)} %get-tuple-element.142), channel_id=1, source_target_pairs={{0,1},{1,2},{2,3},{3,0},{4,5},{5,6},{6,7},{7,4},{8,9},{9,10},{10,1... | collective-permute-start | bytes 589832 | tf_op jit(solution)/shard_map/ppermute | solution.py:411
  47.3 45.1 %collective-permute-start.9 = (bf16[128,1024]{1,0:T(8,128)(2,1)S(1)}, bf16[128,1024]{1,0:T(8,128)(2,1)}, u32[]{:S(2)}, u32[]{:S(2)}) collective-permute-start(bf16[128,1024]{1,0:T(8,128)(2,1)S(1)} %constant_dynamic-update-slice_fusion.refs_0_), channel_id=1, source_target_pairs={{0,16},{4,20},{8,24},{12,28},{16,0},{20,4},{24,8},{28,12},{1,17},{... | collective-permute-start | bytes 786440 | tf_op jit(solution)/shard_map/ppermute | solution.py:408
  55.2 37.1 %collective-permute-start.5 = (bf16[128,1024]{1,0:T(8,128)(2,1)S(1)}, bf16[128,1024]{1,0:T(8,128)(2,1)}, u32[]{:S(2)}, u32[]{:S(2)}) collective-permute-start(bf16[128,1024]{1,0:T(8,128)(2,1)S(1)} %constant_dynamic-update-slice_fusion.refs_0_), channel_id=1, source_target_pairs={{0,8},{4,12},{8,0},{12,4},{16,24},{20,28},{24,16},{28,20},{1,9},{5... | collective-permute-start | bytes 786440 | tf_op jit(solution)/shard_map/ppermute | solution.py:408
  57.2 35.7 %collective-permute-start.3 = (bf16[128,1024]{1,0:T(8,128)(2,1)S(1)}, bf16[128,1024]{1,0:T(8,128)(2,1)}, u32[]{:S(2)}, u32[]{:S(2)}) collective-permute-start(bf16[128,1024]{1,0:T(8,128)(2,1)S(1)} %constant_dynamic-update-slice_fusion.refs_0_), channel_id=1, source_target_pairs={{0,4},{4,0},{8,12},{12,8},{16,20},{20,16},{24,28},{28,24},{1,5},{5... | collective-permute-start | bytes 786440 | tf_op jit(solution)/shard_map/ppermute | solution.py:408
  57.9 35.0 %collective-permute-start.10 = (bf16[128,1024]{1,0:T(8,128)(2,1)}, bf16[128,1024]{1,0:T(8,128)(2,1)}, u32[]{:S(2)}, u32[]{:S(2)}) collective-permute-start(bf16[128,1024]{1,0:T(8,128)(2,1)} %constant_dynamic-update-slice_fusion.5.refs_1_), channel_id=1, source_target_pairs={{0,16},{4,20},{8,24},{12,28},{16,0},{20,4},{24,8},{28,12},{1,17},{... | collective-permute-start | bytes 786440 | tf_op jit(solution)/shard_map/ppermute | solution.py:408
  70.5 21.9 %collective-permute-start.18 = (bf16[384,256]{1,0:T(8,128)(2,1)}, bf16[384,256]{1,0:T(8,128)(2,1)S(1)}, u32[]{:S(2)}, u32[]{:S(2)}) collective-permute-start(bf16[384,256]{1,0:T(8,128)(2,1)} %get-tuple-element.144), channel_id=1, source_target_pairs={{0,2},{1,3},{2,0},{3,1},{4,6},{5,7},{6,4},{7,5},{8,10},{9,11},{10,... | collective-permute-start | bytes 589832 | tf_op jit(solution)/shard_map/ppermute | solution.py:411
  92.4 15.6 %collective-permute-start.11 = (bf16[128,1024]{1,0:T(8,128)(2,1)}, bf16[128,1024]{1,0:T(8,128)(2,1)S(1)}, u32[]{:S(2)}, u32[]{:S(2)}) collective-permute-start(bf16[128,1024]{1,0:T(8,128)(2,1)} %collective-permute-done.9.refs_8_), channel_id=1, source_target_pairs={{0,4},{4,0},{8,12},{12,8},{16,20},{20,16},{24,28},{28,24},{1,5},{5... | collective-permute-start | bytes 786440 | tf_op jit(solution)/shard_map/ppermute | solution.py:408
  92.9 15.2 %collective-permute-start.13 = (bf16[128,1024]{1,0:T(8,128)(2,1)}, bf16[128,1024]{1,0:T(8,128)(2,1)S(1)}, u32[]{:S(2)}, u32[]{:S(2)}) collective-permute-start(bf16[128,1024]{1,0:T(8,128)(2,1)} %collective-permute-done.5.refs_4_), channel_id=1, source_target_pairs={{0,16},{4,20},{8,24},{12,28},{16,0},{20,4},{24,8},{28,12},{1,17},{... | collective-permute-start | bytes 786440 | tf_op jit(solution)/shard_map/ppermute | solution.py:408
  92.9 23.0 %collective-permute-start.14 = (bf16[128,1024]{1,0:T(8,128)(2,1)}, bf16[128,1024]{1,0:T(8,128)(2,1)S(1)}, u32[]{:S(2)}, u32[]{:S(2)}) collective-permute-start(bf16[128,1024]{1,0:T(8,128)(2,1)} %collective-permute-done.10.refs_9_), channel_id=1, source_target_pairs={{0,8},{4,12},{8,0},{12,4},{16,24},{20,28},{24,16},{28,20},{1,9},{5... | collective-permute-start | bytes 786440 | tf_op jit(solution)/shard_map/ppermute | solution.py:408
  120.0 17.5 %collective-permute-start.29 = (bf16[128,1024]{1,0:T(8,128)(2,1)S(1)}, bf16[128,1024]{1,0:T(8,128)(2,1)}, u32[]{:S(2)}, u32[]{:S(2)}) collective-permute-start(bf16[128,1024]{1,0:T(8,128)(2,1)S(1)} %pad_maximum_fusion.2.refs_0_), channel_id=1, source_target_pairs={{0,16},{4,20},{8,24},{12,28},{16,0},{20,4},{24,8},{28,12},{1,17},{... | collective-permute-start | bytes 786440 | tf_op jit(solution)/shard_map/ppermute | solution.py:408
  120.1 17.4 %collective-permute-start.25 = (bf16[128,1024]{1,0:T(8,128)(2,1)S(1)}, bf16[128,1024]{1,0:T(8,128)(2,1)}, u32[]{:S(2)}, u32[]{:S(2)}) collective-permute-start(bf16[128,1024]{1,0:T(8,128)(2,1)S(1)} %pad_maximum_fusion.2.refs_0_), channel_id=1, source_target_pairs={{0,8},{4,12},{8,0},{12,4},{16,24},{20,28},{24,16},{28,20},{1,9},{5... | collective-permute-start | bytes 786440 | tf_op jit(solution)/shard_map/ppermute | solution.py:408
  120.2 17.8 %collective-permute-start.23 = (bf16[128,1024]{1,0:T(8,128)(2,1)S(1)}, bf16[128,1024]{1,0:T(8,128)(2,1)}, u32[]{:S(2)}, u32[]{:S(2)}) collective-permute-start(bf16[128,1024]{1,0:T(8,128)(2,1)S(1)} %pad_maximum_fusion.2.refs_0_), channel_id=1, source_target_pairs={{0,4},{4,0},{8,12},{12,8},{16,20},{20,16},{24,28},{28,24},{1,5},{5... | collective-permute-start | bytes 786440 | tf_op jit(solution)/shard_map/ppermute | solution.py:408
  120.7 17.8 %collective-permute-start.30 = (bf16[128,1024]{1,0:T(8,128)(2,1)}, bf16[128,1024]{1,0:T(8,128)(2,1)}, u32[]{:S(2)}, u32[]{:S(2)}) collective-permute-start(bf16[128,1024]{1,0:T(8,128)(2,1)} %constant_dynamic-update-slice_fusion.7.refs_1_), channel_id=1, source_target_pairs={{0,16},{4,20},{8,24},{12,28},{16,0},{20,4},{24,8},{28,12},{1,17},{... | collective-permute-start | bytes 786440 | tf_op jit(solution)/shard_map/ppermute | solution.py:408
  123.2 17.3 %collective-permute-start.26 = (bf16[128,1024]{1,0:T(8,128)(2,1)}, bf16[128,1024]{1,0:T(8,128)(2,1)}, u32[]{:S(2)}, u32[]{:S(2)}) collective-permute-start(bf16[128,1024]{1,0:T(8,128)(2,1)} %constant_dynamic-update-slice_fusion.7.refs_1_), channel_id=1, source_target_pairs={{0,8},{4,12},{8,0},{12,4},{16,24},{20,28},{24,16},{28,20},{1,9},{5... | collective-permute-start | bytes 786440 | tf_op jit(solution)/shard_map/ppermute | solution.py:408
  140.5 15.2 %collective-permute-start.27 = (bf16[128,1024]{1,0:T(8,128)(2,1)}, bf16[128,1024]{1,0:T(8,128)(2,1)S(1)}, u32[]{:S(2)}, u32[]{:S(2)}) collective-permute-start(bf16[128,1024]{1,0:T(8,128)(2,1)} %collective-permute-done.25.refs_4_), channel_id=1, source_target_pairs={{0,4},{4,0},{8,12},{12,8},{16,20},{20,16},{24,28},{28,24},{1,5},{5... | collective-permute-start | bytes 786440 | tf_op jit(solution)/shard_map/ppermute | solution.py:408
  214.4 61.3 %collective-permute-start.40 = (bf16[512,4096]{1,0:T(8,128)(2,1)}, bf16[512,4096]{1,0:T(8,128)(2,1)}, u32[]{:S(2)}, u32[]{:S(2)}) collective-permute-start(bf16[512,4096]{1,0:T(8,128)(2,1)} %unit_grad.6), channel_id=1, source_target_pairs={{0,4},{4,0},{8,12},{12,8},{16,20},{20,16},{24,28},{28,24},{1,5},{5... | collective-permute-start | bytes 12582920 | tf_op jit(solution)/shard_map/ppermute | solution.py:408
  221.9 59.6 %collective-permute-start.52 = (bf16[512,4096]{1,0:T(8,128)(2,1)}, bf16[512,4096]{1,0:T(8,128)(2,1)}, u32[]{:S(2)}, u32[]{:S(2)}) collective-permute-start(bf16[512,4096]{1,0:T(8,128)(2,1)} %unit_grad.7), channel_id=1, source_target_pairs={{0,4},{4,0},{8,12},{12,8},{16,20},{20,16},{24,28},{28,24},{1,5},{5... | collective-permute-start | bytes 12582920 | tf_op jit(solution)/shard_map/ppermute | solution.py:408
  230.6 20.6 %collective-permute-start.61 = (bf16[512,2048]{1,0:T(8,128)(2,1)}, bf16[512,2048]{1,0:T(8,128)(2,1)}, u32[]{:S(2)}, u32[]{:S(2)}) collective-permute-start(bf16[512,2048]{1,0:T(8,128)(2,1)} %attention_grad.3), channel_id=1, source_target_pairs={{0,4},{4,0},{8,12},{12,8},{16,20},{20,16},{24,28},{28,24},{1,5},{5... | collective-permute-start | bytes 6291464 | tf_op jit(solution)/shard_map/ppermute | solution.py:408
  253.6 18.5 %collective-permute-start.62 = (bf16[256,1024]{1,0:T(8,128)(2,1)}, bf16[256,1024]{1,0:T(8,128)(2,1)}, u32[]{:S(2)}, u32[]{:S(2)}) collective-permute-start(bf16[256,1024]{1,0:T(8,128)(2,1)} %get-tuple-element.135), channel_id=1, source_target_pairs={{0,16},{4,20},{8,24},{12,28},{16,0},{20,4},{24,8},{28,12},{1,17},{... | collective-permute-start | bytes 1572872 | tf_op jit(solution)/shard_map/ppermute | solution.py:408
  254.9 17.2 %collective-permute-start.65 = (bf16[256,1024]{1,0:T(8,128)(2,1)S(1)}, bf16[256,1024]{1,0:T(8,128)(2,1)S(1)}, u32[]{:S(2)}, u32[]{:S(2)}) collective-permute-start(bf16[256,1024]{1,0:T(8,128)(2,1)S(1)} %get-tuple-element.136), channel_id=1, source_target_pairs={{0,8},{4,12},{8,0},{12,4},{16,24},{20,28},{24,16},{28,20},{1,9},{5... | collective-permute-start | bytes 1572872 | tf_op jit(solution)/shard_map/ppermute | solution.py:408
  271.3 15.7 %collective-permute-start.50 = (f32[11,1024]{1,0:T(8,128)S(1)}, f32[11,1024]{1,0:T(8,128)S(1)}, u32[]{:S(2)}, u32[]{:S(2)}) collective-permute-start(f32[11,1024]{1,0:T(8,128)S(1)} %add.396), channel_id=1, source_target_pairs={{0,16},{4,20},{8,24},{12,28},{16,0},{20,4},{24,8},{28,12},{1,17},{... | collective-permute-start | bytes 135176 | tf_op jit(solution)/shard_map/ppermute | solution.py:408
  274.6 26.1 %collective-permute-start.66 = (bf16[128,1024]{1,0:T(8,128)(2,1)}, bf16[128,1024]{1,0:T(8,128)(2,1)S(1)}, u32[]{:S(2)}, u32[]{:S(2)}) collective-permute-start(bf16[128,1024]{1,0:T(8,128)(2,1)} %get-tuple-element.134), channel_id=1, source_target_pairs={{0,16},{4,20},{8,24},{12,28},{16,0},{20,4},{24,8},{28,12},{1,17},{... | collective-permute-start | bytes 786440 | tf_op jit(solution)/shard_map/ppermute | solution.py:408
  280.3 26.3 %collective-permute-start.41 = (bf16[256,2048]{1,0:T(8,128)(2,1)}, bf16[256,2048]{1,0:T(8,128)(2,1)}, u32[]{:S(2)}, u32[]{:S(2)}) collective-permute-start(bf16[256,2048]{1,0:T(8,128)(2,1)} %get-tuple-element.128), channel_id=1, source_target_pairs={{0,16},{4,20},{8,24},{12,28},{16,0},{20,4},{24,8},{28,12},{1,17},{... | collective-permute-start | bytes 3145736 | tf_op jit(solution)/shard_map/ppermute | solution.py:408
  281.5 30.2 %collective-permute-start.44 = (bf16[256,2048]{1,0:T(8,128)(2,1)}, bf16[256,2048]{1,0:T(8,128)(2,1)}, u32[]{:S(2)}, u32[]{:S(2)}) collective-permute-start(bf16[256,2048]{1,0:T(8,128)(2,1)} %get-tuple-element.129), channel_id=1, source_target_pairs={{0,8},{4,12},{8,0},{12,4},{16,24},{20,28},{24,16},{28,20},{1,9},{5... | collective-permute-start | bytes 3145736 | tf_op jit(solution)/shard_map/ppermute | solution.py:408
  287.0 41.0 %collective-permute-start.53 = (bf16[256,2048]{1,0:T(8,128)(2,1)}, bf16[256,2048]{1,0:T(8,128)(2,1)}, u32[]{:S(2)}, u32[]{:S(2)}) collective-permute-start(bf16[256,2048]{1,0:T(8,128)(2,1)} %get-tuple-element.123), channel_id=1, source_target_pairs={{0,16},{4,20},{8,24},{12,28},{16,0},{20,4},{24,8},{28,12},{1,17},{... | collective-permute-start | bytes 3145736 | tf_op jit(solution)/shard_map/ppermute | solution.py:408
  288.6 41.1 %collective-permute-start.56 = (bf16[256,2048]{1,0:T(8,128)(2,1)}, bf16[256,2048]{1,0:T(8,128)(2,1)S(1)}, u32[]{:S(2)}, u32[]{:S(2)}) collective-permute-start(bf16[256,2048]{1,0:T(8,128)(2,1)} %get-tuple-element.124), channel_id=1, source_target_pairs={{0,8},{4,12},{8,0},{12,4},{16,24},{20,28},{24,16},{28,20},{1,9},{5... | collective-permute-start | bytes 3145736 | tf_op jit(solution)/shard_map/ppermute | solution.py:408
  302.1 31.9 %collective-permute-start.67 = (bf16[128,512]{1,0:T(8,128)(2,1)S(1)}, bf16[128,512]{1,0:T(8,128)(2,1)S(1)}, u32[]{:S(2)}, u32[]{:S(2)}) collective-permute-start(bf16[128,512]{1,0:T(8,128)(2,1)S(1)} %get-tuple-element.130), channel_id=1, source_target_pairs={{0,2},{1,3},{2,0},{3,1},{4,6},{5,7},{6,4},{7,5},{8,10},{9,11},{10,... | collective-permute-start | bytes 393224 | tf_op jit(solution)/shard_map/ppermute | solution.py:411
  306.6 33.6 %collective-permute-start.68 = (bf16[128,512]{1,0:T(8,128)(2,1)S(1)}, bf16[128,512]{1,0:T(8,128)(2,1)S(1)}, u32[]{:S(2)}, u32[]{:S(2)}) collective-permute-start(bf16[128,512]{1,0:T(8,128)(2,1)S(1)} %get-tuple-element.131), channel_id=1, source_target_pairs={{0,1},{1,2},{2,3},{3,0},{4,5},{5,6},{6,7},{7,4},{8,9},{9,10},{10,1... | collective-permute-start | bytes 393224 | tf_op jit(solution)/shard_map/ppermute | solution.py:411
  311.7 29.2 %collective-permute-start.64 = (bf16[128,512]{1,0:T(8,128)(2,1)S(1)}, bf16[128,512]{1,0:T(8,128)(2,1)S(1)}, u32[]{:S(2)}, u32[]{:S(2)}) collective-permute-start(bf16[128,512]{1,0:T(8,128)(2,1)S(1)} %get-tuple-element.132), channel_id=1, source_target_pairs={{0,3},{1,0},{2,1},{3,2},{4,7},{5,4},{6,5},{7,6},{8,11},{9,8},{10,9... | collective-permute-start | bytes 393224 | tf_op jit(solution)/shard_map/ppermute | solution.py:411
  327.9 16.3 %collective-permute-start.42 = (bf16[128,2048]{1,0:T(8,128)(2,1)}, bf16[128,2048]{1,0:T(8,128)(2,1)}, u32[]{:S(2)}, u32[]{:S(2)}) collective-permute-start(bf16[128,2048]{1,0:T(8,128)(2,1)} %get-tuple-element.126), channel_id=1, source_target_pairs={{0,8},{4,12},{8,0},{12,4},{16,24},{20,28},{24,16},{28,20},{1,9},{5... | collective-permute-start | bytes 1572872 | tf_op jit(solution)/shard_map/ppermute | solution.py:408
  334.0 72.0 %collective-permute-start.39 = (bf16[384,256]{1,0:T(8,128)(2,1)}, bf16[384,256]{1,0:T(8,128)(2,1)}, u32[]{:S(2)}, u32[]{:S(2)}) collective-permute-start(bf16[384,256]{1,0:T(8,128)(2,1)} %get-tuple-element.137), channel_id=1, source_target_pairs={{0,3},{1,0},{2,1},{3,2},{4,7},{5,4},{6,5},{7,6},{8,11},{9,8},{10,9... | collective-permute-start | bytes 589832 | tf_op jit(solution)/shard_map/ppermute | solution.py:411
  340.9 15.9 %collective-permute-start.57 = (bf16[128,2048]{1,0:T(8,128)(2,1)}, bf16[128,2048]{1,0:T(8,128)(2,1)}, u32[]{:S(2)}, u32[]{:S(2)}) collective-permute-start(bf16[128,2048]{1,0:T(8,128)(2,1)} %get-tuple-element.122), channel_id=1, source_target_pairs={{0,16},{4,20},{8,24},{12,28},{16,0},{20,4},{24,8},{28,12},{1,17},{... | collective-permute-start | bytes 1572872 | tf_op jit(solution)/shard_map/ppermute | solution.py:408
  344.3 61.7 %collective-permute-start.38 = (bf16[384,256]{1,0:T(8,128)(2,1)}, bf16[384,256]{1,0:T(8,128)(2,1)S(1)}, u32[]{:S(2)}, u32[]{:S(2)}) collective-permute-start(bf16[384,256]{1,0:T(8,128)(2,1)} %get-tuple-element.138), channel_id=1, source_target_pairs={{0,2},{1,3},{2,0},{3,1},{4,6},{5,7},{6,4},{7,5},{8,10},{9,11},{10,... | collective-permute-start | bytes 589832 | tf_op jit(solution)/shard_map/ppermute | solution.py:411
  346.7 25.4 %collective-permute-start.46 = (bf16[128,1024]{1,0:T(8,128)(2,1)S(1)}, bf16[128,1024]{1,0:T(8,128)(2,1)S(1)}, u32[]{:S(2)}, u32[]{:S(2)}) collective-permute-start(bf16[128,1024]{1,0:T(8,128)(2,1)S(1)} %get-tuple-element.118), channel_id=1, source_target_pairs={{0,2},{1,3},{2,0},{3,1},{4,6},{5,7},{6,4},{7,5},{8,10},{9,11},{10,... | collective-permute-start | bytes 786440 | tf_op jit(solution)/shard_map/ppermute | solution.py:411
  352.5 19.6 %collective-permute-start.47 = (bf16[128,1024]{1,0:T(8,128)(2,1)S(1)}, bf16[128,1024]{1,0:T(8,128)(2,1)S(1)}, u32[]{:S(2)}, u32[]{:S(2)}) collective-permute-start(bf16[128,1024]{1,0:T(8,128)(2,1)S(1)} %get-tuple-element.119), channel_id=1, source_target_pairs={{0,1},{1,2},{2,3},{3,0},{4,5},{5,6},{6,7},{7,4},{8,9},{9,10},{10,1... | collective-permute-start | bytes 786440 | tf_op jit(solution)/shard_map/ppermute | solution.py:411
  356.8 24.9 %collective-permute-start.43 = (bf16[128,1024]{1,0:T(8,128)(2,1)S(1)}, bf16[128,1024]{1,0:T(8,128)(2,1)S(1)}, u32[]{:S(2)}, u32[]{:S(2)}) collective-permute-start(bf16[128,1024]{1,0:T(8,128)(2,1)S(1)} %get-tuple-element.125), channel_id=1, source_target_pairs={{0,3},{1,0},{2,1},{3,2},{4,7},{5,4},{6,5},{7,6},{8,11},{9,8},{10,9... | collective-permute-start | bytes 786440 | tf_op jit(solution)/shard_map/ppermute | solution.py:411
  372.2 22.5 %collective-permute-start.58 = (bf16[128,1024]{1,0:T(8,128)(2,1)S(1)}, bf16[128,1024]{1,0:T(8,128)(2,1)S(1)}, u32[]{:S(2)}, u32[]{:S(2)}) collective-permute-start(bf16[128,1024]{1,0:T(8,128)(2,1)S(1)} %get-tuple-element.116), channel_id=1, source_target_pairs={{0,2},{1,3},{2,0},{3,1},{4,6},{5,7},{6,4},{7,5},{8,10},{9,11},{10,... | collective-permute-start | bytes 786440 | tf_op jit(solution)/shard_map/ppermute | solution.py:411
  372.2 22.5 %collective-permute-start.59 = (bf16[128,1024]{1,0:T(8,128)(2,1)S(1)}, bf16[128,1024]{1,0:T(8,128)(2,1)S(1)}, u32[]{:S(2)}, u32[]{:S(2)}) collective-permute-start(bf16[128,1024]{1,0:T(8,128)(2,1)S(1)} %get-tuple-element.117), channel_id=1, source_target_pairs={{0,1},{1,2},{2,3},{3,0},{4,5},{5,6},{6,7},{7,4},{8,9},{9,10},{10,1... | collective-permute-start | bytes 786440 | tf_op jit(solution)/shard_map/ppermute | solution.py:411
  381.7 21.1 %collective-permute-start.55 = (bf16[128,1024]{1,0:T(8,128)(2,1)S(1)}, bf16[128,1024]{1,0:T(8,128)(2,1)S(1)}, u32[]{:S(2)}, u32[]{:S(2)}) collective-permute-start(bf16[128,1024]{1,0:T(8,128)(2,1)S(1)} %get-tuple-element.120), channel_id=1, source_target_pairs={{0,3},{1,0},{2,1},{3,2},{4,7},{5,4},{6,5},{7,6},{8,11},{9,8},{10,9... | collective-permute-start | bytes 786440 | tf_op jit(solution)/shard_map/ppermute | solution.py:411
  (89 other events, 817.8 us)
Sparse Core Ops, SparseCore 0:
  12.0 122.1 all-gather.2
  231.3 66.2 all-gather.4
